TPU v7x, 256 devices: a whole 4x4x8 slice. The times are simulated.
256 devices in a mesh: tm: 32 (over z, x), fsdp: 8 (over y, core).
Axes of the slice: x: 4, y: 4, z: 8, core: 2. Of those that a mesh axis runs over, the one named last changes fastest.
Arguments:
- frames: bfloat16 [64, 64, 256, 128], P('tm', None, 'fsdp'), may hold values from -6 to 6
- conv_weight: bfloat16 [3, 3, 3, 128, 128], P(None, None, None, None, 'fsdp'), may hold values from -0.109375 to 0.109375
- mix_weight: bfloat16 [3, 128, 128], P(None, None, 'fsdp'), may hold values from -0.3125 to 0.3125
- cotangent: bfloat16 [32, 64, 256, 128], P(None, 'tm', 'fsdp'), may hold values from -0.008239746 to 0.008239746
Outputs:
- encoded: bfloat16 [32, 64, 256, 128], P(None, 'tm', 'fsdp')
- mix_grad: float32 [49152], P(('tm', 'fsdp'))
All inputs are finite; a program needn't handle non-finite values.
Results may differ from a plain program's by a relative error of at most 0.0058.
Values may be sent and summed in bfloat16 or wider, within the bound.
A program may use at most 64 MiB of HBM per device.

v0:
```python
import jax
import jax.numpy as jnp
from jax import lax
from jax.sharding import PartitionSpec as P


def from_behind(block, axis, distance):
    devices = range(lax.axis_size(axis))
    route = [(i - distance, i) for i in devices if i - distance in devices]
    return lax.ppermute(block, axis, route)


def with_halo(cells, sides, width):
    for axis, dim in sides:
        count = lax.axis_size(axis)
        ends = count - 1
        head = lax.slice_in_dim(cells, 0, width, axis=dim)
        tail = lax.slice_in_dim(cells, cells.shape[dim] - width, cells.shape[dim], axis=dim)
        cells = jnp.concatenate(
            [
                lax.ppermute(tail, axis, [(i, (i + 1) % count) for i in range(ends)]),
                cells,
                lax.ppermute(head, axis, [((i + 1) % count, i) for i in range(ends)]),
            ],
            axis=dim,
        )
    return cells


def pool_pairs(hidden):
    shaped = hidden.reshape((hidden.shape[0] // 2, 2) + hidden.shape[1:]).astype(jnp.float32)
    return ((shaped[:, 0] + shaped[:, 1]) * 0.5).astype(jnp.bfloat16)


def delayed(block, offset):
    return jnp.pad(block, ((offset, 0), (0, 0), (0, 0), (0, 0)))[: block.shape[0]]


def local(frames, conv_weight, mix_weight, cotangent):
    full_conv, full_mix = (
        lax.all_gather(conv_weight, "fsdp", axis=4, tiled=True),
        lax.all_gather(mix_weight, "fsdp", axis=2, tiled=True),
    )
    count_frames, height, width, channels = frames.shape
    previous = from_behind(frames, "tm", 1)
    timed = jnp.concatenate([previous, frames], axis=0)
    padded = with_halo(timed, (("fsdp", 2),), 1)
    padded = jnp.pad(padded, ((0, 0), (1, 1), (0, 0), (0, 0)))
    accum = jnp.zeros((count_frames * height * width, channels), jnp.float32)
    for row_tap in range(3):
        for col_tap in range(3):
            stacked = jnp.concatenate(
                [
                    padded[
                        step : step + count_frames,
                        row_tap : row_tap + height,
                        col_tap : col_tap + width,
                        :,
                    ]
                    for step in range(3)
                ],
                axis=3,
            ).reshape(-1, 3 * channels)
            kernel = full_conv[:, row_tap, col_tap].reshape(3 * channels, channels)
            accum = accum + jnp.dot(stacked, kernel, preferred_element_type=jnp.float32)
    hidden = jax.nn.silu(accum).astype(jnp.bfloat16).reshape(count_frames, height, width, channels)
    pooled = lax.all_to_all(pool_pairs(hidden), "tm", split_axis=1, concat_axis=0, tiled=True)
    branch = pooled.astype(jnp.float32).reshape(-1, channels)
    flat_cot = cotangent.reshape(-1, channels)
    grad_terms = []
    for offset in range(3):
        lagged = delayed(pooled, offset).reshape(-1, channels)
        branch = branch + jnp.dot(lagged, full_mix[offset], preferred_element_type=jnp.float32)
        grad_terms.append(
            lax.dot_general(
                lagged, flat_cot, (((0,), (0,)), ((), ())), preferred_element_type=jnp.float32
            )
        )
    encoded = branch.astype(jnp.bfloat16).reshape(pooled.shape)
    mix_grad = lax.psum_scatter(
        jnp.stack(grad_terms).reshape(-1), ("tm", "fsdp"), scatter_dimension=0, tiled=True
    )
    return (encoded, mix_grad)


def solution(mesh):
    return jax.shard_map(
        local,
        mesh=mesh,
        in_specs=(
            P("tm", None, "fsdp", None),
            P(None, None, None, None, "fsdp"),
            P(None, None, "fsdp"),
            P(None, "tm", "fsdp", None),
        ),
        out_specs=(P(None, "tm", "fsdp", None), P(("tm", "fsdp"))),
        check_vma=False,
    )
```

profile of v0, /device:TPU:1, one launch (start us, length us, event | category | flops | bytes accessed | tf_op | source)
XLA Modules:
  0.0 362.0 jit_solution(556332334706884073)
XLA Ops:
  7.2 4.1 %collective-permute-start = (bf16[2,64,32,128]{3,2,1,0:T(8,128)(2,1)}, bf16[2,64,32,128]{3,2,1,0:T(8,128)(2,1)S(1)}, u32[]{:S(2)}, u32[]{:S(2)}) collective-permute-start(bf16[2,64,32,128]{3,2,1,0:T(8,128)(2,1)} %param.4), channel_id=1, source_target_pairs={{0,8},{8,16},{16,24},{24,32},{32,40},{40,48},{48,56},{56,64},{64,7... | collective-permute-start | bytes 3145736 | tf_op jit(solution)/shard_map/ppermute | solution.py:10
  11.3 15.0 %all_gather.6 = bf16[3,3,3,128,128]{3,4,2,1,0:T(8,128)(2,1)S(1)} all-gather(bf16[3,3,3,128,16]{3,4,2,1,0:T(8,128)(2,1)} %param.5), channel_id=1, replica_groups=mesh['tm'=32,'fsdp'=8] {'fsdp'}, dimensions={4}, use_global_device_ids=true | all-gather | bytes 995328 | tf_op jit(solution)/shard_map/all_gather | solution.py:41
  26.4 7.0 %collective-permute-done = bf16[2,64,32,128]{3,2,1,0:T(8,128)(2,1)S(1)} collective-permute-done((bf16[2,64,32,128]{3,2,1,0:T(8,128)(2,1)}, bf16[2,64,32,128]{3,2,1,0:T(8,128)(2,1)S(1)}, u32[]{:S(2)}, u32[]{:S(2)}) %collective-permute-start) | collective-permute-done | bytes 1048608 | tf_op jit(solution)/shard_map/ppermute | solution.py:10
  33.6 0.9 fusion.17
  34.6 3.4 collective-permute-start.2
  38.0 3.1 collective-permute-start.1
  41.1 0.7 fusion.18
  41.9 1.6 copy.18
  43.5 0.7 copy.19
  44.9 1.0 copy.25
  45.9 1.6 copy.26
  47.6 1.5 fusion.7
  49.1 6.9 %fusion.16 = (bf16[2,64,32,128]{3,2,1,0:T(8,128)(2,1)S(1)}, bf16[2,64,32,128]{3,2,1,0:T(8,128)(2,1)S(1)}, bf16[2,64,32,128]{3,2,1,0:T(8,128)(2,1)S(1)}, bf16[2,6...) fusion(bf16[4,66,34,128]{3,2,1,0:T(8,128)(2,1)S(1)} %fusion.7), kind=kLoop, calls=%fused_computation.59 | loop fusion | bytes 37748736 | tf_op jit(solution)/shard_map/slice | solution.py:54
  56.0 3.3 pad_maximum_fusion.2
  59.3 1.0 fusion.19
  60.3 1.1 convolution_add_fusion.7
  61.5 0.3 copy-done.2
  61.9 0.3 copy-done.3
  62.2 0.3 copy-done.4
  62.5 0.9 pad_maximum_fusion.4
  63.3 1.0 convolution_add_fusion.6
  64.3 2.1 fusion.10
  66.5 2.5 fusion.1
  69.0 1.0 convolution_add_fusion.5
  70.0 0.2 copy-done.6
  70.2 0.3 copy-done.8
  70.5 0.4 pad_maximum_fusion.5
  70.9 1.0 convolution_add_fusion.4
  72.0 1.0 convolution_add_fusion.3
  73.0 1.0 convolution_add_fusion.2
  74.0 0.9 pad_maximum_fusion.7
  74.9 1.0 convolution_add_fusion.1
  76.0 1.1 multiply_convert_fusion
  77.1 0.3 convert.1
  77.4 1.0 fusion.15
  78.4 12.8 %all-to-all-start = ((bf16[1,64,32,128]{3,2,0,1:T(8,128)(2,1)}), bf16[1,64,32,128]{3,2,0,1:T(8,128)(2,1)S(1)}, u32[]{:S(2)}, u32[]{:S(2)}) async-start(bf16[1,64,32,128]{3,2,0,1:T(8,128)(2,1)} %fusion.15), calls=%async_computation | async-start | bytes 1048576 | tf_op jit(solution)/shard_map/all_to_all | solution.py:67
  91.3 12.7 %all_gather.7 = bf16[3,128,128]{1,2,0:T(8,128)(2,1)S(1)} all-gather(bf16[3,128,16]{1,2,0:T(8,128)(2,1)S(1)} %copy-done.12), channel_id=1, replica_groups=mesh['tm'=32,'fsdp'=8] {'fsdp'}, dimensions={2}, use_global_device_ids=true | all-gather | bytes 110592 | tf_op jit(solution)/shard_map/all_gather | solution.py:42
  104.0 4.6 %all-to-all-done = bf16[1,64,32,128]{3,2,0,1:T(8,128)(2,1)S(1)} async-done(((bf16[1,64,32,128]{3,2,0,1:T(8,128)(2,1)}), bf16[1,64,32,128]{3,2,0,1:T(8,128)(2,1)S(1)}, u32[]{:S(2)}, u32[]{:S(2)}) %all-to-all-start) | async-done | bytes 524320 | tf_op jit(solution)/shard_map/all_to_all | solution.py:67
  108.6 0.2 pad_slice_fusion.8
  108.8 0.3 convolution_bitcast_fusion
  109.2 0.3 convolution_bitcast_fusion.1
  109.5 0.3 convolution_add_fusion.10
  109.8 0.3 convolution_bitcast_fusion.2
  110.2 0.7 pad_maximum_fusion.9
  110.9 0.3 convolution_add_fusion.9
  111.2 1.1 fusion.8
  112.3 241.5 %all-reduce.6.cloned.1.call-done = f32[49152]{0:T(1024)} async-done(((f32[49152]{0:T(1024)}), f32[49152]{0:T(1024)}) %all-reduce.6.cloned.1.call-update) | async-done | bytes 196624
  353.8 1.3 dynamic-slice
  (32 shorter events, 1.1 us)
Async XLA Ops:
  7.2 101.7 %copy-start = (bf16[32,2,32,128]{3,2,1,0:T(8,128)(2,1)S(1)}, bf16[32,2,32,128]{3,2,1,0:T(8,128)(2,1)}, u32[]{:S(2)}) copy-start(bf16[32,2,32,128]{3,2,1,0:T(8,128)(2,1)} %param.7) | copy-start | bytes 1572868
  7.2 26.3 %copy-start.5 = (bf16[2,64,32,128]{3,2,1,0:T(8,128)(2,1)S(1)}, bf16[2,64,32,128]{3,2,1,0:T(8,128)(2,1)}, u32[]{:S(2)}) copy-start(bf16[2,64,32,128]{3,2,1,0:T(8,128)(2,1)} %param.4) | copy-start | bytes 3145732
  7.2 26.2 %collective-permute-start = (bf16[2,64,32,128]{3,2,1,0:T(8,128)(2,1)}, bf16[2,64,32,128]{3,2,1,0:T(8,128)(2,1)S(1)}, u32[]{:S(2)}, u32[]{:S(2)}) collective-permute-start(bf16[2,64,32,128]{3,2,1,0:T(8,128)(2,1)} %param.4), channel_id=1, source_target_pairs={{0,8},{8,16},{16,24},{24,32},{32,40},{40,48},{48,56},{56,64},{64,7... | collective-permute-start | bytes 3145736 | tf_op jit(solution)/shard_map/ppermute | solution.py:10
  33.4 8.5 %copy-start.7 = (bf16[2,64,32,128]{3,2,1,0:T(8,128)(2,1)}, bf16[2,64,32,128]{3,2,1,0:T(8,128)(2,1)S(1)}, u32[]{:S(2)}) copy-start(bf16[2,64,32,128]{3,2,1,0:T(8,128)(2,1)S(1)} %collective-permute-done) | copy-start | bytes 3145732
  34.6 13.0 %collective-permute-start.2 = (bf16[4,64,1,128]{3,2,1,0:T(2,128)(2,1)}, bf16[4,64,1,128]{3,2,1,0:T(2,128)(2,1)S(1)}, u32[]{:S(2)}, u32[]{:S(2)}) collective-permute-start(bf16[4,64,1,128]{3,2,1,0:T(2,128)(2,1)} %get-tuple-element.30), channel_id=1, source_target_pairs={{1,0},{2,1},{3,2},{4,3},{5,4},{6,5},{7,6},{9,8},{10,9},{11,10},{12... | collective-permute-start | bytes 196616 | tf_op jit(solution)/shard_map/ppermute | solution.py:23
  38.0 9.6 %collective-permute-start.1 = (bf16[4,64,1,128]{3,2,1,0:T(2,128)(2,1)}, bf16[4,64,1,128]{3,2,1,0:T(2,128)(2,1)S(1)}, u32[]{:S(2)}, u32[]{:S(2)}) collective-permute-start(bf16[4,64,1,128]{3,2,1,0:T(2,128)(2,1)} %get-tuple-element.29), channel_id=1, source_target_pairs={{0,1},{1,2},{2,3},{3,4},{4,5},{5,6},{6,7},{8,9},{9,10},{10,11},{11... | collective-permute-start | bytes 196616 | tf_op jit(solution)/shard_map/ppermute | solution.py:21
  56.0 3.3 copy-start.10
  59.3 1.0 copy-start.9
  60.3 1.2 copy-start.1
  60.3 1.5 copy-start.2
  60.3 1.8 copy-start.3
  60.3 2.1 copy-start.4
  69.0 1.2 copy-start.6
  69.0 1.5 copy-start.8
  74.9 1.0 copy-start.11
  77.1 14.2 %copy-start.12 = (bf16[3,128,16]{1,2,0:T(8,128)(2,1)S(1)}, bf16[3,128,16]{1,2,0:T(8,128)(2,1)}, u32[]{:S(2)}) copy-start(bf16[3,128,16]{1,2,0:T(8,128)(2,1)} %param.6) | copy-start | bytes 36868
  78.4 30.2 %all-to-all-start = ((bf16[1,64,32,128]{3,2,0,1:T(8,128)(2,1)}), bf16[1,64,32,128]{3,2,0,1:T(8,128)(2,1)S(1)}, u32[]{:S(2)}, u32[]{:S(2)}) async-start(bf16[1,64,32,128]{3,2,0,1:T(8,128)(2,1)} %fusion.15), calls=%async_computation | async-start | bytes 1048576 | tf_op jit(solution)/shard_map/all_to_all | solution.py:67
  91.2 262.6 %all-reduce.6.cloned.1.call-start = ((), (), s32[]{:S(2)}) async-start(), calls=%async_computation.1 | async-start | bytes 393216
Sparse Core Ops, SparseCore 0:
  111.0 242.7 all-reduce.5
where the time goes:
time: 362 us
  waiting for transfers between devices  253 us (70%)
  blocking collectives  27.7 us (8%)
  starting transfers between devices  23.5 us (6%)
  local copies, waits for them, and re-layouts  17.7 us (5%)
  between operations  14.4 us (4%)
  other arithmetic  13.6 us (4%)
  matrix products  11.9 us (3%)
    unnamed x2, waiting for transfers between devices  242 us
    all_gather x1, blocking collectives, local(): lax.all_gather(conv_weight, 'fsdp', axis=4, tiled=True)  15 us
    all_to_all x1, starting transfers between devices, local(): lax.all_to_all(pool_pairs(hidden), 'tm', split_axis=1, concat_axis=0, til...  12.8 us
    all_gather x1, blocking collectives, local(): lax.all_gather(mix_weight, 'fsdp', axis=2, tiled=True)  12.7 us
    dot_general x9, matrix products, local(): accum = accum + jnp.dot(stacked, kernel, preferred_element_type=jnp.float32)  9.18 us
    unnamed x37, local copies, waits for them, and re-layouts  8.72 us
    concatenate x5, other arithmetic, local(): jnp.concatenate([padded[step:step + count_frames, row_tap:row_tap + heigh...  7.93 us
  transfers between devices with their start and end apart: 5, of which 3 were waited for; matrix products, arithmetic and copies ran while one was open for 2% of the time, Pallas kernels for 0%

commit v1 on v0

--- a/solution.py
+++ b/solution.py
@@ -77,9 +77,10 @@
             )
         )
     encoded = branch.astype(jnp.bfloat16).reshape(pooled.shape)
-    mix_grad = lax.psum_scatter(
-        jnp.stack(grad_terms).reshape(-1), ("tm", "fsdp"), scatter_dimension=0, tiled=True
-    )
+    parts = lax.axis_size("tm") * lax.axis_size("fsdp")
+    mix_grad = lax.all_to_all(
+        jnp.stack(grad_terms).reshape(parts, -1), ("tm", "fsdp"), 0, 0, tiled=True
+    ).sum(0)
     return (encoded, mix_grad)
 
 

time: 362 us -> 130 us (0.36)
  waiting for transfers between devices: 253 us -> 25.6 us
  between operations: 14.4 us -> 1.04 us
  starting transfers between devices: 23.5 us -> 32 us
    unnamed x2 -> x0, waiting for transfers between devices: 242 us -> none
    all_to_all x0 -> x1, waiting for transfers between devices: none -> 13.9 us  [local(): lax.all_to_all(jnp.stack(grad_terms).reshape(parts, -1), ('tm', 'fsdp'),...]
    all_to_all x0 -> x1, starting transfers between devices: none -> 8.54 us  [local(): lax.all_to_all(jnp.stack(grad_terms).reshape(parts, -1), ('tm', 'fsdp'),...]
    unnamed x37 -> x36, local copies, waits for them, and re-layouts: 8.72 us -> 7.4 us
  transfers between devices with their start and end apart: 5 -> 5, of which waited for: 3 -> 3; matrix products, arithmetic and copies ran while one was open for 2% -> 6% of each run, Pallas kernels for 0% -> 0%
where the time goes in v1:
time: 130 us
  starting transfers between devices  32 us (25%)
  blocking collectives  27.7 us (21%)
  waiting for transfers between devices  25.6 us (20%)
  local copies, waits for them, and re-layouts  17.5 us (13%)
  other arithmetic  13.8 us (11%)
  matrix products  11.9 us (9%)
    all_gather x1, blocking collectives, local(): lax.all_gather(conv_weight, 'fsdp', axis=4, tiled=True)  15 us
    all_to_all x1, waiting for transfers between devices, local(): lax.all_to_all(jnp.stack(grad_terms).reshape(parts, -1), ('tm', 'fsdp'),...  13.9 us
    all_to_all x1, starting transfers between devices, local(): lax.all_to_all(pool_pairs(hidden), 'tm', split_axis=1, concat_axis=0, til...  12.8 us
    all_gather x1, blocking collectives, local(): lax.all_gather(mix_weight, 'fsdp', axis=2, tiled=True)  12.7 us
    dot_general x9, matrix products, local(): accum = accum + jnp.dot(stacked, kernel, preferred_element_type=jnp.float32)  9.18 us
    all_to_all x1, starting transfers between devices, local(): lax.all_to_all(jnp.stack(grad_terms).reshape(parts, -1), ('tm', 'fsdp'),...  8.54 us
    concatenate x5, other arithmetic, local(): jnp.concatenate([padded[step:step + count_frames, row_tap:row_tap + heigh...  7.93 us
    unnamed x36, local copies, waits for them, and re-layouts  7.4 us
  transfers between devices with their start and end apart: 5, of which 3 were waited for; matrix products, arithmetic and copies ran while one was open for 6% of the time, Pallas kernels for 0%

profile of v1, /device:TPU:1, one launch (start us, length us, event | category | flops | bytes accessed | tf_op | source)
XLA Modules:
  0.0 129.5 jit_solution(5271844698895392121)
XLA Ops:
  0.7 4.1 %collective-permute-start = (bf16[2,64,32,128]{3,2,1,0:T(8,128)(2,1)}, bf16[2,64,32,128]{3,2,1,0:T(8,128)(2,1)S(1)}, u32[]{:S(2)}, u32[]{:S(2)}) collective-permute-start(bf16[2,64,32,128]{3,2,1,0:T(8,128)(2,1)} %param.4), channel_id=1, source_target_pairs={{0,8},{8,16},{16,24},{24,32},{32,40},{40,48},{48,56},{56,64},{64,7... | collective-permute-start | bytes 3145736 | tf_op jit(solution)/shard_map/ppermute | solution.py:10
  4.8 15.0 %all_gather.6 = bf16[3,3,3,128,128]{3,4,2,1,0:T(8,128)(2,1)S(1)} all-gather(bf16[3,3,3,128,16]{3,4,2,1,0:T(8,128)(2,1)} %param.5), channel_id=1, replica_groups=mesh['tm'=32,'fsdp'=8] {'fsdp'}, dimensions={4}, use_global_device_ids=true | all-gather | bytes 995328 | tf_op jit(solution)/shard_map/all_gather | solution.py:41
  19.8 7.0 %collective-permute-done = bf16[2,64,32,128]{3,2,1,0:T(8,128)(2,1)S(1)} collective-permute-done((bf16[2,64,32,128]{3,2,1,0:T(8,128)(2,1)}, bf16[2,64,32,128]{3,2,1,0:T(8,128)(2,1)S(1)}, u32[]{:S(2)}, u32[]{:S(2)}) %collective-permute-start) | collective-permute-done | bytes 1048608 | tf_op jit(solution)/shard_map/ppermute | solution.py:10
  27.1 0.9 fusion.17
  28.0 3.4 %collective-permute-start.2 = (bf16[4,64,1,128]{3,2,1,0:T(2,128)(2,1)}, bf16[4,64,1,128]{3,2,1,0:T(2,128)(2,1)S(1)}, u32[]{:S(2)}, u32[]{:S(2)}) collective-permute-start(bf16[4,64,1,128]{3,2,1,0:T(2,128)(2,1)} %get-tuple-element.30), channel_id=1, source_target_pairs={{1,0},{2,1},{3,2},{4,3},{5,4},{6,5},{7,6},{9,8},{10,9},{11,10},{12... | collective-permute-start | bytes 196616 | tf_op jit(solution)/shard_map/ppermute | solution.py:23
  31.5 3.1 %collective-permute-start.1 = (bf16[4,64,1,128]{3,2,1,0:T(2,128)(2,1)}, bf16[4,64,1,128]{3,2,1,0:T(2,128)(2,1)S(1)}, u32[]{:S(2)}, u32[]{:S(2)}) collective-permute-start(bf16[4,64,1,128]{3,2,1,0:T(2,128)(2,1)} %get-tuple-element.29), channel_id=1, source_target_pairs={{0,1},{1,2},{2,3},{3,4},{4,5},{5,6},{6,7},{8,9},{9,10},{10,11},{11... | collective-permute-start | bytes 196616 | tf_op jit(solution)/shard_map/ppermute | solution.py:21
  34.6 0.8 fusion.18
  35.3 1.6 %copy.19 = bf16[3,1,1,128,128]{4,3,0,2,1:T(8,128)(2,1)} copy(bf16[3,1,1,128,128]{3,4,2,1,0:T(8,128)(2,1)} %get-tuple-element.39) | data formatting | bytes 196608
  37.0 0.8 copy.20
  38.4 1.0 copy.26
  39.4 1.6 %copy.27 = bf16[3,1,1,128,128]{4,3,0,2,1:T(8,128)(2,1)} copy(bf16[3,1,1,128,128]{3,4,2,1,0:T(8,128)(2,1)} %get-tuple-element.31) | data formatting | bytes 196608
  41.1 1.5 %fusion.7 = bf16[4,66,34,128]{3,2,1,0:T(8,128)(2,1)S(1)} fusion(bf16[4,64,1,128]{3,2,1,0:T(2,128)(2,1)S(1)} %collective-permute-done.2, bf16[4,64,32,128]{3,2,1,0:T(8,128)(2,1)S(1)} %constant_dynamic-update-slice_fusion, bf16[4,64,1,128]{3,2,1,0:T(2,128)(2,1)S(1)} %collective-permute-done.1), kind=kLoop, calls=%fused_computation.30 | loop fusion | flops 13787136 | bytes 4526080 | tf_op jit(solution)/shard_map/concatenate | solution.py:19
  42.6 6.9 %fusion.16 = (bf16[2,64,32,128]{3,2,1,0:T(8,128)(2,1)S(1)}, bf16[2,64,32,128]{3,2,1,0:T(8,128)(2,1)S(1)}, bf16[2,64,32,128]{3,2,1,0:T(8,128)(2,1)S(1)}, bf16[2,6...) fusion(bf16[4,66,34,128]{3,2,1,0:T(8,128)(2,1)S(1)} %fusion.7), kind=kLoop, calls=%fused_computation.59 | loop fusion | bytes 37748736 | tf_op jit(solution)/shard_map/slice | solution.py:54
  49.5 3.3 %pad_maximum_fusion.2 = (bf16[2,64,32,384]{3,2,1,0:T(8,128)(2,1)S(1)}, bf16[2,64,32,384]{3,2,1,0:T(8,128)(2,1)S(1)}) fusion(bf16[2,64,32,128]{3,2,1,0:T(8,128)(2,1)} %get-tuple-element.16, bf16[2,64,32,128]{3,2,1,0:T(8,128)(2,1)} %get-tuple-element.17, bf16[2,64,32,128]{3,2,1,0:T(8,128)(2,1)} %get-tuple-element.18, ...), kind=kLoop, calls=%fused_computation.19 | loop fusion | flops 18874368 | bytes 12582912 | tf_op jit(solution)/shard_map/concatenate | solution.py:52
  52.8 1.0 fusion.19
  53.9 1.1 convolution_add_fusion.7
  55.0 0.3 copy-done.2
  55.4 0.3 copy-done.3
  55.7 0.3 copy-done.4
  56.0 0.9 pad_maximum_fusion.4
  56.9 1.0 convolution_add_fusion.6
  57.8 2.1 %fusion.10 = (bf16[2,64,32,128]{3,2,1,0:T(8,128)(2,1)S(1)}, bf16[2,64,32,128]{3,2,1,0:T(8,128)(2,1)S(1)}, bf16[2,64,32,128]{3,2,1,0:T(8,128)(2,1)S(1)}, bf16[2,6...) fusion(bf16[4,64,32,128]{3,2,1,0:T(8,128)(2,1)S(1)} %constant_dynamic-update-slice_fusion, ...), kind=kLoop, calls=%fused_computation.44 | loop fusion | flops 8388608 | bytes 8650752 | tf_op jit(solution)/shard_map/concatenate | solution.py:19
  60.0 2.5 %fusion.1 = (bf16[2,64,32,384]{3,2,1,0:T(8,128)(2,1)S(1)}, bf16[2,64,32,384]{3,2,1,0:T(8,128)(2,1)S(1)}) fusion(bf16[4,64,1,128]{3,2,1,0:T(2,128)(2,1)S(1)} %collective-permute-done.2, bf16[4,64,32,128]{3,2,1,0:T(8,128)(2,1)S(1)} %constant_dynamic-update-slice_fusion, bf16[2,64,32,128]{3,2,1,0:T(8,128)(2,1)S(1)} %get-tuple-element.21, ...), kind=kLoop, calls=%fused_computation.16 | loop fusion | flops 25165824 | bytes 12713984 | tf_op jit(solution)/shard_map/concatenate | solution.py:52
  62.5 1.0 convolution_add_fusion.5
  63.7 0.3 copy-done.8
  64.0 0.4 pad_maximum_fusion.5
  64.5 1.0 convolution_add_fusion.4
  65.5 1.0 convolution_add_fusion.3
  66.5 1.0 convolution_add_fusion.2
  67.5 0.9 pad_maximum_fusion.7
  68.4 1.0 convolution_add_fusion.1
  69.5 1.1 multiply_convert_fusion
  70.6 0.3 convert.1
  70.9 1.0 fusion.15
  71.9 12.8 %all-to-all-start = ((bf16[1,64,32,128]{3,2,0,1:T(8,128)(2,1)}), bf16[1,64,32,128]{3,2,0,1:T(8,128)(2,1)S(1)}, u32[]{:S(2)}, u32[]{:S(2)}) async-start(bf16[1,64,32,128]{3,2,0,1:T(8,128)(2,1)} %fusion.15), calls=%async_computation | async-start | bytes 1048576 | tf_op jit(solution)/shard_map/all_to_all | solution.py:67
  84.8 12.7 %all_gather.7 = bf16[3,128,128]{1,2,0:T(8,128)(2,1)S(1)} all-gather(bf16[3,128,16]{1,2,0:T(8,128)(2,1)S(1)} %copy-done.12), channel_id=1, replica_groups=mesh['tm'=32,'fsdp'=8] {'fsdp'}, dimensions={2}, use_global_device_ids=true | all-gather | bytes 110592 | tf_op jit(solution)/shard_map/all_gather | solution.py:42
  97.4 4.7 %all-to-all-done = bf16[1,64,32,128]{3,2,0,1:T(8,128)(2,1)S(1)} async-done(((bf16[1,64,32,128]{3,2,0,1:T(8,128)(2,1)}), bf16[1,64,32,128]{3,2,0,1:T(8,128)(2,1)S(1)}, u32[]{:S(2)}, u32[]{:S(2)}) %all-to-all-start) | async-done | bytes 524320 | tf_op jit(solution)/shard_map/all_to_all | solution.py:67
  102.1 0.2 pad_slice_fusion.8
  102.4 0.3 convolution_bitcast_fusion
  102.7 0.3 convolution_bitcast_fusion.1
  103.0 0.3 convolution_add_fusion.10
  103.3 0.3 convolution_bitcast_fusion.2
  103.7 1.1 all_to_all.22
  104.9 8.5 %all-to-all-start.1 = ((f32[256,1,192]{2,1,0:T(1,128)}), f32[256,1,192]{2,1,0:T(1,128)S(1)}, u32[]{:S(2)}, u32[]{:S(2)}) async-start(f32[256,1,192]{2,1,0:T(1,128)} %all_to_all.22), calls=%async_computation.1 | async-start | bytes 524288 | tf_op jit(solution)/shard_map/all_to_all | solution.py:81
  113.4 0.3 convolution_add_fusion.9
  113.7 1.1 fusion.8
  114.8 13.9 %all-to-all-done.1 = f32[256,1,192]{2,1,0:T(1,128)S(1)} async-done(((f32[256,1,192]{2,1,0:T(1,128)}), f32[256,1,192]{2,1,0:T(1,128)S(1)}, u32[]{:S(2)}, u32[]{:S(2)}) %all-to-all-start.1) | async-done | bytes 196640 | tf_op jit(solution)/shard_map/all_to_all | solution.py:81
  128.7 0.9 reduce_sum.9
  (32 shorter events, 1.3 us)
Async XLA Ops:
  0.6 101.7 %copy-start = (bf16[32,2,32,128]{3,2,1,0:T(8,128)(2,1)S(1)}, bf16[32,2,32,128]{3,2,1,0:T(8,128)(2,1)}, u32[]{:S(2)}) copy-start(bf16[32,2,32,128]{3,2,1,0:T(8,128)(2,1)} %param.7) | copy-start | bytes 1572868
  0.6 26.3 %copy-start.5 = (bf16[2,64,32,128]{3,2,1,0:T(8,128)(2,1)S(1)}, bf16[2,64,32,128]{3,2,1,0:T(8,128)(2,1)}, u32[]{:S(2)}) copy-start(bf16[2,64,32,128]{3,2,1,0:T(8,128)(2,1)} %param.4) | copy-start | bytes 3145732
  0.7 26.2 %collective-permute-start = (bf16[2,64,32,128]{3,2,1,0:T(8,128)(2,1)}, bf16[2,64,32,128]{3,2,1,0:T(8,128)(2,1)S(1)}, u32[]{:S(2)}, u32[]{:S(2)}) collective-permute-start(bf16[2,64,32,128]{3,2,1,0:T(8,128)(2,1)} %param.4), channel_id=1, source_target_pairs={{0,8},{8,16},{16,24},{24,32},{32,40},{40,48},{48,56},{56,64},{64,7... | collective-permute-start | bytes 3145736 | tf_op jit(solution)/shard_map/ppermute | solution.py:10
  26.9 8.5 %copy-start.7 = (bf16[2,64,32,128]{3,2,1,0:T(8,128)(2,1)}, bf16[2,64,32,128]{3,2,1,0:T(8,128)(2,1)S(1)}, u32[]{:S(2)}) copy-start(bf16[2,64,32,128]{3,2,1,0:T(8,128)(2,1)S(1)} %collective-permute-done) | copy-start | bytes 3145732
  28.0 13.0 %collective-permute-start.2 = (bf16[4,64,1,128]{3,2,1,0:T(2,128)(2,1)}, bf16[4,64,1,128]{3,2,1,0:T(2,128)(2,1)S(1)}, u32[]{:S(2)}, u32[]{:S(2)}) collective-permute-start(bf16[4,64,1,128]{3,2,1,0:T(2,128)(2,1)} %get-tuple-element.30), channel_id=1, source_target_pairs={{1,0},{2,1},{3,2},{4,3},{5,4},{6,5},{7,6},{9,8},{10,9},{11,10},{12... | collective-permute-start | bytes 196616 | tf_op jit(solution)/shard_map/ppermute | solution.py:23
  31.5 9.6 %collective-permute-start.1 = (bf16[4,64,1,128]{3,2,1,0:T(2,128)(2,1)}, bf16[4,64,1,128]{3,2,1,0:T(2,128)(2,1)S(1)}, u32[]{:S(2)}, u32[]{:S(2)}) collective-permute-start(bf16[4,64,1,128]{3,2,1,0:T(2,128)(2,1)} %get-tuple-element.29), channel_id=1, source_target_pairs={{0,1},{1,2},{2,3},{3,4},{4,5},{5,6},{6,7},{8,9},{9,10},{10,11},{11... | collective-permute-start | bytes 196616 | tf_op jit(solution)/shard_map/ppermute | solution.py:21
  49.5 3.3 %copy-start.10 = (bf16[3,1,1,128,128]{4,3,0,2,1:T(8,128)(2,1)S(1)}, bf16[3,1,1,128,128]{4,3,0,2,1:T(8,128)(2,1)}, u32[]{:S(2)}) copy-start(bf16[3,1,1,128,128]{4,3,0,2,1:T(8,128)(2,1)} %copy.19) | copy-start | bytes 294916
  52.8 1.0 copy-start.9
  53.8 1.2 copy-start.1
  53.8 1.5 %copy-start.2 = (bf16[2,64,32,128]{3,2,1,0:T(8,128)(2,1)S(1)}, bf16[2,64,32,128]{3,2,1,0:T(8,128)(2,1)}, u32[]{:S(2)}) copy-start(bf16[2,64,32,128]{3,2,1,0:T(8,128)(2,1)} %get-tuple-element.10) | copy-start | bytes 3145732
  53.8 1.8 %copy-start.3 = (bf16[2,64,32,128]{3,2,1,0:T(8,128)(2,1)S(1)}, bf16[2,64,32,128]{3,2,1,0:T(8,128)(2,1)}, u32[]{:S(2)}) copy-start(bf16[2,64,32,128]{3,2,1,0:T(8,128)(2,1)} %get-tuple-element.11) | copy-start | bytes 3145732
  53.8 2.1 %copy-start.4 = (bf16[2,64,32,128]{3,2,1,0:T(8,128)(2,1)S(1)}, bf16[2,64,32,128]{3,2,1,0:T(8,128)(2,1)}, u32[]{:S(2)}) copy-start(bf16[2,64,32,128]{3,2,1,0:T(8,128)(2,1)} %get-tuple-element.12) | copy-start | bytes 3145732
  62.5 1.2 copy-start.6
  62.5 1.5 %copy-start.8 = (bf16[2,64,32,128]{3,2,1,0:T(8,128)(2,1)S(1)}, bf16[2,64,32,128]{3,2,1,0:T(8,128)(2,1)}, u32[]{:S(2)}) copy-start(bf16[2,64,32,128]{3,2,1,0:T(8,128)(2,1)} %copy-done.7) | copy-start | bytes 3145732
  68.4 1.0 copy-start.11
  70.6 14.1 %copy-start.12 = (bf16[3,128,16]{1,2,0:T(8,128)(2,1)S(1)}, bf16[3,128,16]{1,2,0:T(8,128)(2,1)}, u32[]{:S(2)}) copy-start(bf16[3,128,16]{1,2,0:T(8,128)(2,1)} %param.6) | copy-start | bytes 36868
  71.9 30.2 %all-to-all-start = ((bf16[1,64,32,128]{3,2,0,1:T(8,128)(2,1)}), bf16[1,64,32,128]{3,2,0,1:T(8,128)(2,1)S(1)}, u32[]{:S(2)}, u32[]{:S(2)}) async-start(bf16[1,64,32,128]{3,2,0,1:T(8,128)(2,1)} %fusion.15), calls=%async_computation | async-start | bytes 1048576 | tf_op jit(solution)/shard_map/all_to_all | solution.py:67
  104.9 23.8 %all-to-all-start.1 = ((f32[256,1,192]{2,1,0:T(1,128)}), f32[256,1,192]{2,1,0:T(1,128)S(1)}, u32[]{:S(2)}, u32[]{:S(2)}) async-start(f32[256,1,192]{2,1,0:T(1,128)} %all_to_all.22), calls=%async_computation.1 | async-start | bytes 524288 | tf_op jit(solution)/shard_map/all_to_all | solution.py:81

commit v2 on v1

--- a/solution.py
+++ b/solution.py
@@ -37,10 +37,15 @@
 
 
 def local(frames, conv_weight, mix_weight, cotangent):
-    full_conv, full_mix = (
-        lax.all_gather(conv_weight, "fsdp", axis=4, tiled=True),
-        lax.all_gather(mix_weight, "fsdp", axis=2, tiled=True),
+    channels_out = conv_weight.shape[-1]
+    shards = jnp.concatenate(
+        [conv_weight.reshape(-1, channels_out), mix_weight.reshape(-1, channels_out)], axis=0
     )
+    gathered = lax.all_gather(shards, "fsdp", axis=0, tiled=False)
+    gathered = jnp.transpose(gathered, (1, 0, 2)).reshape(shards.shape[0], -1)
+    split = conv_weight.size // channels_out
+    full_conv = gathered[:split].reshape(conv_weight.shape[:-1] + (-1,))
+    full_mix = gathered[split:].reshape(mix_weight.shape[:-1] + (-1,))
     count_frames, height, width, channels = frames.shape
     previous = from_behind(frames, "tm", 1)
     timed = jnp.concatenate([previous, frames], axis=0)

time: 130 us -> 141 us (1.085)
  local copies, waits for them, and re-layouts: 17.5 us -> 31.5 us
  blocking collectives: 27.7 us -> 14.9 us
  waiting for transfers between devices: 25.6 us -> 31.3 us
  starting transfers between devices: 32 us -> 34 us
    all_gather x2 -> x1, blocking collectives: 27.7 us -> 14.9 us  [local(): gathered = lax.all_gather(shards, 'fsdp', axis=0, tiled=False)]
    slice x1 -> x10, local copies, waits for them, and re-layouts: 0.76 us -> 13.4 us  [local(): kernel = full_conv[:, row_tap, col_tap].reshape(3 * channels, channels)]
    all_to_all x1, waiting for transfers between devices: 4.69 us -> 15.6 us  [local(): lax.all_to_all(pool_pairs(hidden), 'tm', split_axis=1, concat_axis=0, til...]
    ppermute x1, waiting for transfers between devices: 7.05 us -> 2.19 us  [from_behind(): return lax.ppermute(block, axis, route)]
    unnamed x36 -> x32, local copies, waits for them, and re-layouts: 7.4 us -> 4.6 us
    reshape x0 -> x3, local copies, waits for them, and re-layouts: none -> 1.98 us  [the longest x1 1.17 us: local(): full_conv = gathered[:split].reshape(conv_weight.shape[:-1] + (-1,))]
    ppermute x1, starting transfers between devices: 3.44 us -> 1.92 us  [with_halo(): lax.ppermute(head, axis, [((i + 1) % count, i) for i in range(ends)])]
    ppermute x1, starting transfers between devices: 3.1 us -> 4.62 us  [with_halo(): lax.ppermute(tail, axis, [(i, (i + 1) % count) for i in range(ends)])]
  transfers between devices with their start and end apart: 5 -> 5, of which waited for: 3 -> 3; matrix products, arithmetic and copies ran while one was open for 6% -> 14% of each run, Pallas kernels for 0% -> 0%
where the time goes in v2:
time: 141 us; the launch traced here: 140 us
  starting transfers between devices  34 us (24%)
  local copies, waits for them, and re-layouts  31.5 us (22%)
  waiting for transfers between devices  31.3 us (22%)
  other arithmetic  15 us (11%)
  blocking collectives  14.9 us (11%)
  matrix products  11.9 us (8%)
    all_to_all x1, waiting for transfers between devices, local(): lax.all_to_all(pool_pairs(hidden), 'tm', split_axis=1, concat_axis=0, til...  15.6 us
    all_gather x1, blocking collectives, local(): gathered = lax.all_gather(shards, 'fsdp', axis=0, tiled=False)  14.9 us
    all_to_all x1, waiting for transfers between devices, local(): lax.all_to_all(jnp.stack(grad_terms).reshape(parts, -1), ('tm', 'fsdp'),...  13.5 us
    slice x10, local copies, waits for them, and re-layouts, local(): kernel = full_conv[:, row_tap, col_tap].reshape(3 * channels, channels)  13.4 us
    all_to_all x1, starting transfers between devices, local(): lax.all_to_all(pool_pairs(hidden), 'tm', split_axis=1, concat_axis=0, til...  12.9 us
    all_to_all x1, starting transfers between devices, local(): lax.all_to_all(jnp.stack(grad_terms).reshape(parts, -1), ('tm', 'fsdp'),...  9.52 us
    dot_general x9, matrix products, local(): accum = accum + jnp.dot(stacked, kernel, preferred_element_type=jnp.float32)  9.2 us
    concatenate x5, other arithmetic, local(): jnp.concatenate([padded[step:step + count_frames, row_tap:row_tap + heigh...  9.19 us
  transfers between devices with their start and end apart: 5, of which 3 were waited for; matrix products, arithmetic and copies ran while one was open for 14% of the time, Pallas kernels for 0%

profile of v2, /device:TPU:1, one launch (start us, length us, event | category | flops | bytes accessed | tf_op | source)
XLA Modules:
  0.0 139.7 jit_solution(10097987589259066946)
XLA Ops:
  0.6 5.1 %collective-permute-start = (bf16[2,64,32,128]{3,2,1,0:T(8,128)(2,1)}, bf16[2,64,32,128]{3,2,1,0:T(8,128)(2,1)}, u32[]{:S(2)}, u32[]{:S(2)}) collective-permute-start(bf16[2,64,32,128]{3,2,1,0:T(8,128)(2,1)} %param.4), channel_id=1, source_target_pairs={{0,8},{8,16},{16,24},{24,32},{32,40},{40,48},{48,56},{56,64},{64,7... | collective-permute-start | bytes 3145736 | tf_op jit(solution)/shard_map/ppermute | solution.py:10
  5.7 1.0 copy.21
  6.8 0.7 copy_bitcast_fusion
  7.5 14.9 %all-gather = bf16[30720,16]{0,1:T(8,128)(2,1)S(1)} all-gather(bf16[3840,16]{0,1:T(8,128)(2,1)S(1)} %pad_maximum_fusion.10), channel_id=2, replica_groups=mesh['tm'=32,'fsdp'=8] {'fsdp'}, dimensions={0}, use_global_device_ids=true | all-gather | bytes 1105920 | tf_op jit(solution)/shard_map/all_gather | solution.py:44
  22.5 1.0 copy-done.7
  23.5 1.2 reshape.124
  24.7 2.2 %collective-permute-done = bf16[2,64,32,128]{3,2,1,0:T(8,128)(2,1)} collective-permute-done((bf16[2,64,32,128]{3,2,1,0:T(8,128)(2,1)}, bf16[2,64,32,128]{3,2,1,0:T(8,128)(2,1)}, u32[]{:S(2)}, u32[]{:S(2)}) %collective-permute-start) | collective-permute-done | bytes 1048608 | tf_op jit(solution)/shard_map/ppermute | solution.py:10
  26.9 1.3 constant_dynamic-update-slice_fusion.1
  28.2 1.4 constant_dynamic-update-slice_fusion
  29.5 0.9 fusion.17
  30.5 4.6 %collective-permute-start.1 = (bf16[4,64,1,128]{3,2,1,0:T(2,128)(2,1)}, bf16[4,64,1,128]{3,2,1,0:T(2,128)(2,1)S(1)}, u32[]{:S(2)}, u32[]{:S(2)}) collective-permute-start(bf16[4,64,1,128]{3,2,1,0:T(2,128)(2,1)} %get-tuple-element.29), channel_id=1, source_target_pairs={{0,1},{1,2},{2,3},{3,4},{4,5},{5,6},{6,7},{8,9},{9,10},{10,11},{11... | collective-permute-start | bytes 196616 | tf_op jit(solution)/shard_map/ppermute | solution.py:21
  35.1 1.9 %collective-permute-start.2 = (bf16[4,64,1,128]{3,2,1,0:T(2,128)(2,1)}, bf16[4,64,1,128]{3,2,1,0:T(2,128)(2,1)S(1)}, u32[]{:S(2)}, u32[]{:S(2)}) collective-permute-start(bf16[4,64,1,128]{3,2,1,0:T(2,128)(2,1)} %get-tuple-element.30), channel_id=1, source_target_pairs={{1,0},{2,1},{3,2},{4,3},{5,4},{6,5},{7,6},{9,8},{10,9},{11,10},{12... | collective-permute-start | bytes 196616 | tf_op jit(solution)/shard_map/ppermute | solution.py:23
  37.0 2.3 %fusion.18 = (bf16[3,1,1,128,128]{3,2,1,0,4:T(2,128)(2,1)S(1)}, bf16[3,1,1,128,128]{3,2,1,0,4:T(2,128)(2,1)S(1)}, bf16[3,1,1,128,128]{3,2,1,0,4:T(2,128)(2,1)S(1...) fusion(bf16[3,3,3,128,128]{3,2,1,0,4:T(4,128)(2,1)S(1)} %copy-d, ...), kind=kLoop, calls=%fused_computation.61 | loop fusion | bytes 1769472 | tf_op jit(solution)/shard_map/slice | solution.py:69
  39.3 1.7 %copy.24 = bf16[3,1,1,128,128]{4,3,0,2,1:T(8,128)(2,1)} copy(bf16[3,1,1,128,128]{3,2,1,0,4:T(2,128)(2,1)} %get-tuple-element.39) | data formatting | bytes 196608 | tf_op jit(solution)/shard_map/slice | solution.py:69
  41.0 1.7 %copy.25 = bf16[3,1,1,128,128]{4,3,0,2,1:T(8,128)(2,1)} copy(bf16[3,1,1,128,128]{3,2,1,0,4:T(2,128)(2,1)} %get-tuple-element.38) | data formatting | bytes 196608 | tf_op jit(solution)/shard_map/slice | solution.py:69
  42.7 1.7 %copy.26 = bf16[3,1,1,128,128]{4,3,0,2,1:T(8,128)(2,1)} copy(bf16[3,1,1,128,128]{3,2,1,0,4:T(2,128)(2,1)} %get-tuple-element.37) | data formatting | bytes 196608 | tf_op jit(solution)/shard_map/slice | solution.py:69
  44.3 1.7 %copy.27 = bf16[3,1,1,128,128]{4,3,0,2,1:T(8,128)(2,1)} copy(bf16[3,1,1,128,128]{3,2,1,0,4:T(2,128)(2,1)} %get-tuple-element.36) | data formatting | bytes 196608 | tf_op jit(solution)/shard_map/slice | solution.py:69
  46.0 1.7 %copy.28 = bf16[3,1,1,128,128]{4,3,0,2,1:T(8,128)(2,1)} copy(bf16[3,1,1,128,128]{3,2,1,0,4:T(2,128)(2,1)} %get-tuple-element.35) | data formatting | bytes 196608 | tf_op jit(solution)/shard_map/slice | solution.py:69
  47.7 1.7 %copy.29 = bf16[3,1,1,128,128]{4,3,0,2,1:T(8,128)(2,1)} copy(bf16[3,1,1,128,128]{3,2,1,0,4:T(2,128)(2,1)} %get-tuple-element.34) | data formatting | bytes 196608 | tf_op jit(solution)/shard_map/slice | solution.py:69
  49.4 0.8 copy.30
  50.4 1.6 %fusion.7 = bf16[4,66,34,128]{3,2,1,0:T(8,128)(2,1)S(1)} fusion(bf16[4,64,1,128]{3,2,1,0:T(2,128)(2,1)S(1)} %collective-permute-done.2, bf16[4,64,32,128]{3,2,1,0:T(8,128)(2,1)S(1)} %constant_dynamic-update-slice_fusion, bf16[4,64,1,128]{3,2,1,0:T(2,128)(2,1)S(1)} %collective-permute-done.1), kind=kLoop, calls=%fused_computation.30 | loop fusion | flops 13787136 | bytes 4526080 | tf_op jit(solution)/shard_map/concatenate | solution.py:19
  52.0 6.9 %fusion.16 = (bf16[2,64,32,128]{3,2,1,0:T(8,128)(2,1)S(1)}, bf16[2,64,32,128]{3,2,1,0:T(8,128)(2,1)S(1)}, bf16[2,64,32,128]{3,2,1,0:T(8,128)(2,1)S(1)}, bf16[2,6...) fusion(bf16[4,66,34,128]{3,2,1,0:T(8,128)(2,1)S(1)} %fusion.7), kind=kLoop, calls=%fused_computation.59 | loop fusion | bytes 37748736 | tf_op jit(solution)/shard_map/slice | solution.py:59
  59.0 3.3 %pad_maximum_fusion.2 = (bf16[2,64,32,384]{3,2,1,0:T(8,128)(2,1)S(1)}, bf16[2,64,32,384]{3,2,1,0:T(8,128)(2,1)S(1)}) fusion(bf16[2,64,32,128]{3,2,1,0:T(8,128)(2,1)} %get-tuple-element.16, bf16[2,64,32,128]{3,2,1,0:T(8,128)(2,1)} %get-tuple-element.17, bf16[2,64,32,128]{3,2,1,0:T(8,128)(2,1)} %get-tuple-element.18, ...), kind=kLoop, calls=%fused_computation.19 | loop fusion | flops 18874368 | bytes 12582912 | tf_op jit(solution)/shard_map/concatenate | solution.py:57
  62.2 1.0 fusion.20
  63.3 1.1 convolution_add_fusion.7
  65.4 0.9 pad_maximum_fusion.4
  66.3 1.0 convolution_add_fusion.6
  67.3 2.1 %fusion.10 = (bf16[2,64,32,128]{3,2,1,0:T(8,128)(2,1)S(1)}, bf16[2,64,32,128]{3,2,1,0:T(8,128)(2,1)S(1)}, bf16[2,64,32,128]{3,2,1,0:T(8,128)(2,1)S(1)}, bf16[2,6...) fusion(bf16[4,64,32,128]{3,2,1,0:T(8,128)(2,1)S(1)} %constant_dynamic-update-slice_fusion, ...), kind=kLoop, calls=%fused_computation.44 | loop fusion | flops 8388608 | bytes 8650752 | tf_op jit(solution)/shard_map/concatenate | solution.py:19
  69.4 2.5 %fusion.1 = (bf16[2,64,32,384]{3,2,1,0:T(8,128)(2,1)S(1)}, bf16[2,64,32,384]{3,2,1,0:T(8,128)(2,1)S(1)}) fusion(bf16[4,64,1,128]{3,2,1,0:T(2,128)(2,1)S(1)} %collective-permute-done.2, bf16[4,64,32,128]{3,2,1,0:T(8,128)(2,1)S(1)} %constant_dynamic-update-slice_fusion, bf16[2,64,32,128]{3,2,1,0:T(8,128)(2,1)S(1)} %get-tuple-element.21, ...), kind=kLoop, calls=%fused_computation.16 | loop fusion | flops 25165824 | bytes 12713984 | tf_op jit(solution)/shard_map/concatenate | solution.py:57
  72.0 1.0 convolution_add_fusion.5
  73.2 1.7 %pad_maximum_fusion.5 = bf16[2,64,32,384]{3,2,1,0:T(8,128)(2,1)S(1)} fusion(bf16[2,64,32,128]{3,2,1,0:T(8,128)(2,1)S(1)} %copy-done.6, bf16[2,64,32,128]{3,2,1,0:T(8,128)(2,1)S(1)} %get-tuple-element.28, bf16[2,64,32,128]{3,2,1,0:T(8,128)(2,1)} %collective-permute-done), kind=kLoop, calls=%fused_computation.22 | loop fusion | flops 9437184 | bytes 6291456 | tf_op jit(solution)/shard_map/concatenate | solution.py:57
  74.9 1.0 convolution_add_fusion.4
  75.9 1.0 convolution_add_fusion.3
  77.0 1.0 convolution_add_fusion.2
  78.0 0.9 pad_maximum_fusion.7
  78.9 1.0 convolution_add_fusion.1
  79.9 1.1 multiply_convert_fusion
  81.3 1.0 fusion.15
  82.4 12.9 %all-to-all-start = ((bf16[1,64,32,128]{3,2,0,1:T(8,128)(2,1)}), bf16[1,64,32,128]{3,2,0,1:T(8,128)(2,1)S(1)}, u32[]{:S(2)}, u32[]{:S(2)}) async-start(bf16[1,64,32,128]{3,2,0,1:T(8,128)(2,1)} %fusion.15), calls=%async_computation | async-start | bytes 1048576 | tf_op jit(solution)/shard_map/all_to_all | solution.py:72
  95.3 0.8 fusion.19
  96.1 15.6 %all-to-all-done = bf16[1,64,32,128]{3,2,0,1:T(8,128)(2,1)S(1)} async-done(((bf16[1,64,32,128]{3,2,0,1:T(8,128)(2,1)}), bf16[1,64,32,128]{3,2,0,1:T(8,128)(2,1)S(1)}, u32[]{:S(2)}, u32[]{:S(2)}) %all-to-all-start) | async-done | bytes 524320 | tf_op jit(solution)/shard_map/all_to_all | solution.py:72
  112.0 0.3 convolution_bitcast_fusion.1
  112.6 0.3 convolution_bitcast_fusion.2
  113.0 1.1 all_to_all.22
  114.1 9.5 %all-to-all-start.1 = ((f32[256,1,192]{2,1,0:T(1,128)}), f32[256,1,192]{2,1,0:T(1,128)S(1)}, u32[]{:S(2)}, u32[]{:S(2)}) async-start(f32[256,1,192]{2,1,0:T(1,128)} %all_to_all.22), calls=%async_computation.1 | async-start | bytes 524288 | tf_op jit(solution)/shard_map/all_to_all | solution.py:86
  124.2 1.1 fusion.8
  125.3 13.5 %all-to-all-done.1 = f32[256,1,192]{2,1,0:T(1,128)S(1)} async-done(((f32[256,1,192]{2,1,0:T(1,128)}), f32[256,1,192]{2,1,0:T(1,128)S(1)}, u32[]{:S(2)}, u32[]{:S(2)}) %all-to-all-start.1) | async-done | bytes 196640 | tf_op jit(solution)/shard_map/all_to_all | solution.py:86
  138.9 0.9 reduce_sum.9
  (43 shorter events, 3.3 us)
Async XLA Ops:
  0.6 111.0 %copy-start = (bf16[32,2,32,128]{3,2,1,0:T(8,128)(2,1)S(1)}, bf16[32,2,32,128]{3,2,1,0:T(8,128)(2,1)}, u32[]{:S(2)}) copy-start(bf16[32,2,32,128]{3,2,1,0:T(8,128)(2,1)} %param.7) | copy-start | bytes 1572868
  0.6 26.2 %collective-permute-start = (bf16[2,64,32,128]{3,2,1,0:T(8,128)(2,1)}, bf16[2,64,32,128]{3,2,1,0:T(8,128)(2,1)}, u32[]{:S(2)}, u32[]{:S(2)}) collective-permute-start(bf16[2,64,32,128]{3,2,1,0:T(8,128)(2,1)} %param.4), channel_id=1, source_target_pairs={{0,8},{8,16},{16,24},{24,32},{32,40},{40,48},{48,56},{56,64},{64,7... | collective-permute-start | bytes 3145736 | tf_op jit(solution)/shard_map/ppermute | solution.py:10
  22.5 1.0 copy-start.7
  24.7 12.4 %copy-start.1 = (bf16[3,3,3,128,128]{3,2,1,0,4:T(4,128)(2,1)S(1)}, bf16[3,3,3,128,128]{3,2,1,0,4:T(4,128)(2,1)}, u32[]{:S(2)}) copy-start(bf16[3,3,3,128,128]{3,2,1,0,4:T(4,128)(2,1)} %reshape.124) | copy-start | bytes 2654212
  30.5 20.0 %collective-permute-start.1 = (bf16[4,64,1,128]{3,2,1,0:T(2,128)(2,1)}, bf16[4,64,1,128]{3,2,1,0:T(2,128)(2,1)S(1)}, u32[]{:S(2)}, u32[]{:S(2)}) collective-permute-start(bf16[4,64,1,128]{3,2,1,0:T(2,128)(2,1)} %get-tuple-element.29), channel_id=1, source_target_pairs={{0,1},{1,2},{2,3},{3,4},{4,5},{5,6},{6,7},{8,9},{9,10},{10,11},{11... | collective-permute-start | bytes 196616 | tf_op jit(solution)/shard_map/ppermute | solution.py:21
  35.1 15.3 %collective-permute-start.2 = (bf16[4,64,1,128]{3,2,1,0:T(2,128)(2,1)}, bf16[4,64,1,128]{3,2,1,0:T(2,128)(2,1)S(1)}, u32[]{:S(2)}, u32[]{:S(2)}) collective-permute-start(bf16[4,64,1,128]{3,2,1,0:T(2,128)(2,1)} %get-tuple-element.30), channel_id=1, source_target_pairs={{1,0},{2,1},{3,2},{4,3},{5,4},{6,5},{7,6},{9,8},{10,9},{11,10},{12... | collective-permute-start | bytes 196616 | tf_op jit(solution)/shard_map/ppermute | solution.py:23
  58.9 3.3 %copy-start.14 = (bf16[3,1,1,128,128]{4,3,0,2,1:T(8,128)(2,1)S(1)}, bf16[3,1,1,128,128]{4,3,0,2,1:T(8,128)(2,1)}, u32[]{:S(2)}) copy-start(bf16[3,1,1,128,128]{4,3,0,2,1:T(8,128)(2,1)} %copy.24) | copy-start | bytes 294916
  62.2 1.0 copy-start.13
  63.2 1.2 copy-start.2
  63.2 1.5 %copy-start.3 = (bf16[2,64,32,128]{3,2,1,0:T(8,128)(2,1)S(1)}, bf16[2,64,32,128]{3,2,1,0:T(8,128)(2,1)}, u32[]{:S(2)}) copy-start(bf16[2,64,32,128]{3,2,1,0:T(8,128)(2,1)} %get-tuple-element.10) | copy-start | bytes 3145732
  63.3 1.8 %copy-start.4 = (bf16[2,64,32,128]{3,2,1,0:T(8,128)(2,1)S(1)}, bf16[2,64,32,128]{3,2,1,0:T(8,128)(2,1)}, u32[]{:S(2)}) copy-start(bf16[2,64,32,128]{3,2,1,0:T(8,128)(2,1)} %get-tuple-element.11) | copy-start | bytes 3145732
  63.3 2.1 %copy-start.5 = (bf16[2,64,32,128]{3,2,1,0:T(8,128)(2,1)S(1)}, bf16[2,64,32,128]{3,2,1,0:T(8,128)(2,1)}, u32[]{:S(2)}) copy-start(bf16[2,64,32,128]{3,2,1,0:T(8,128)(2,1)} %get-tuple-element.12) | copy-start | bytes 3145732
  65.4 0.9 copy-start.12
  69.4 2.5 %copy-start.11 = (bf16[3,1,1,128,128]{4,3,0,2,1:T(8,128)(2,1)S(1)}, bf16[3,1,1,128,128]{4,3,0,2,1:T(8,128)(2,1)}, u32[]{:S(2)}) copy-start(bf16[3,1,1,128,128]{4,3,0,2,1:T(8,128)(2,1)} %copy.27) | copy-start | bytes 294916
  72.0 1.2 copy-start.6
  73.2 1.7 %copy-start.10 = (bf16[3,1,1,128,128]{4,3,0,2,1:T(8,128)(2,1)S(1)}, bf16[3,1,1,128,128]{4,3,0,2,1:T(8,128)(2,1)}, u32[]{:S(2)}) copy-start(bf16[3,1,1,128,128]{4,3,0,2,1:T(8,128)(2,1)} %copy.28) | copy-start | bytes 294916
  74.9 1.0 copy-start.9
  75.9 1.0 copy-start.8
  82.4 29.3 %all-to-all-start = ((bf16[1,64,32,128]{3,2,0,1:T(8,128)(2,1)}), bf16[1,64,32,128]{3,2,0,1:T(8,128)(2,1)S(1)}, u32[]{:S(2)}, u32[]{:S(2)}) async-start(bf16[1,64,32,128]{3,2,0,1:T(8,128)(2,1)} %fusion.15), calls=%async_computation | async-start | bytes 1048576 | tf_op jit(solution)/shard_map/all_to_all | solution.py:72
  114.1 24.8 %all-to-all-start.1 = ((f32[256,1,192]{2,1,0:T(1,128)}), f32[256,1,192]{2,1,0:T(1,128)S(1)}, u32[]{:S(2)}, u32[]{:S(2)}) async-start(f32[256,1,192]{2,1,0:T(1,128)} %all_to_all.22), calls=%async_computation.1 | async-start | bytes 524288 | tf_op jit(solution)/shard_map/all_to_all | solution.py:86

commit v3 on v0

--- a/solution.py
+++ b/solution.py
@@ -1,7 +1,11 @@
 import jax
 import jax.numpy as jnp
 from jax import lax
+from jax.experimental import pallas as pl
+from jax.experimental.pallas import tpu as pltpu
 from jax.sharding import PartitionSpec as P
+
+MESH = pl.DeviceIdType.MESH
 
 
 def from_behind(block, axis, distance):
@@ -34,6 +38,132 @@
 
 def delayed(block, offset):
     return jnp.pad(block, ((offset, 0), (0, 0), (0, 0), (0, 0)))[: block.shape[0]]
+
+
+def exchange_kernel(x_ref, o_ref, send_sem, recv_sem, local_sem):
+    count, rows = o_ref.shape[0], o_ref.shape[1]
+    me = lax.axis_index("tm")
+    barrier = pltpu.get_barrier_semaphore()
+    for k in range(1, count):
+        pl.semaphore_signal(
+            barrier, inc=1, device_id={"tm": lax.rem(me + k, count)}, device_id_type=MESH
+        )
+    pl.semaphore_wait(barrier, count - 1)
+    local = pltpu.make_async_copy(
+        x_ref.at[0, pl.ds(me * rows, rows)], o_ref.at[me], local_sem
+    )
+    local.start()
+    copies = []
+    for k in range(1, count):
+        peer = lax.rem(me + k, count)
+        copy = pltpu.make_async_remote_copy(
+            src_ref=x_ref.at[0, pl.ds(peer * rows, rows)],
+            dst_ref=o_ref.at[me],
+            send_sem=send_sem.at[k],
+            recv_sem=recv_sem.at[k],
+            device_id={"tm": peer},
+            device_id_type=MESH,
+        )
+        copy.start()
+        copies.append(copy)
+    local.wait()
+    for copy in copies:
+        copy.wait()
+
+
+def exchange_rows(block):
+    count = lax.axis_size("tm")
+    _, height, width, channels = block.shape
+    return pl.pallas_call(
+        exchange_kernel,
+        out_shape=jax.ShapeDtypeStruct((count, height // count, width, channels), block.dtype),
+        in_specs=[pl.BlockSpec(memory_space=pltpu.VMEM)],
+        out_specs=pl.BlockSpec(memory_space=pltpu.VMEM),
+        scratch_shapes=[
+            pltpu.SemaphoreType.DMA((count,)),
+            pltpu.SemaphoreType.DMA((count,)),
+            pltpu.SemaphoreType.DMA,
+        ],
+        compiler_params=pltpu.CompilerParams(collective_id=0, has_side_effects=True),
+    )(block)
+
+
+def scatter_kernel(p_ref, o_ref, first, second, summed, s1, r1, s2, r2, l1, l2):
+    groups, count = first.shape[0], second.shape[0]
+    f, t = lax.axis_index("fsdp"), lax.axis_index("tm")
+    barrier = pltpu.get_barrier_semaphore()
+    for k in range(1, groups):
+        pl.semaphore_signal(
+            barrier, inc=1, device_id={"fsdp": lax.rem(f + k, groups)}, device_id_type=MESH
+        )
+    for k in range(1, count):
+        pl.semaphore_signal(
+            barrier, inc=1, device_id={"tm": lax.rem(t + k, count)}, device_id_type=MESH
+        )
+    pl.semaphore_wait(barrier, groups - 1 + count - 1)
+    local = pltpu.make_async_copy(p_ref.at[f], first.at[f], l1)
+    local.start()
+    copies = []
+    for k in range(1, groups):
+        peer = lax.rem(f + k, groups)
+        copy = pltpu.make_async_remote_copy(
+            src_ref=p_ref.at[peer],
+            dst_ref=first.at[f],
+            send_sem=s1.at[k],
+            recv_sem=r1.at[k],
+            device_id={"fsdp": peer},
+            device_id_type=MESH,
+        )
+        copy.start()
+        copies.append(copy)
+    local.wait()
+    for copy in copies:
+        copy.wait()
+    summed[...] = jnp.sum(first[...], axis=0)
+    local = pltpu.make_async_copy(summed.at[t], second.at[t], l2)
+    local.start()
+    copies = []
+    for k in range(1, count):
+        peer = lax.rem(t + k, count)
+        copy = pltpu.make_async_remote_copy(
+            src_ref=summed.at[peer],
+            dst_ref=second.at[t],
+            send_sem=s2.at[k],
+            recv_sem=r2.at[k],
+            device_id={"tm": peer},
+            device_id_type=MESH,
+        )
+        copy.start()
+        copies.append(copy)
+    local.wait()
+    for copy in copies:
+        copy.wait()
+    o_ref[...] = jnp.sum(second[...], axis=0)
+
+
+def scatter_sum(partial):
+    groups, count = lax.axis_size("fsdp"), lax.axis_size("tm")
+    piece = partial.size // (groups * count)
+    arranged = jnp.transpose(partial.reshape(count, groups, 1, piece), (1, 0, 2, 3))
+    out = pl.pallas_call(
+        scatter_kernel,
+        out_shape=jax.ShapeDtypeStruct((1, piece), jnp.float32),
+        in_specs=[pl.BlockSpec(memory_space=pltpu.VMEM)],
+        out_specs=pl.BlockSpec(memory_space=pltpu.VMEM),
+        scratch_shapes=[
+            pltpu.VMEM((groups, count, 1, piece), jnp.float32),
+            pltpu.VMEM((count, 1, piece), jnp.float32),
+            pltpu.VMEM((count, 1, piece), jnp.float32),
+            pltpu.SemaphoreType.DMA((groups,)),
+            pltpu.SemaphoreType.DMA((groups,)),
+            pltpu.SemaphoreType.DMA((count,)),
+            pltpu.SemaphoreType.DMA((count,)),
+            pltpu.SemaphoreType.DMA,
+            pltpu.SemaphoreType.DMA,
+        ],
+        compiler_params=pltpu.CompilerParams(collective_id=1, has_side_effects=True),
+    )(arranged)
+    return out.reshape(piece)
 
 
 def local(frames, conv_weight, mix_weight, cotangent):
@@ -64,7 +194,7 @@
             kernel = full_conv[:, row_tap, col_tap].reshape(3 * channels, channels)
             accum = accum + jnp.dot(stacked, kernel, preferred_element_type=jnp.float32)
     hidden = jax.nn.silu(accum).astype(jnp.bfloat16).reshape(count_frames, height, width, channels)
-    pooled = lax.all_to_all(pool_pairs(hidden), "tm", split_axis=1, concat_axis=0, tiled=True)
+    pooled = exchange_rows(pool_pairs(hidden))
     branch = pooled.astype(jnp.float32).reshape(-1, channels)
     flat_cot = cotangent.reshape(-1, channels)
     grad_terms = []
@@ -77,9 +207,7 @@
             )
         )
     encoded = branch.astype(jnp.bfloat16).reshape(pooled.shape)
-    mix_grad = lax.psum_scatter(
-        jnp.stack(grad_terms).reshape(-1), ("tm", "fsdp"), scatter_dimension=0, tiled=True
-    )
+    mix_grad = scatter_sum(jnp.stack(grad_terms).reshape(-1))
     return (encoded, mix_grad)
 
 

time: 362 us -> 138 us (0.38)
  waiting for transfers between devices: 253 us -> 7.05 us
  Pallas kernels: 0 us -> 45.5 us
  between operations: 14.4 us -> 1.07 us
  starting transfers between devices: 23.5 us -> 10.7 us
    unnamed x2 -> x0, waiting for transfers between devices: 242 us -> none
    pallas_call x0 -> x2, Pallas kernels: none -> 45.5 us  [the longest x1 27 us: exchange_rows(): pl.pallas_call(exchange_kernel, out_shape=jax.ShapeDtypeStruct((count, he...]
    all_to_all x1 -> x0, starting transfers between devices: 12.8 us -> none  [local(): lax.all_to_all(pool_pairs(hidden), 'tm', split_axis=1, concat_axis=0, til...]
    all_to_all x1 -> x0, waiting for transfers between devices: 4.6 us -> none  [local(): lax.all_to_all(pool_pairs(hidden), 'tm', split_axis=1, concat_axis=0, til...]
    unnamed x37 -> x43, local copies, waits for them, and re-layouts: 8.72 us -> 7.98 us
  transfers between devices with their start and end apart: 5 -> 3, of which waited for: 3 -> 1; matrix products, arithmetic and copies ran while one was open for 2% -> 5% of each run, Pallas kernels for 0% -> 0%
where the time goes in v3:
time: 138 us
  Pallas kernels  45.5 us (33%)
  blocking collectives  28.6 us (21%)
  local copies, waits for them, and re-layouts  19.1 us (14%)
  matrix products  13 us (9%)
  other arithmetic  12.9 us (9%)
  starting transfers between devices  10.7 us (8%)
  waiting for transfers between devices  7.05 us (5%)
    pallas_call x1, Pallas kernels, exchange_rows(): pl.pallas_call(exchange_kernel, out_shape=jax.ShapeDtypeStruct((count, he...  27 us
    pallas_call x1, Pallas kernels, scatter_sum(): pl.pallas_call(scatter_kernel, out_shape=jax.ShapeDtypeStruct((1, piece),...  18.5 us
    all_gather x1, blocking collectives, local(): lax.all_gather(conv_weight, 'fsdp', axis=4, tiled=True)  15 us
    all_gather x1, blocking collectives, local(): lax.all_gather(mix_weight, 'fsdp', axis=2, tiled=True)  13.6 us
    dot_general x9, matrix products, local(): accum = accum + jnp.dot(stacked, kernel, preferred_element_type=jnp.float32)  9.23 us
    unnamed x43, local copies, waits for them, and re-layouts  7.98 us
    concatenate x5, other arithmetic, local(): jnp.concatenate([padded[step:step + count_frames, row_tap:row_tap + heigh...  7.93 us
    ppermute x1, waiting for transfers between devices, from_behind(): return lax.ppermute(block, axis, route)  7.05 us
  transfers between devices with their start and end apart: 3, of which 1 were waited for; matrix products, arithmetic and copies ran while one was open for 5% of the time, Pallas kernels for 0%

profile of v3, /device:TPU:1, one launch (start us, length us, event | category | flops | bytes accessed | tf_op | source)
XLA Modules:
  0.0 137.9 jit_solution(14801753570461925942)
XLA Ops:
  0.7 4.1 %collective-permute-start = (bf16[2,64,32,128]{3,2,1,0:T(8,128)(2,1)}, bf16[2,64,32,128]{3,2,1,0:T(8,128)(2,1)S(1)}, u32[]{:S(2)}, u32[]{:S(2)}) collective-permute-start(bf16[2,64,32,128]{3,2,1,0:T(8,128)(2,1)} %param.4), channel_id=1, source_target_pairs={{0,8},{8,16},{16,24},{24,32},{32,40},{40,48},{48,56},{56,64},{64,7... | collective-permute-start | bytes 3145736 | tf_op jit(solution)/shard_map/ppermute | solution.py:14
  4.8 15.0 %all_gather.6 = bf16[3,3,3,128,128]{3,4,2,1,0:T(8,128)(2,1)S(1)} all-gather(bf16[3,3,3,128,16]{3,4,2,1,0:T(8,128)(2,1)} %param.5), channel_id=1, replica_groups=mesh['tm'=32,'fsdp'=8] {'fsdp'}, dimensions={4}, use_global_device_ids=true | all-gather | bytes 995328 | tf_op jit(solution)/shard_map/all_gather | solution.py:171
  19.8 7.0 %collective-permute-done = bf16[2,64,32,128]{3,2,1,0:T(8,128)(2,1)S(1)} collective-permute-done((bf16[2,64,32,128]{3,2,1,0:T(8,128)(2,1)}, bf16[2,64,32,128]{3,2,1,0:T(8,128)(2,1)S(1)}, u32[]{:S(2)}, u32[]{:S(2)}) %collective-permute-start) | collective-permute-done | bytes 1048608 | tf_op jit(solution)/shard_map/ppermute | solution.py:14
  27.0 0.1 constant_dynamic-update-slice_fusion
  27.1 0.9 fusion.17
  28.0 3.4 %collective-permute-start.2 = (bf16[4,64,1,128]{3,2,1,0:T(2,128)(2,1)}, bf16[4,64,1,128]{3,2,1,0:T(2,128)(2,1)S(1)}, u32[]{:S(2)}, u32[]{:S(2)}) collective-permute-start(bf16[4,64,1,128]{3,2,1,0:T(2,128)(2,1)} %get-tuple-element.30), channel_id=1, source_target_pairs={{1,0},{2,1},{3,2},{4,3},{5,4},{6,5},{7,6},{9,8},{10,9},{11,10},{12... | collective-permute-start | bytes 196616 | tf_op jit(solution)/shard_map/ppermute | solution.py:27
  31.5 3.1 %collective-permute-start.1 = (bf16[4,64,1,128]{3,2,1,0:T(2,128)(2,1)}, bf16[4,64,1,128]{3,2,1,0:T(2,128)(2,1)S(1)}, u32[]{:S(2)}, u32[]{:S(2)}) collective-permute-start(bf16[4,64,1,128]{3,2,1,0:T(2,128)(2,1)} %get-tuple-element.29), channel_id=1, source_target_pairs={{0,1},{1,2},{2,3},{3,4},{4,5},{5,6},{6,7},{8,9},{9,10},{10,11},{11... | collective-permute-start | bytes 196616 | tf_op jit(solution)/shard_map/ppermute | solution.py:25
  34.6 0.7 fusion.18
  35.3 1.6 %copy.21 = bf16[3,1,1,128,128]{4,3,0,2,1:T(8,128)(2,1)} copy(bf16[3,1,1,128,128]{3,4,2,1,0:T(8,128)(2,1)} %get-tuple-element.39) | data formatting | bytes 196608
  37.0 0.7 copy.22
  38.4 1.0 copy.28
  39.4 1.6 %copy.29 = bf16[3,1,1,128,128]{4,3,0,2,1:T(8,128)(2,1)} copy(bf16[3,1,1,128,128]{3,4,2,1,0:T(8,128)(2,1)} %get-tuple-element.31) | data formatting | bytes 196608
  41.0 13.6 %all_gather.7 = bf16[3,128,128]{1,2,0:T(8,128)(2,1)} all-gather(bf16[3,128,16]{1,2,0:T(8,128)(2,1)S(1)} %copy-done.14), channel_id=1, replica_groups=mesh['tm'=32,'fsdp'=8] {'fsdp'}, dimensions={2}, use_global_device_ids=true | all-gather | bytes 110592 | tf_op jit(solution)/shard_map/all_gather | solution.py:172
  54.6 1.6 %fusion.7 = bf16[4,66,34,128]{3,2,1,0:T(8,128)(2,1)S(1)} fusion(bf16[4,64,1,128]{3,2,1,0:T(2,128)(2,1)S(1)} %collective-permute-done.2, bf16[4,64,32,128]{3,2,1,0:T(8,128)(2,1)S(1)} %constant_dynamic-update-slice_fusion, bf16[4,64,1,128]{3,2,1,0:T(2,128)(2,1)S(1)} %collective-permute-done.1), kind=kLoop, calls=%fused_computation.30 | loop fusion | flops 13787136 | bytes 4526080 | tf_op jit(solution)/shard_map/concatenate | solution.py:23
  56.2 6.9 %fusion.16 = (bf16[2,64,32,128]{3,2,1,0:T(8,128)(2,1)S(1)}, bf16[2,64,32,128]{3,2,1,0:T(8,128)(2,1)S(1)}, bf16[2,64,32,128]{3,2,1,0:T(8,128)(2,1)S(1)}, bf16[2,6...) fusion(bf16[4,66,34,128]{3,2,1,0:T(8,128)(2,1)S(1)} %fusion.7), kind=kLoop, calls=%fused_computation.60 | loop fusion | bytes 37748736 | tf_op jit(solution)/shard_map/slice | solution.py:184
  63.1 3.3 %pad_maximum_fusion.2 = (bf16[2,64,32,384]{3,2,1,0:T(8,128)(2,1)S(1)}, bf16[2,64,32,384]{3,2,1,0:T(8,128)(2,1)S(1)}) fusion(bf16[2,64,32,128]{3,2,1,0:T(8,128)(2,1)} %get-tuple-element.16, bf16[2,64,32,128]{3,2,1,0:T(8,128)(2,1)} %get-tuple-element.17, bf16[2,64,32,128]{3,2,1,0:T(8,128)(2,1)} %get-tuple-element.18, ...), kind=kLoop, calls=%fused_computation.19 | loop fusion | flops 18874368 | bytes 12582912 | tf_op jit(solution)/shard_map/concatenate | solution.py:182
  66.4 1.0 fusion.19
  67.4 1.0 convolution_add_fusion.7
  68.6 0.3 copy-done.3
  68.9 0.3 copy-done.4
  69.2 0.3 copy-done.5
  69.5 0.9 pad_maximum_fusion.4
  70.4 1.0 convolution_add_fusion.6
  71.5 2.1 %fusion.10 = (bf16[2,64,32,128]{3,2,1,0:T(8,128)(2,1)S(1)}, bf16[2,64,32,128]{3,2,1,0:T(8,128)(2,1)S(1)}, bf16[2,64,32,128]{3,2,1,0:T(8,128)(2,1)S(1)}, bf16[2,6...) fusion(bf16[4,64,32,128]{3,2,1,0:T(8,128)(2,1)S(1)} %constant_dynamic-update-slice_fusion, ...), kind=kLoop, calls=%fused_computation.44 | loop fusion | flops 8388608 | bytes 8650752 | tf_op jit(solution)/shard_map/concatenate | solution.py:23
  73.6 2.5 %fusion.1 = (bf16[2,64,32,384]{3,2,1,0:T(8,128)(2,1)S(1)}, bf16[2,64,32,384]{3,2,1,0:T(8,128)(2,1)S(1)}) fusion(bf16[4,64,1,128]{3,2,1,0:T(2,128)(2,1)S(1)} %collective-permute-done.2, bf16[4,64,32,128]{3,2,1,0:T(8,128)(2,1)S(1)} %constant_dynamic-update-slice_fusion, bf16[2,64,32,128]{3,2,1,0:T(8,128)(2,1)S(1)} %get-tuple-element.21, ...), kind=kLoop, calls=%fused_computation.16 | loop fusion | flops 25165824 | bytes 12713984 | tf_op jit(solution)/shard_map/concatenate | solution.py:182
  76.1 1.0 convolution_add_fusion.5
  77.1 0.2 copy-done.7
  77.3 0.3 copy-done.9
  77.7 0.4 pad_maximum_fusion.5
  78.1 1.0 convolution_add_fusion.4
  79.1 1.0 convolution_add_fusion.3
  80.1 1.0 convolution_add_fusion.2
  81.1 0.9 pad_maximum_fusion.7
  82.0 1.0 convolution_add_fusion.1
  83.1 1.1 multiply_convert_fusion
  84.2 0.3 convert.2
  84.5 1.0 fusion.15.x_ref
  85.5 27.0 %shard_map.59 = bf16[32,2,32,128]{3,2,1,0:T(8,128)(2,1)} custom-call(bf16[1,64,32,128]{3,2,1,0:T(8,128)(2,1)} %fusion.15.x_ref), custom_call_target="tpu_custom_call" | custom-call | tf_op jit(solution)/shard_map/pallas_call | solution.py:77
  112.6 1.3 pad_slice_fusion.8
  113.9 1.4 convolution_bitcast_fusion
  115.3 0.3 convolution_bitcast_fusion.1
  115.6 0.3 convolution_bitcast_fusion.2
  116.1 1.0 copy.31
  117.1 18.5 %shard_map.60 = f32[1,192]{1,0:T(1,128)} custom-call(f32[8,32,1,192]{3,2,1,0:T(1,128)} %bitcast.97), custom_call_target="tpu_custom_call" | custom-call | tf_op jit(solution)/shard_map/pallas_call | solution.py:148
  135.6 0.3 convolution_add_fusion.10
  135.9 0.3 convolution_add_fusion.9
  136.2 1.1 fusion.8
  137.3 0.6 copy.34
  (37 shorter events, 1.0 us)
Async XLA Ops:
  0.6 113.3 %copy-start = (bf16[32,2,32,128]{3,2,1,0:T(8,128)(2,1)S(1)}, bf16[32,2,32,128]{3,2,1,0:T(8,128)(2,1)}, u32[]{:S(2)}) copy-start(bf16[32,2,32,128]{3,2,1,0:T(8,128)(2,1)} %param.7) | copy-start | bytes 1572868
  0.6 26.3 %copy-start.6 = (bf16[2,64,32,128]{3,2,1,0:T(8,128)(2,1)S(1)}, bf16[2,64,32,128]{3,2,1,0:T(8,128)(2,1)}, u32[]{:S(2)}) copy-start(bf16[2,64,32,128]{3,2,1,0:T(8,128)(2,1)} %param.4) | copy-start | bytes 3145732
  0.7 26.2 %collective-permute-start = (bf16[2,64,32,128]{3,2,1,0:T(8,128)(2,1)}, bf16[2,64,32,128]{3,2,1,0:T(8,128)(2,1)S(1)}, u32[]{:S(2)}, u32[]{:S(2)}) collective-permute-start(bf16[2,64,32,128]{3,2,1,0:T(8,128)(2,1)} %param.4), channel_id=1, source_target_pairs={{0,8},{8,16},{16,24},{24,32},{32,40},{40,48},{48,56},{56,64},{64,7... | collective-permute-start | bytes 3145736 | tf_op jit(solution)/shard_map/ppermute | solution.py:14
  26.9 8.5 %copy-start.8 = (bf16[2,64,32,128]{3,2,1,0:T(8,128)(2,1)}, bf16[2,64,32,128]{3,2,1,0:T(8,128)(2,1)S(1)}, u32[]{:S(2)}) copy-start(bf16[2,64,32,128]{3,2,1,0:T(8,128)(2,1)S(1)} %collective-permute-done) | copy-start | bytes 3145732
  27.0 14.1 %copy-start.14 = (bf16[3,128,16]{1,2,0:T(8,128)(2,1)S(1)}, bf16[3,128,16]{1,2,0:T(8,128)(2,1)}, u32[]{:S(2)}) copy-start(bf16[3,128,16]{1,2,0:T(8,128)(2,1)} %param.6) | copy-start | bytes 36868
  28.0 26.6 %collective-permute-start.2 = (bf16[4,64,1,128]{3,2,1,0:T(2,128)(2,1)}, bf16[4,64,1,128]{3,2,1,0:T(2,128)(2,1)S(1)}, u32[]{:S(2)}, u32[]{:S(2)}) collective-permute-start(bf16[4,64,1,128]{3,2,1,0:T(2,128)(2,1)} %get-tuple-element.30), channel_id=1, source_target_pairs={{1,0},{2,1},{3,2},{4,3},{5,4},{6,5},{7,6},{9,8},{10,9},{11,10},{12... | collective-permute-start | bytes 196616 | tf_op jit(solution)/shard_map/ppermute | solution.py:27
  31.5 23.1 %collective-permute-start.1 = (bf16[4,64,1,128]{3,2,1,0:T(2,128)(2,1)}, bf16[4,64,1,128]{3,2,1,0:T(2,128)(2,1)S(1)}, u32[]{:S(2)}, u32[]{:S(2)}) collective-permute-start(bf16[4,64,1,128]{3,2,1,0:T(2,128)(2,1)} %get-tuple-element.29), channel_id=1, source_target_pairs={{0,1},{1,2},{2,3},{3,4},{4,5},{5,6},{6,7},{8,9},{9,10},{10,11},{11... | collective-permute-start | bytes 196616 | tf_op jit(solution)/shard_map/ppermute | solution.py:25
  63.1 3.3 %copy-start.12 = (bf16[3,1,1,128,128]{4,3,0,2,1:T(8,128)(2,1)S(1)}, bf16[3,1,1,128,128]{4,3,0,2,1:T(8,128)(2,1)}, u32[]{:S(2)}) copy-start(bf16[3,1,1,128,128]{4,3,0,2,1:T(8,128)(2,1)} %copy.21) | copy-start | bytes 294916
  66.4 1.0 copy-start.10
  67.4 1.2 copy-start.2
  67.4 1.5 %copy-start.3 = (bf16[2,64,32,128]{3,2,1,0:T(8,128)(2,1)S(1)}, bf16[2,64,32,128]{3,2,1,0:T(8,128)(2,1)}, u32[]{:S(2)}) copy-start(bf16[2,64,32,128]{3,2,1,0:T(8,128)(2,1)} %get-tuple-element.10) | copy-start | bytes 3145732
  67.4 1.8 %copy-start.4 = (bf16[2,64,32,128]{3,2,1,0:T(8,128)(2,1)S(1)}, bf16[2,64,32,128]{3,2,1,0:T(8,128)(2,1)}, u32[]{:S(2)}) copy-start(bf16[2,64,32,128]{3,2,1,0:T(8,128)(2,1)} %get-tuple-element.11) | copy-start | bytes 3145732
  67.4 2.1 %copy-start.5 = (bf16[2,64,32,128]{3,2,1,0:T(8,128)(2,1)S(1)}, bf16[2,64,32,128]{3,2,1,0:T(8,128)(2,1)}, u32[]{:S(2)}) copy-start(bf16[2,64,32,128]{3,2,1,0:T(8,128)(2,1)} %get-tuple-element.12) | copy-start | bytes 3145732
  76.1 1.2 copy-start.7
  76.1 1.5 %copy-start.9 = (bf16[2,64,32,128]{3,2,1,0:T(8,128)(2,1)S(1)}, bf16[2,64,32,128]{3,2,1,0:T(8,128)(2,1)}, u32[]{:S(2)}) copy-start(bf16[2,64,32,128]{3,2,1,0:T(8,128)(2,1)} %copy-done.8) | copy-start | bytes 3145732
  82.0 1.0 copy-start.13
  112.6 2.7 %copy-start.1 = (bf16[32,2,32,128]{3,2,1,0:T(8,128)(2,1)S(1)}, bf16[32,2,32,128]{3,2,1,0:T(8,128)(2,1)}, u32[]{:S(2)}) copy-start(bf16[32,2,32,128]{3,2,1,0:T(8,128)(2,1)} %shard_map.59) | copy-start | bytes 1572868
  115.3 20.3 %copy-start.11 = (bf16[3,128,128]{1,2,0:T(8,128)(2,1)S(1)}, bf16[3,128,128]{1,2,0:T(8,128)(2,1)}, u32[]{:S(2)}) copy-start(bf16[3,128,128]{1,2,0:T(8,128)(2,1)} %all_gather.7) | copy-start | bytes 294916
  135.6 1.7 %copy-start.15 = (f32[1,192]{1,0:T(1,128)S(1)}, f32[1,192]{1,0:T(1,128)}, u32[]{:S(2)}) copy-start(f32[1,192]{1,0:T(1,128)} %shard_map.60) | copy-start | bytes 2308

commit v4 on v3

--- a/solution.py
+++ b/solution.py
@@ -166,15 +166,97 @@
     return out.reshape(piece)
 
 
+def prologue_kernel(x_ref, lcol_ref, rcol_ref, w_ref, halo_ref, left_ref, right_ref, wall_ref, sends, recvs, wsends, wrecvs, local_sem):
+    count, groups = lax.axis_size("tm"), lax.axis_size("fsdp")
+    t, f = lax.axis_index("tm"), lax.axis_index("fsdp")
+    t_next, t_prev = lax.rem(t + 1, count), lax.rem(t + count - 1, count)
+    f_next, f_prev = lax.rem(f + 1, groups), lax.rem(f + groups - 1, groups)
+    peers = [(t_next, f), (t_prev, f)]
+    peers += [(t, lax.rem(f + k, groups)) for k in range(1, groups)]
+    peers += [(a, b) for a in (t_next, t_prev) for b in (f_next, f_prev)]
+    barrier = pltpu.get_barrier_semaphore()
+    for a, b in peers:
+        pl.semaphore_signal(barrier, inc=1, device_id=(a, b), device_id_type=MESH)
+    pl.semaphore_wait(barrier, len(peers))
+    depth = x_ref.shape[0]
+    plan = [
+        (x_ref, halo_ref, (t_next, f)),
+        (rcol_ref, left_ref.at[pl.ds(depth, depth)], (t, f_next)),
+        (rcol_ref, left_ref.at[pl.ds(0, depth)], (t_next, f_next)),
+        (lcol_ref, right_ref.at[pl.ds(depth, depth)], (t, f_prev)),
+        (lcol_ref, right_ref.at[pl.ds(0, depth)], (t_next, f_prev)),
+    ]
+    copies = []
+    for i, (src, dst, dev) in enumerate(plan):
+        copy = pltpu.make_async_remote_copy(
+            src_ref=src, dst_ref=dst, send_sem=sends.at[i], recv_sem=recvs.at[i],
+            device_id=dev, device_id_type=MESH,
+        )
+        copy.start()
+        copies.append(copy)
+    local = pltpu.make_async_copy(w_ref, wall_ref.at[f], local_sem)
+    local.start()
+    for k in range(1, groups):
+        copy = pltpu.make_async_remote_copy(
+            src_ref=w_ref, dst_ref=wall_ref.at[f], send_sem=wsends.at[k], recv_sem=wrecvs.at[k],
+            device_id=(t, lax.rem(f + k, groups)), device_id_type=MESH,
+        )
+        copy.start()
+        copies.append(copy)
+    local.wait()
+    for copy in copies:
+        copy.wait()
+
+
+def prologue(frames, shard):
+    groups = lax.axis_size("fsdp")
+    depth, height, width, channels = frames.shape
+    lcol = frames[:, :, 0, :]
+    rcol = frames[:, :, width - 1, :]
+    edge = jax.ShapeDtypeStruct((2 * depth, height, channels), frames.dtype)
+    vmem = pl.BlockSpec(memory_space=pltpu.VMEM)
+    return pl.pallas_call(
+        prologue_kernel,
+        out_shape=(
+            jax.ShapeDtypeStruct(frames.shape, frames.dtype),
+            edge,
+            edge,
+            jax.ShapeDtypeStruct((groups,) + shard.shape, shard.dtype),
+        ),
+        in_specs=[vmem] * 4,
+        out_specs=(vmem,) * 4,
+        scratch_shapes=[
+            pltpu.SemaphoreType.DMA((5,)),
+            pltpu.SemaphoreType.DMA((5,)),
+            pltpu.SemaphoreType.DMA((groups,)),
+            pltpu.SemaphoreType.DMA((groups,)),
+            pltpu.SemaphoreType.DMA,
+        ],
+        compiler_params=pltpu.CompilerParams(collective_id=2, has_side_effects=True),
+    )(frames, lcol, rcol, shard)
+
+
 def local(frames, conv_weight, mix_weight, cotangent):
-    full_conv, full_mix = (
-        lax.all_gather(conv_weight, "fsdp", axis=4, tiled=True),
-        lax.all_gather(mix_weight, "fsdp", axis=2, tiled=True),
-    )
+    groups = lax.axis_size("fsdp")
+    t, f = lax.axis_index("tm"), lax.axis_index("fsdp")
+    part = conv_weight.shape[-1]
+    shard = jnp.concatenate(
+        [conv_weight.reshape(-1, part), mix_weight.reshape(-1, part)], axis=0
+    ).reshape(-1, 128)
+    halo, left, right, wall = prologue(frames, shard)
+    wall = wall.reshape(groups, -1, part)
+    wall = jnp.transpose(wall, (1, 0, 2)).reshape(wall.shape[1], groups * part)
+    split = conv_weight.size // part
+    full_conv = wall[:split].reshape(conv_weight.shape[:-1] + (-1,))
+    full_mix = wall[split:].reshape(mix_weight.shape[:-1] + (-1,))
     count_frames, height, width, channels = frames.shape
-    previous = from_behind(frames, "tm", 1)
-    timed = jnp.concatenate([previous, frames], axis=0)
-    padded = with_halo(timed, (("fsdp", 2),), 1)
+    zero = jnp.zeros((), frames.dtype)
+    halo = jnp.where(t > 0, halo, zero)
+    timed = jnp.concatenate([halo, frames], axis=0)
+    first = jnp.arange(2 * count_frames)[:, None, None] >= count_frames
+    left = jnp.where((f > 0) & ((t > 0) | first), left, zero)
+    right = jnp.where((f < groups - 1) & ((t > 0) | first), right, zero)
+    padded = jnp.concatenate([left[:, :, None], timed, right[:, :, None]], axis=2)
     padded = jnp.pad(padded, ((0, 0), (1, 1), (0, 0), (0, 0)))
     accum = jnp.zeros((count_frames * height * width, channels), jnp.float32)
     for row_tap in range(3):

time: 138 us -> 184 us (1.33)
  local copies, waits for them, and re-layouts: 19.1 us -> 68.8 us
  Pallas kernels: 45.5 us -> 80.2 us
  blocking collectives: 28.6 us -> 0 us
  starting transfers between devices: 10.7 us -> 0 us
  waiting for transfers between devices: 7.05 us -> 0 us
  other arithmetic: 12.9 us -> 18.7 us
    pallas_call x0 -> x1, Pallas kernels: none -> 40 us  [prologue(): pl.pallas_call(prologue_kernel, out_shape=(jax.ShapeDtypeStruct(frames.sh...]
    all_gather x2 -> x0, blocking collectives: 28.6 us -> none  [the longest x1 15 us: local(): lax.all_gather(conv_weight, 'fsdp', axis=4, tiled=True)]
    slice x1 -> x7, local copies, waits for them, and re-layouts: 0.91 us -> 19.5 us  [the longest x2 12.9 us: local(): full_conv = wall[:split].reshape(conv_weight.shape[:-1] + (-1,))]
    slice x1 -> x10, local copies, waits for them, and re-layouts: 0.74 us -> 18.4 us  [local(): kernel = full_conv[:, row_tap, col_tap].reshape(3 * channels, channels)]
    reshape x0 -> x5, local copies, waits for them, and re-layouts: none -> 14.4 us  [the longest x1 8.86 us: local(): wall = wall.reshape(groups, -1, part)]
    ppermute x3 -> x0, starting transfers between devices: 10.7 us -> none  [the longest x1 4.14 us: from_behind(): return lax.ppermute(block, axis, route)]
    pallas_call x1, Pallas kernels: 27 us -> 19.4 us  [exchange_rows(): pl.pallas_call(exchange_kernel, out_shape=jax.ShapeDtypeStruct((count, he...]
    ppermute x3 -> x0, waiting for transfers between devices: 7.05 us -> none  [the longest x1 7.05 us: from_behind(): return lax.ppermute(block, axis, route)]
  transfers between devices with their start and end apart: 3 -> 0, of which waited for: 1 -> 0; matrix products, arithmetic and copies ran while one was open for 5% -> 0% of each run, Pallas kernels for 0% -> 0%
where the time goes in v4:
time: 184 us; the launch traced here: 183 us
  Pallas kernels  80.2 us (44%)
  local copies, waits for them, and re-layouts  68.8 us (37%)
  other arithmetic  18.7 us (10%)
  matrix products  14 us (8%)
    pallas_call x1, Pallas kernels, prologue(): pl.pallas_call(prologue_kernel, out_shape=(jax.ShapeDtypeStruct(frames.sh...  40 us
    pallas_call x1, Pallas kernels, scatter_sum(): pl.pallas_call(scatter_kernel, out_shape=jax.ShapeDtypeStruct((1, piece),...  20.7 us
    pallas_call x1, Pallas kernels, exchange_rows(): pl.pallas_call(exchange_kernel, out_shape=jax.ShapeDtypeStruct((count, he...  19.4 us
    slice x10, local copies, waits for them, and re-layouts, local(): kernel = full_conv[:, row_tap, col_tap].reshape(3 * channels, channels)  18.4 us
    slice x2, local copies, waits for them, and re-layouts, local(): full_conv = wall[:split].reshape(conv_weight.shape[:-1] + (-1,))  12.9 us
    concatenate x9, other arithmetic, local(): jnp.concatenate([padded[step:step + count_frames, row_tap:row_tap + heigh...  10.5 us
    dot_general x9, matrix products, local(): accum = accum + jnp.dot(stacked, kernel, preferred_element_type=jnp.float32)  9.15 us
    reshape x1, local copies, waits for them, and re-layouts, local(): wall = wall.reshape(groups, -1, part)  8.86 us

profile of v4, /device:TPU:1, one launch (start us, length us, event | category | flops | bytes accessed | tf_op | source)
XLA Modules:
  0.0 182.8 jit_solution(1028498434636605682)
XLA Ops:
  1.4 1.1 fusion.15
  3.2 1.0 copy.28
  4.8 1.3 reshape.138.w_ref
  6.1 40.0 %shard_map.59 = (bf16[2,64,32,128]{3,2,1,0:T(8,128)(2,1)}, bf16[4,64,128]{2,1,0:T(8,128)(2,1)}, bf16[4,64,128]{2,1,0:T(8,128)(2,1)}, bf16[8,480,128]{2,1,0:T(8,128)(2,1)}) custom-call(bf16[2,64,32,128]{3,2,1,0:T(8,128)(2,1)} %x_ref.1, bf16[2,64,128]{2,1,0:T(8,128)(2,1)} %get-tuple-element.53.lcol_ref, bf16[2,64,128]{2,1,0:T(8,128)(2,1)} %get-tuple-element.52.rcol_ref, ...), custom_call_target="tpu_custom_call" | custom-call | tf_op jit(solution)/shard_map/pallas_call | solution.py:218
  46.1 0.9 select_bitcast_fusion.1
  47.0 0.9 select_bitcast_fusion
  48.2 3.5 %select_maximum_fusion = bf16[4,66,34,128]{3,2,1,0:T(8,128)(2,1)S(1)} fusion(bf16[4,64,1,128]{3,2,1,0:T(2,128)(2,1)S(1)} %copy.32, bf16[4,64,1,128]{3,2,1,0:T(2,128)(2,1)S(1)} %copy.31, bf16[2,64,32,128]{3,2,1,0:T(8,128)(2,1)} %x_ref.1, bf16[2,64,32,128]{3,2,1,0:T(8,128)(2,1)S(1)} %broadcast_select_fusion), kind=kLoop, calls=%fused_computation.22 | loop fusion | flops 17233920 | bytes 4526080 | tf_op jit(solution)/shard_map/concatenate | solution.py:259
  51.7 1.9 %fusion.2 = bf16[2,64,32,384]{3,2,1,0:T(8,128)(2,1)} fusion(bf16[2,64,32,128]{3,2,1,0:T(8,128)(2,1)S(1)} %copy-done.4, bf16[2,64,32,128]{3,2,1,0:T(8,128)(2,1)S(1)} %broadcast_select_fusion), kind=kLoop, calls=%fused_computation.13 | loop fusion | flops 12582912 | bytes 5242880 | tf_op jit(solution)/shard_map/concatenate | solution.py:264
  53.6 1.5 pad_maximum_fusion.9
  55.1 1.2 fusion.12
  56.3 2.1 %pad_maximum_fusion.5 = bf16[2,64,32,384]{3,2,1,0:T(8,128)(2,1)} fusion(bf16[2,64,32,128]{3,2,1,0:T(8,128)(2,1)S(1)} %get-tuple-element.32, bf16[2,64,32,128]{3,2,1,0:T(8,128)(2,1)S(1)} %get-tuple-element.33, bf16[2,64,32,128]{3,2,1,0:T(8,128)(2,1)S(1)} %get-tuple-element.31), kind=kLoop, calls=%fused_computation.18 | loop fusion | flops 9437184 | bytes 6291456 | tf_op jit(solution)/shard_map/concatenate | solution.py:264
  58.9 2.0 %pad_maximum_fusion.4 = bf16[2,64,32,384]{3,2,1,0:T(8,128)(2,1)} fusion(bf16[2,64,32,128]{3,2,1,0:T(8,128)(2,1)S(1)} %get-tuple-element.35, bf16[2,64,32,128]{3,2,1,0:T(8,128)(2,1)S(1)} %get-tuple-element.36, bf16[2,64,32,128]{3,2,1,0:T(8,128)(2,1)S(1)} %get-tuple-element.34), kind=kLoop, calls=%fused_computation.17 | loop fusion | flops 9437184 | bytes 6291456 | tf_op jit(solution)/shard_map/concatenate | solution.py:264
  61.0 8.9 %reshape.140 = bf16[8,3840,16]{2,1,0:T(8,128)(2,1)} reshape(bf16[8,480,128]{2,1,0:T(8,128)(2,1)} %get-tuple-element.9) | data formatting | bytes 1966080 | tf_op jit(solution)/shard_map/reshape | solution.py:247
  69.8 2.0 %fusion.10 = (bf16[128,8,16]{2,0,1:T(8,128)(2,1)}, bf16[128,8,16]{2,0,1:T(8,128)(2,1)}, bf16[128,8,16]{2,0,1:T(8,128)(2,1)S(1)}) fusion(bf16[3840,8,16]{2,0,1:T(8,128)(2,1)} %bitcast.99), kind=kLoop, calls=%fused_computation.55 | loop fusion | bytes 196608 | tf_op jit(solution)/shard_map/slice | solution.py:285
  71.8 6.5 %slice.208 = bf16[3456,8,16]{2,0,1:T(8,128)(2,1)} slice(bf16[3840,8,16]{2,0,1:T(8,128)(2,1)} %bitcast.100), slice={[0:3456], [0:8], [0:16]} | slice | bytes 1769472 | tf_op jit(solution)/shard_map/slice | solution.py:250
  78.3 6.4 %copy.33 = bf16[3456,8,16]{0,2,1:T(8,128)(2,1)} copy(bf16[3456,8,16]{2,0,1:T(8,128)(2,1)} %slice.208) | data formatting | bytes 1769472 | tf_op jit(solution)/shard_map/slice | solution.py:250
  84.7 1.1 copy.47
  85.8 1.7 copy.46
  88.2 3.3 %reshape.141 = bf16[3,3,3,128,128]{3,2,1,0,4:T(4,128)(2,1)} reshape(bf16[3456,8,16]{0,2,1:T(8,128)(2,1)} %copy.33) | data formatting | bytes 1769472 | tf_op jit(solution)/shard_map/reshape | solution.py:250
  91.5 4.8 %fusion.14 = (bf16[3,1,1,128,128]{3,2,1,0,4:T(2,128)(2,1)}, bf16[3,1,1,128,128]{3,2,1,0,4:T(2,128)(2,1)}, bf16[3,1,1,128,128]{3,2,1,0,4:T(2,128)(2,1)}, bf16[3,1...) fusion(bf16[3,3,3,128,128]{3,2,1,0,4:T(4,128)(2,1)} %reshape.141), kind=kLoop, calls=%fused_computation.59 | loop fusion | bytes 1769472 | tf_op jit(solution)/shard_map/slice | solution.py:276
  96.3 1.7 copy.44
  98.0 1.1 copy.43
  99.1 1.7 copy.42
  100.8 1.7 copy.41
  102.5 1.7 copy.39
  104.2 1.7 copy.38
  105.9 1.7 copy.36
  107.5 1.7 copy.35
  110.0 6.0 %fusion.11 = (bf16[2,64,32,128]{3,2,1,0:T(8,128)(2,1)}, bf16[2,64,32,128]{3,2,1,0:T(8,128)(2,1)}, bf16[2,64,32,128]{3,2,1,0:T(8,128)(2,1)}, bf16[2,64,32,128]{3,...) fusion(bf16[4,66,34,128]{3,2,1,0:T(8,128)(2,1)S(1)} %select_max, ...), kind=kLoop, calls=%fused_computation.56 | loop fusion | bytes 37748736 | tf_op jit(solution)/shard_map/slice | solution.py:266
  116.0 2.4 %pad_maximum_fusion.8 = bf16[2,64,32,384]{3,2,1,0:T(8,128)(2,1)S(1)} fusion(bf16[2,64,32,128]{3,2,1,0:T(8,128)(2,1)} %get-tuple-element.30, bf16[2,64,32,128]{3,2,1,0:T(8,128)(2,1)} %get-tuple-element.14, bf16[2,64,32,128]{3,2,1,0:T(8,128)(2,1)} %get-tuple-element.13), kind=kLoop, calls=%fused_computation.21 | loop fusion | flops 9437184 | bytes 6291456 | tf_op jit(solution)/shard_map/concatenate | solution.py:264
  122.5 1.0 fusion.16
  123.5 1.0 convolution_add_fusion.7
  124.6 1.0 convolution_add_fusion.6
  125.6 0.9 copy-done.3
  126.5 1.0 convolution_add_fusion.5
  127.5 0.9 copy-done.1
  128.3 1.0 convolution_add_fusion.4
  130.2 1.0 convolution_add_fusion.3
  131.2 1.0 convolution_add_fusion.2
  132.3 1.0 convolution_add_fusion.1
  133.3 1.1 multiply_convert_fusion
  134.7 1.0 fusion.9.x_ref
  135.7 19.4 %shard_map.60 = bf16[32,2,32,128]{3,2,1,0:T(8,128)(2,1)} custom-call(bf16[1,64,32,128]{3,2,1,0:T(8,128)(2,1)} %fusion.9.x_ref), custom_call_target="tpu_custom_call" | custom-call | tf_op jit(solution)/shard_map/pallas_call | solution.py:77
  155.2 1.4 convolution_bitcast_fusion.1
  156.6 1.4 convolution_bitcast_fusion.2
  158.5 1.0 copy.59
  159.5 20.7 %shard_map.61 = f32[1,192]{1,0:T(1,128)} custom-call(f32[8,32,1,192]{3,2,1,0:T(1,128)} %bitcast.114), custom_call_target="tpu_custom_call" | custom-call | tf_op jit(solution)/shard_map/pallas_call | solution.py:148
  181.1 1.1 fusion.6
  (67 shorter events, 11.4 us)
Async XLA Ops:
  0.6 154.5 %copy-start = (bf16[32,2,32,128]{3,2,1,0:T(8,128)(2,1)S(1)}, bf16[32,2,32,128]{3,2,1,0:T(8,128)(2,1)}, u32[]{:S(2)}) copy-start(bf16[32,2,32,128]{3,2,1,0:T(8,128)(2,1)} %param.7) | copy-start | bytes 1572868
  48.1 3.6 %copy-start.4 = (bf16[2,64,32,128]{3,2,1,0:T(8,128)(2,1)S(1)}, bf16[2,64,32,128]{3,2,1,0:T(8,128)(2,1)}, u32[]{:S(2)}) copy-start(bf16[2,64,32,128]{3,2,1,0:T(8,128)(2,1)} %x_ref.1) | copy-start | bytes 3145732
  116.0 2.4 %copy-start.8 = (bf16[2,64,32,128]{3,2,1,0:T(8,128)(2,1)S(1)}, bf16[2,64,32,128]{3,2,1,0:T(8,128)(2,1)}, u32[]{:S(2)}) copy-start(bf16[2,64,32,128]{3,2,1,0:T(8,128)(2,1)} %get-tuple-element.15) | copy-start | bytes 3145732
  116.0 2.5 %copy-start.9 = (bf16[2,64,32,128]{3,2,1,0:T(8,128)(2,1)S(1)}, bf16[2,64,32,128]{3,2,1,0:T(8,128)(2,1)}, u32[]{:S(2)}) copy-start(bf16[2,64,32,128]{3,2,1,0:T(8,128)(2,1)} %get-tuple-element.16) | copy-start | bytes 3145732
  116.0 2.8 %copy-start.10 = (bf16[2,64,32,128]{3,2,1,0:T(8,128)(2,1)S(1)}, bf16[2,64,32,128]{3,2,1,0:T(8,128)(2,1)}, u32[]{:S(2)}) copy-start(bf16[2,64,32,128]{3,2,1,0:T(8,128)(2,1)} %get-tuple-element.17) | copy-start | bytes 3145732
  118.8 1.2 copy-start.6
  118.8 1.5 copy-start.7
  121.6 0.9 copy-start.17
  122.5 1.0 copy-start.16
  123.5 1.0 copy-start.15
  124.6 1.9 %copy-start.3 = (bf16[2,64,32,384]{3,2,1,0:T(8,128)(2,1)S(1)}, bf16[2,64,32,384]{3,2,1,0:T(8,128)(2,1)}, u32[]{:S(2)}) copy-start(bf16[2,64,32,384]{3,2,1,0:T(8,128)(2,1)} %pad_maximum_fusion.4) | copy-start | bytes 9437188
  124.6 1.9 %copy-start.14 = (bf16[3,1,1,128,128]{4,3,0,2,1:T(8,128)(2,1)S(1)}, bf16[3,1,1,128,128]{4,3,0,2,1:T(8,128)(2,1)}, u32[]{:S(2)}) copy-start(bf16[3,1,1,128,128]{4,3,0,2,1:T(8,128)(2,1)} %copy.38) | copy-start | bytes 294916
  126.4 1.9 %copy-start.1 = (bf16[2,64,32,384]{3,2,1,0:T(8,128)(2,1)S(1)}, bf16[2,64,32,384]{3,2,1,0:T(8,128)(2,1)}, u32[]{:S(2)}) copy-start(bf16[2,64,32,384]{3,2,1,0:T(8,128)(2,1)} %fusion.2) | copy-start | bytes 9437188
  126.4 1.9 %copy-start.13 = (bf16[3,1,1,128,128]{4,3,0,2,1:T(8,128)(2,1)S(1)}, bf16[3,1,1,128,128]{4,3,0,2,1:T(8,128)(2,1)}, u32[]{:S(2)}) copy-start(bf16[3,1,1,128,128]{4,3,0,2,1:T(8,128)(2,1)} %copy.39) | copy-start | bytes 294916
  128.3 1.9 %copy-start.2 = (bf16[2,64,32,384]{3,2,1,0:T(8,128)(2,1)S(1)}, bf16[2,64,32,384]{3,2,1,0:T(8,128)(2,1)}, u32[]{:S(2)}) copy-start(bf16[2,64,32,384]{3,2,1,0:T(8,128)(2,1)} %pad_maximum_fusion.5) | copy-start | bytes 9437188
  128.3 1.9 %copy-start.12 = (bf16[3,1,1,128,128]{4,3,0,2,1:T(8,128)(2,1)S(1)}, bf16[3,1,1,128,128]{4,3,0,2,1:T(8,128)(2,1)}, u32[]{:S(2)}) copy-start(bf16[3,1,1,128,128]{4,3,0,2,1:T(8,128)(2,1)} %copy.41) | copy-start | bytes 294916
  130.2 1.0 copy-start.11
  132.2 1.0 copy-start.20
  155.1 2.9 %copy-start.5 = (bf16[32,2,32,128]{3,2,1,0:T(8,128)(2,1)S(1)}, bf16[32,2,32,128]{3,2,1,0:T(8,128)(2,1)}, u32[]{:S(2)}) copy-start(bf16[32,2,32,128]{3,2,1,0:T(8,128)(2,1)} %shard_map.60) | copy-start | bytes 1572868
  156.6 23.6 %copy-start.18 = (bf16[128,8,16]{0,2,1:T(8,128)(2,1)S(1)}, bf16[128,8,16]{0,2,1:T(8,128)(2,1)}, u32[]{:S(2)}) copy-start(bf16[128,8,16]{0,2,1:T(8,128)(2,1)} %copy.45) | copy-start | bytes 98308
  158.0 22.8 %copy-start.19 = (bf16[128,8,16]{0,2,1:T(8,128)(2,1)S(1)}, bf16[128,8,16]{0,2,1:T(8,128)(2,1)}, u32[]{:S(2)}) copy-start(bf16[128,8,16]{0,2,1:T(8,128)(2,1)} %copy.46) | copy-start | bytes 98308
  180.5 1.7 copy-start.21

commit v5 on v3

--- a/solution.py
+++ b/solution.py
@@ -38,54 +38,6 @@
 
 def delayed(block, offset):
     return jnp.pad(block, ((offset, 0), (0, 0), (0, 0), (0, 0)))[: block.shape[0]]
-
-
-def exchange_kernel(x_ref, o_ref, send_sem, recv_sem, local_sem):
-    count, rows = o_ref.shape[0], o_ref.shape[1]
-    me = lax.axis_index("tm")
-    barrier = pltpu.get_barrier_semaphore()
-    for k in range(1, count):
-        pl.semaphore_signal(
-            barrier, inc=1, device_id={"tm": lax.rem(me + k, count)}, device_id_type=MESH
-        )
-    pl.semaphore_wait(barrier, count - 1)
-    local = pltpu.make_async_copy(
-        x_ref.at[0, pl.ds(me * rows, rows)], o_ref.at[me], local_sem
-    )
-    local.start()
-    copies = []
-    for k in range(1, count):
-        peer = lax.rem(me + k, count)
-        copy = pltpu.make_async_remote_copy(
-            src_ref=x_ref.at[0, pl.ds(peer * rows, rows)],
-            dst_ref=o_ref.at[me],
-            send_sem=send_sem.at[k],
-            recv_sem=recv_sem.at[k],
-            device_id={"tm": peer},
-            device_id_type=MESH,
-        )
-        copy.start()
-        copies.append(copy)
-    local.wait()
-    for copy in copies:
-        copy.wait()
-
-
-def exchange_rows(block):
-    count = lax.axis_size("tm")
-    _, height, width, channels = block.shape
-    return pl.pallas_call(
-        exchange_kernel,
-        out_shape=jax.ShapeDtypeStruct((count, height // count, width, channels), block.dtype),
-        in_specs=[pl.BlockSpec(memory_space=pltpu.VMEM)],
-        out_specs=pl.BlockSpec(memory_space=pltpu.VMEM),
-        scratch_shapes=[
-            pltpu.SemaphoreType.DMA((count,)),
-            pltpu.SemaphoreType.DMA((count,)),
-            pltpu.SemaphoreType.DMA,
-        ],
-        compiler_params=pltpu.CompilerParams(collective_id=0, has_side_effects=True),
-    )(block)
 
 
 def scatter_kernel(p_ref, o_ref, first, second, summed, s1, r1, s2, r2, l1, l2):
@@ -194,7 +146,7 @@
             kernel = full_conv[:, row_tap, col_tap].reshape(3 * channels, channels)
             accum = accum + jnp.dot(stacked, kernel, preferred_element_type=jnp.float32)
     hidden = jax.nn.silu(accum).astype(jnp.bfloat16).reshape(count_frames, height, width, channels)
-    pooled = exchange_rows(pool_pairs(hidden))
+    pooled = lax.all_to_all(pool_pairs(hidden), "tm", split_axis=1, concat_axis=0, tiled=True)
     branch = pooled.astype(jnp.float32).reshape(-1, channels)
     flat_cot = cotangent.reshape(-1, channels)
     grad_terms = []

time: 138 us -> 126 us (0.913)
  Pallas kernels: 45.5 us -> 18.7 us
  starting transfers between devices: 10.7 us -> 23.4 us
  waiting for transfers between devices: 7.05 us -> 11.7 us
    pallas_call x1 -> x0, Pallas kernels: 27 us -> none  [exchange_rows(): pl.pallas_call(exchange_kernel, out_shape=jax.ShapeDtypeStruct((count, he...]
    all_to_all x0 -> x1, starting transfers between devices: none -> 12.7 us  [local(): lax.all_to_all(pool_pairs(hidden), 'tm', split_axis=1, concat_axis=0, til...]
    all_to_all x0 -> x1, waiting for transfers between devices: none -> 4.64 us  [local(): lax.all_to_all(pool_pairs(hidden), 'tm', split_axis=1, concat_axis=0, til...]
    unnamed x43 -> x39, local copies, waits for them, and re-layouts: 7.98 us -> 7.96 us
  transfers between devices with their start and end apart: 3 -> 4, of which waited for: 1 -> 2; matrix products, arithmetic and copies ran while one was open for 5% -> 5% of each run, Pallas kernels for 0% -> 0%
where the time goes in v5:
time: 126 us; the launch traced here: 125 us
  blocking collectives  27.7 us (22%)
  starting transfers between devices  23.4 us (19%)
  Pallas kernels  18.7 us (15%)
  local copies, waits for them, and re-layouts  18 us (14%)
  other arithmetic  12.9 us (10%)
  matrix products  11.9 us (9%)
  waiting for transfers between devices  11.7 us (9%)
    pallas_call x1, Pallas kernels, scatter_sum(): pl.pallas_call(scatter_kernel, out_shape=jax.ShapeDtypeStruct((1, piece),...  18.7 us
    all_gather x1, blocking collectives, local(): lax.all_gather(conv_weight, 'fsdp', axis=4, tiled=True)  15 us
    all_to_all x1, starting transfers between devices, local(): lax.all_to_all(pool_pairs(hidden), 'tm', split_axis=1, concat_axis=0, til...  12.7 us
    all_gather x1, blocking collectives, local(): lax.all_gather(mix_weight, 'fsdp', axis=2, tiled=True)  12.7 us
    dot_general x9, matrix products, local(): accum = accum + jnp.dot(stacked, kernel, preferred_element_type=jnp.float32)  9.2 us
    unnamed x39, local copies, waits for them, and re-layouts  7.96 us
    concatenate x5, other arithmetic, local(): jnp.concatenate([padded[step:step + count_frames, row_tap:row_tap + heigh...  7.93 us
    ppermute x1, waiting for transfers between devices, from_behind(): return lax.ppermute(block, axis, route)  7.05 us
  transfers between devices with their start and end apart: 4, of which 2 were waited for; matrix products, arithmetic and copies ran while one was open for 5% of the time, Pallas kernels for 0%

profile of v5, /device:TPU:1, one launch (start us, length us, event | category | flops | bytes accessed | tf_op | source)
XLA Modules:
  0.0 125.4 jit_solution(14433612952853049122)
XLA Ops:
  0.7 4.1 %collective-permute-start = (bf16[2,64,32,128]{3,2,1,0:T(8,128)(2,1)}, bf16[2,64,32,128]{3,2,1,0:T(8,128)(2,1)S(1)}, u32[]{:S(2)}, u32[]{:S(2)}) collective-permute-start(bf16[2,64,32,128]{3,2,1,0:T(8,128)(2,1)} %param.4), channel_id=1, source_target_pairs={{0,8},{8,16},{16,24},{24,32},{32,40},{40,48},{48,56},{56,64},{64,7... | collective-permute-start | bytes 3145736 | tf_op jit(solution)/shard_map/ppermute | solution.py:14
  4.8 15.0 %all_gather.6 = bf16[3,3,3,128,128]{3,4,2,1,0:T(8,128)(2,1)S(1)} all-gather(bf16[3,3,3,128,16]{3,4,2,1,0:T(8,128)(2,1)} %param.5), channel_id=1, replica_groups=mesh['tm'=32,'fsdp'=8] {'fsdp'}, dimensions={4}, use_global_device_ids=true | all-gather | bytes 995328 | tf_op jit(solution)/shard_map/all_gather | solution.py:123
  19.8 7.0 %collective-permute-done = bf16[2,64,32,128]{3,2,1,0:T(8,128)(2,1)S(1)} collective-permute-done((bf16[2,64,32,128]{3,2,1,0:T(8,128)(2,1)}, bf16[2,64,32,128]{3,2,1,0:T(8,128)(2,1)S(1)}, u32[]{:S(2)}, u32[]{:S(2)}) %collective-permute-start) | collective-permute-done | bytes 1048608 | tf_op jit(solution)/shard_map/ppermute | solution.py:14
  27.1 0.9 fusion.17
  28.0 3.4 %collective-permute-start.2 = (bf16[4,64,1,128]{3,2,1,0:T(2,128)(2,1)}, bf16[4,64,1,128]{3,2,1,0:T(2,128)(2,1)S(1)}, u32[]{:S(2)}, u32[]{:S(2)}) collective-permute-start(bf16[4,64,1,128]{3,2,1,0:T(2,128)(2,1)} %get-tuple-element.30), channel_id=1, source_target_pairs={{1,0},{2,1},{3,2},{4,3},{5,4},{6,5},{7,6},{9,8},{10,9},{11,10},{12... | collective-permute-start | bytes 196616 | tf_op jit(solution)/shard_map/ppermute | solution.py:27
  31.5 3.1 %collective-permute-start.1 = (bf16[4,64,1,128]{3,2,1,0:T(2,128)(2,1)}, bf16[4,64,1,128]{3,2,1,0:T(2,128)(2,1)S(1)}, u32[]{:S(2)}, u32[]{:S(2)}) collective-permute-start(bf16[4,64,1,128]{3,2,1,0:T(2,128)(2,1)} %get-tuple-element.29), channel_id=1, source_target_pairs={{0,1},{1,2},{2,3},{3,4},{4,5},{5,6},{6,7},{8,9},{9,10},{10,11},{11... | collective-permute-start | bytes 196616 | tf_op jit(solution)/shard_map/ppermute | solution.py:25
  34.6 0.7 fusion.18
  35.3 1.6 %copy.20 = bf16[3,1,1,128,128]{4,3,0,2,1:T(8,128)(2,1)} copy(bf16[3,1,1,128,128]{3,4,2,1,0:T(8,128)(2,1)} %get-tuple-element.39) | data formatting | bytes 196608
  36.9 0.7 copy.21
  38.4 1.0 copy.27
  39.4 1.6 %copy.28 = bf16[3,1,1,128,128]{4,3,0,2,1:T(8,128)(2,1)} copy(bf16[3,1,1,128,128]{3,4,2,1,0:T(8,128)(2,1)} %get-tuple-element.31) | data formatting | bytes 196608
  41.0 1.5 %fusion.7 = bf16[4,66,34,128]{3,2,1,0:T(8,128)(2,1)S(1)} fusion(bf16[4,64,1,128]{3,2,1,0:T(2,128)(2,1)S(1)} %collective-permute-done.2, bf16[4,64,32,128]{3,2,1,0:T(8,128)(2,1)S(1)} %constant_dynamic-update-slice_fusion, bf16[4,64,1,128]{3,2,1,0:T(2,128)(2,1)S(1)} %collective-permute-done.1), kind=kLoop, calls=%fused_computation.30 | loop fusion | flops 13787136 | bytes 4526080 | tf_op jit(solution)/shard_map/concatenate | solution.py:23
  42.6 6.9 %fusion.16 = (bf16[2,64,32,128]{3,2,1,0:T(8,128)(2,1)S(1)}, bf16[2,64,32,128]{3,2,1,0:T(8,128)(2,1)S(1)}, bf16[2,64,32,128]{3,2,1,0:T(8,128)(2,1)S(1)}, bf16[2,6...) fusion(bf16[4,66,34,128]{3,2,1,0:T(8,128)(2,1)S(1)} %fusion.7), kind=kLoop, calls=%fused_computation.60 | loop fusion | bytes 37748736 | tf_op jit(solution)/shard_map/slice | solution.py:136
  49.5 3.3 %pad_maximum_fusion.2 = (bf16[2,64,32,384]{3,2,1,0:T(8,128)(2,1)S(1)}, bf16[2,64,32,384]{3,2,1,0:T(8,128)(2,1)S(1)}) fusion(bf16[2,64,32,128]{3,2,1,0:T(8,128)(2,1)} %get-tuple-element.16, bf16[2,64,32,128]{3,2,1,0:T(8,128)(2,1)} %get-tuple-element.17, bf16[2,64,32,128]{3,2,1,0:T(8,128)(2,1)} %get-tuple-element.18, ...), kind=kLoop, calls=%fused_computation.19 | loop fusion | flops 18874368 | bytes 12582912 | tf_op jit(solution)/shard_map/concatenate | solution.py:134
  52.8 1.0 fusion.19
  53.8 1.1 convolution_add_fusion.7
  55.0 0.3 copy-done.2
  55.3 0.3 copy-done.3
  55.6 0.3 copy-done.4
  55.9 0.9 pad_maximum_fusion.4
  56.8 1.0 convolution_add_fusion.6
  57.8 2.1 %fusion.10 = (bf16[2,64,32,128]{3,2,1,0:T(8,128)(2,1)S(1)}, bf16[2,64,32,128]{3,2,1,0:T(8,128)(2,1)S(1)}, bf16[2,64,32,128]{3,2,1,0:T(8,128)(2,1)S(1)}, bf16[2,6...) fusion(bf16[4,64,32,128]{3,2,1,0:T(8,128)(2,1)S(1)} %constant_dynamic-update-slice_fusion, ...), kind=kLoop, calls=%fused_computation.44 | loop fusion | flops 8388608 | bytes 8650752 | tf_op jit(solution)/shard_map/concatenate | solution.py:23
  59.9 2.5 %fusion.1 = (bf16[2,64,32,384]{3,2,1,0:T(8,128)(2,1)S(1)}, bf16[2,64,32,384]{3,2,1,0:T(8,128)(2,1)S(1)}) fusion(bf16[4,64,1,128]{3,2,1,0:T(2,128)(2,1)S(1)} %collective-permute-done.2, bf16[4,64,32,128]{3,2,1,0:T(8,128)(2,1)S(1)} %constant_dynamic-update-slice_fusion, bf16[2,64,32,128]{3,2,1,0:T(8,128)(2,1)S(1)} %get-tuple-element.21, ...), kind=kLoop, calls=%fused_computation.16 | loop fusion | flops 25165824 | bytes 12713984 | tf_op jit(solution)/shard_map/concatenate | solution.py:134
  62.5 1.0 convolution_add_fusion.5
  63.5 0.2 copy-done.6
  63.7 0.3 copy-done.8
  64.0 0.4 pad_maximum_fusion.5
  64.4 1.0 convolution_add_fusion.4
  65.4 1.0 convolution_add_fusion.3
  66.5 1.0 convolution_add_fusion.2
  67.5 0.9 pad_maximum_fusion.7
  68.4 1.0 convolution_add_fusion.1
  69.4 1.1 multiply_convert_fusion
  70.6 0.3 convert.1
  70.9 1.0 fusion.15
  71.9 12.7 %all-to-all-start = ((bf16[1,64,32,128]{3,2,0,1:T(8,128)(2,1)}), bf16[1,64,32,128]{3,2,0,1:T(8,128)(2,1)S(1)}, u32[]{:S(2)}, u32[]{:S(2)}) async-start(bf16[1,64,32,128]{3,2,0,1:T(8,128)(2,1)} %fusion.15), calls=%async_computation | async-start | bytes 1048576 | tf_op jit(solution)/shard_map/all_to_all | solution.py:149
  84.7 12.7 %all_gather.7 = bf16[3,128,128]{1,2,0:T(8,128)(2,1)S(1)} all-gather(bf16[3,128,16]{1,2,0:T(8,128)(2,1)S(1)} %copy-done.12), channel_id=1, replica_groups=mesh['tm'=32,'fsdp'=8] {'fsdp'}, dimensions={2}, use_global_device_ids=true | all-gather | bytes 110592 | tf_op jit(solution)/shard_map/all_gather | solution.py:124
  97.4 4.6 %all-to-all-done = bf16[1,64,32,128]{3,2,0,1:T(8,128)(2,1)S(1)} async-done(((bf16[1,64,32,128]{3,2,0,1:T(8,128)(2,1)}), bf16[1,64,32,128]{3,2,0,1:T(8,128)(2,1)S(1)}, u32[]{:S(2)}, u32[]{:S(2)}) %all-to-all-start) | async-done | bytes 524320 | tf_op jit(solution)/shard_map/all_to_all | solution.py:149
  102.0 0.2 pad_slice_fusion.8
  102.3 0.3 convolution_bitcast_fusion
  102.6 0.3 convolution_bitcast_fusion.1
  103.0 0.3 convolution_add_fusion.10
  103.3 0.3 convolution_bitcast_fusion.2
  103.7 1.0 copy.30
  104.7 18.7 %shard_map.59 = f32[1,192]{1,0:T(1,128)} custom-call(f32[8,32,1,192]{3,2,1,0:T(1,128)} %bitcast.100), custom_call_target="tpu_custom_call" | custom-call | tf_op jit(solution)/shard_map/pallas_call | solution.py:100
  123.4 0.3 convolution_add_fusion.9
  123.7 1.1 fusion.8
  124.8 0.6 copy.33
  (34 shorter events, 1.1 us)
Async XLA Ops:
  0.6 101.6 %copy-start = (bf16[32,2,32,128]{3,2,1,0:T(8,128)(2,1)S(1)}, bf16[32,2,32,128]{3,2,1,0:T(8,128)(2,1)}, u32[]{:S(2)}) copy-start(bf16[32,2,32,128]{3,2,1,0:T(8,128)(2,1)} %param.7) | copy-start | bytes 1572868
  0.6 26.3 %copy-start.5 = (bf16[2,64,32,128]{3,2,1,0:T(8,128)(2,1)S(1)}, bf16[2,64,32,128]{3,2,1,0:T(8,128)(2,1)}, u32[]{:S(2)}) copy-start(bf16[2,64,32,128]{3,2,1,0:T(8,128)(2,1)} %param.4) | copy-start | bytes 3145732
  0.7 26.2 %collective-permute-start = (bf16[2,64,32,128]{3,2,1,0:T(8,128)(2,1)}, bf16[2,64,32,128]{3,2,1,0:T(8,128)(2,1)S(1)}, u32[]{:S(2)}, u32[]{:S(2)}) collective-permute-start(bf16[2,64,32,128]{3,2,1,0:T(8,128)(2,1)} %param.4), channel_id=1, source_target_pairs={{0,8},{8,16},{16,24},{24,32},{32,40},{40,48},{48,56},{56,64},{64,7... | collective-permute-start | bytes 3145736 | tf_op jit(solution)/shard_map/ppermute | solution.py:14
  26.9 8.4 %copy-start.7 = (bf16[2,64,32,128]{3,2,1,0:T(8,128)(2,1)}, bf16[2,64,32,128]{3,2,1,0:T(8,128)(2,1)S(1)}, u32[]{:S(2)}) copy-start(bf16[2,64,32,128]{3,2,1,0:T(8,128)(2,1)S(1)} %collective-permute-done) | copy-start | bytes 3145732
  28.0 13.0 %collective-permute-start.2 = (bf16[4,64,1,128]{3,2,1,0:T(2,128)(2,1)}, bf16[4,64,1,128]{3,2,1,0:T(2,128)(2,1)S(1)}, u32[]{:S(2)}, u32[]{:S(2)}) collective-permute-start(bf16[4,64,1,128]{3,2,1,0:T(2,128)(2,1)} %get-tuple-element.30), channel_id=1, source_target_pairs={{1,0},{2,1},{3,2},{4,3},{5,4},{6,5},{7,6},{9,8},{10,9},{11,10},{12... | collective-permute-start | bytes 196616 | tf_op jit(solution)/shard_map/ppermute | solution.py:27
  31.5 9.6 %collective-permute-start.1 = (bf16[4,64,1,128]{3,2,1,0:T(2,128)(2,1)}, bf16[4,64,1,128]{3,2,1,0:T(2,128)(2,1)S(1)}, u32[]{:S(2)}, u32[]{:S(2)}) collective-permute-start(bf16[4,64,1,128]{3,2,1,0:T(2,128)(2,1)} %get-tuple-element.29), channel_id=1, source_target_pairs={{0,1},{1,2},{2,3},{3,4},{4,5},{5,6},{6,7},{8,9},{9,10},{10,11},{11... | collective-permute-start | bytes 196616 | tf_op jit(solution)/shard_map/ppermute | solution.py:25
  49.5 3.3 %copy-start.10 = (bf16[3,1,1,128,128]{4,3,0,2,1:T(8,128)(2,1)S(1)}, bf16[3,1,1,128,128]{4,3,0,2,1:T(8,128)(2,1)}, u32[]{:S(2)}) copy-start(bf16[3,1,1,128,128]{4,3,0,2,1:T(8,128)(2,1)} %copy.20) | copy-start | bytes 294916
  52.8 1.0 copy-start.9
  53.8 1.2 copy-start.1
  53.8 1.5 %copy-start.2 = (bf16[2,64,32,128]{3,2,1,0:T(8,128)(2,1)S(1)}, bf16[2,64,32,128]{3,2,1,0:T(8,128)(2,1)}, u32[]{:S(2)}) copy-start(bf16[2,64,32,128]{3,2,1,0:T(8,128)(2,1)} %get-tuple-element.10) | copy-start | bytes 3145732
  53.8 1.8 %copy-start.3 = (bf16[2,64,32,128]{3,2,1,0:T(8,128)(2,1)S(1)}, bf16[2,64,32,128]{3,2,1,0:T(8,128)(2,1)}, u32[]{:S(2)}) copy-start(bf16[2,64,32,128]{3,2,1,0:T(8,128)(2,1)} %get-tuple-element.11) | copy-start | bytes 3145732
  53.8 2.1 %copy-start.4 = (bf16[2,64,32,128]{3,2,1,0:T(8,128)(2,1)S(1)}, bf16[2,64,32,128]{3,2,1,0:T(8,128)(2,1)}, u32[]{:S(2)}) copy-start(bf16[2,64,32,128]{3,2,1,0:T(8,128)(2,1)} %get-tuple-element.12) | copy-start | bytes 3145732
  62.5 1.2 copy-start.6
  62.5 1.5 %copy-start.8 = (bf16[2,64,32,128]{3,2,1,0:T(8,128)(2,1)S(1)}, bf16[2,64,32,128]{3,2,1,0:T(8,128)(2,1)}, u32[]{:S(2)}) copy-start(bf16[2,64,32,128]{3,2,1,0:T(8,128)(2,1)} %copy-done.7) | copy-start | bytes 3145732
  68.4 1.0 copy-start.11
  70.6 14.1 %copy-start.12 = (bf16[3,128,16]{1,2,0:T(8,128)(2,1)S(1)}, bf16[3,128,16]{1,2,0:T(8,128)(2,1)}, u32[]{:S(2)}) copy-start(bf16[3,128,16]{1,2,0:T(8,128)(2,1)} %param.6) | copy-start | bytes 36868
  71.9 30.1 %all-to-all-start = ((bf16[1,64,32,128]{3,2,0,1:T(8,128)(2,1)}), bf16[1,64,32,128]{3,2,0,1:T(8,128)(2,1)S(1)}, u32[]{:S(2)}, u32[]{:S(2)}) async-start(bf16[1,64,32,128]{3,2,0,1:T(8,128)(2,1)} %fusion.15), calls=%async_computation | async-start | bytes 1048576 | tf_op jit(solution)/shard_map/all_to_all | solution.py:149
  123.4 1.4 %copy-start.13 = (f32[1,192]{1,0:T(1,128)S(1)}, f32[1,192]{1,0:T(1,128)}, u32[]{:S(2)}) copy-start(f32[1,192]{1,0:T(1,128)} %shard_map.59) | copy-start | bytes 2308

commit v6 on v5

--- a/solution.py
+++ b/solution.py
@@ -118,6 +118,47 @@
     return out.reshape(piece)
 
 
+def conv_pool_kernel(xs_ref, w_ref, o_ref):
+    height, width, channels = o_ref.shape
+    rows = 8
+
+    def body(r, carry):
+        top = pl.multiple_of(r * rows, rows)
+        hidden = []
+        for j in range(2):
+            acc = jnp.zeros((rows * width, channels), jnp.float32)
+            for b in range(3):
+                for c in range(3):
+                    taps = [xs_ref[c, j + a, pl.ds(top + b, rows)] for a in range(3)]
+                    lhs = jnp.concatenate(taps, axis=-1).reshape(rows * width, 3 * channels)
+                    acc = acc + jnp.dot(lhs, w_ref[b * 3 + c], preferred_element_type=jnp.float32)
+            silu = acc / (1.0 + jnp.exp(-acc))
+            hidden.append(silu.astype(jnp.bfloat16).astype(jnp.float32))
+        pooled = ((hidden[0] + hidden[1]) * 0.5).astype(o_ref.dtype)
+        o_ref[pl.ds(top, rows)] = pooled.reshape(rows, width, channels)
+        return carry
+
+    lax.fori_loop(0, height // rows, body, 0)
+
+
+def conv_pool(shifted, weights):
+    _, _, rows, width, channels = shifted.shape
+    height = rows - 2
+    vmem = pl.BlockSpec(memory_space=pltpu.VMEM)
+    flops = 2 * 2 * height * width * weights.shape[0] * weights.shape[1] * channels
+    return pl.pallas_call(
+        conv_pool_kernel,
+        out_shape=jax.ShapeDtypeStruct((height, width, channels), jnp.bfloat16),
+        in_specs=[vmem, vmem],
+        out_specs=vmem,
+        cost_estimate=pl.CostEstimate(
+            flops=flops,
+            transcendentals=2 * height * width * channels,
+            bytes_accessed=shifted.size * 2 + weights.size * 2 + height * width * channels * 2,
+        ),
+    )(shifted, weights)
+
+
 def local(frames, conv_weight, mix_weight, cotangent):
     full_conv, full_mix = (
         lax.all_gather(conv_weight, "fsdp", axis=4, tiled=True),
@@ -128,25 +169,10 @@
     timed = jnp.concatenate([previous, frames], axis=0)
     padded = with_halo(timed, (("fsdp", 2),), 1)
     padded = jnp.pad(padded, ((0, 0), (1, 1), (0, 0), (0, 0)))
-    accum = jnp.zeros((count_frames * height * width, channels), jnp.float32)
-    for row_tap in range(3):
-        for col_tap in range(3):
-            stacked = jnp.concatenate(
-                [
-                    padded[
-                        step : step + count_frames,
-                        row_tap : row_tap + height,
-                        col_tap : col_tap + width,
-                        :,
-                    ]
-                    for step in range(3)
-                ],
-                axis=3,
-            ).reshape(-1, 3 * channels)
-            kernel = full_conv[:, row_tap, col_tap].reshape(3 * channels, channels)
-            accum = accum + jnp.dot(stacked, kernel, preferred_element_type=jnp.float32)
-    hidden = jax.nn.silu(accum).astype(jnp.bfloat16).reshape(count_frames, height, width, channels)
-    pooled = lax.all_to_all(pool_pairs(hidden), "tm", split_axis=1, concat_axis=0, tiled=True)
+    shifted = jnp.stack([padded[:, :, c : c + width] for c in range(3)])
+    weights = jnp.transpose(full_conv, (1, 2, 0, 3, 4)).reshape(9, 3 * channels, -1)
+    pooled = conv_pool(shifted, weights)[None]
+    pooled = lax.all_to_all(pooled, "tm", split_axis=1, concat_axis=0, tiled=True)
     branch = pooled.astype(jnp.float32).reshape(-1, channels)
     flat_cot = cotangent.reshape(-1, channels)
     grad_terms = []

time: 126 us -> 123 us (0.976)
  waiting for transfers between devices: 11.7 us -> 25.7 us
  Pallas kernels: 18.7 us -> 30.9 us
  local copies, waits for them, and re-layouts: 18 us -> 6.1 us
  matrix products: 11.9 us -> 2.7 us
  other arithmetic: 12.9 us -> 5.77 us
    ppermute x1, waiting for transfers between devices: 7.05 us -> 22.1 us  [from_behind(): return lax.ppermute(block, axis, route)]
    pallas_call x0 -> x1, Pallas kernels: none -> 12.7 us  [conv_pool(): pl.pallas_call(conv_pool_kernel, out_shape=jax.ShapeDtypeStruct((height,...]
    dot_general x9 -> x0, matrix products: 9.2 us -> none  [local(): accum = accum + jnp.dot(stacked, kernel, preferred_element_type=jnp.float32)]
    concatenate x5 -> x0, other arithmetic: 7.93 us -> none  [local(): jnp.concatenate([padded[step:step + count_frames, row_tap:row_tap + heigh...]
    slice x2 -> x0, local copies, waits for them, and re-layouts: 7.65 us -> none  [the longest x1 6.91 us: local(): padded[step:step + count_frames, row_tap:row_tap + height, col_tap:col_ta...]
    unnamed x39 -> x12, local copies, waits for them, and re-layouts: 7.96 us -> 0.66 us
    another operation x0 -> x1, other arithmetic: none -> 3.23 us  [local(): shifted = jnp.stack([padded[:, :, c:c + width] for c in range(3)])]
    another operation x0 -> x1, local copies, waits for them, and re-layouts: none -> 1.58 us  [local(): shifted = jnp.stack([padded[:, :, c:c + width] for c in range(3)])]
  transfers between devices with their start and end apart: 4 -> 4, of which waited for: 2 -> 2; matrix products, arithmetic and copies ran while one was open for 5% -> 1% of each run, Pallas kernels for 0% -> 0%
where the time goes in v6:
time: 123 us
  Pallas kernels  30.9 us (25%)
  blocking collectives  27.4 us (22%)
  waiting for transfers between devices  25.7 us (21%)
  starting transfers between devices  23.5 us (19%)
  local copies, waits for them, and re-layouts  6.1 us (5%)
  other arithmetic  5.77 us (5%)
  matrix products  2.7 us (2%)
    ppermute x1, waiting for transfers between devices, from_behind(): return lax.ppermute(block, axis, route)  22.1 us
    pallas_call x1, Pallas kernels, scatter_sum(): pl.pallas_call(scatter_kernel, out_shape=jax.ShapeDtypeStruct((1, piece),...  18.2 us
    all_gather x1, blocking collectives, local(): lax.all_gather(conv_weight, 'fsdp', axis=4, tiled=True)  14.4 us
    all_gather x1, blocking collectives, local(): lax.all_gather(mix_weight, 'fsdp', axis=2, tiled=True)  13 us
    all_to_all x1, starting transfers between devices, local(): lax.all_to_all(pooled, 'tm', split_axis=1, concat_axis=0, tiled=True)  12.8 us
    pallas_call x1, Pallas kernels, conv_pool(): pl.pallas_call(conv_pool_kernel, out_shape=jax.ShapeDtypeStruct((height,...  12.7 us
    ppermute x1, starting transfers between devices, with_halo(): lax.ppermute(tail, axis, [(i, (i + 1) % count) for i in range(ends)])  4.63 us
    ppermute x1, starting transfers between devices, from_behind(): return lax.ppermute(block, axis, route)  4.14 us
  transfers between devices with their start and end apart: 4, of which 2 were waited for; matrix products, arithmetic and copies ran while one was open for 1% of the time, Pallas kernels for 0%

profile of v6, /device:TPU:1, one launch (start us, length us, event | category | flops | bytes accessed | tf_op | source)
XLA Modules:
  0.0 122.9 jit_solution(11573580315733701602)
XLA Ops:
  0.6 0.0 copy-start
  0.6 0.0 copy-start.1
  0.7 0.0 copy-start.2
  0.7 4.1 %collective-permute-start = (bf16[2,64,32,128]{3,2,1,0:T(8,128)(2,1)}, bf16[2,64,32,128]{3,2,1,0:T(8,128)(2,1)S(1)}, u32[]{:S(2)}, u32[]{:S(2)}) collective-permute-start(bf16[2,64,32,128]{3,2,1,0:T(8,128)(2,1)} %param.4), channel_id=1, source_target_pairs={{0,8},{8,16},{16,24},{24,32},{32,40},{40,48},{48,56},{56,64},{64,7... | collective-permute-start | bytes 3145736 | tf_op jit(solution)/shard_map/ppermute | solution.py:14
  4.8 22.1 %collective-permute-done = bf16[2,64,32,128]{3,2,1,0:T(8,128)(2,1)S(1)} collective-permute-done((bf16[2,64,32,128]{3,2,1,0:T(8,128)(2,1)}, bf16[2,64,32,128]{3,2,1,0:T(8,128)(2,1)S(1)}, u32[]{:S(2)}, u32[]{:S(2)}) %collective-permute-start) | collective-permute-done | bytes 1048608 | tf_op jit(solution)/shard_map/ppermute | solution.py:14
  26.9 0.1 constant_dynamic-update-slice_fusion.1
  26.9 0.0 copy-done.1
  27.0 0.1 constant_dynamic-update-slice_fusion
  27.1 0.9 fusion.7
  28.0 4.6 %collective-permute-start.1 = (bf16[4,64,1,128]{3,2,1,0:T(2,128)(2,1)}, bf16[4,64,1,128]{3,2,1,0:T(2,128)(2,1)}, u32[]{:S(2)}, u32[]{:S(2)}) collective-permute-start(bf16[4,64,1,128]{3,2,1,0:T(2,128)(2,1)} %get-tuple-element.5), channel_id=1, source_target_pairs={{0,1},{1,2},{2,3},{3,4},{4,5},{5,6},{6,7},{8,9},{9,10},{10,11},{11... | collective-permute-start | bytes 196616 | tf_op jit(solution)/shard_map/ppermute | solution.py:25
  32.6 1.9 %collective-permute-start.2 = (bf16[4,64,1,128]{3,2,1,0:T(2,128)(2,1)}, bf16[4,64,1,128]{3,2,1,0:T(2,128)(2,1)}, u32[]{:S(2)}, u32[]{:S(2)}) collective-permute-start(bf16[4,64,1,128]{3,2,1,0:T(2,128)(2,1)} %get-tuple-element.6), channel_id=1, source_target_pairs={{1,0},{2,1},{3,2},{4,3},{5,4},{6,5},{7,6},{9,8},{10,9},{11,10},{12... | collective-permute-start | bytes 196616 | tf_op jit(solution)/shard_map/ppermute | solution.py:27
  34.6 0.0 copy-done.2
  34.6 14.4 %all_gather.6 = bf16[3,3,3,128,128]{3,4,2,1,0:T(8,128)(2,1)S(1)} all-gather(bf16[3,3,3,128,16]{3,4,2,1,0:T(8,128)(2,1)S(1)} %copy-done.2), channel_id=1, replica_groups=mesh['tm'=32,'fsdp'=8] {'fsdp'}, dimensions={4}, use_global_device_ids=true | all-gather | bytes 995328 | tf_op jit(solution)/shard_map/all_gather | solution.py:164
  49.0 1.5 %copy.9 = bf16[3,3,3,128,128]{4,3,2,1,0:T(8,128)(2,1)} copy(bf16[3,3,3,128,128]{3,4,1,0,2:T(8,128)(2,1)S(1)} %bitcast.59) | data formatting | bytes 1769472 | tf_op jit(solution)/shard_map/transpose | solution.py:173
  50.5 0.0 collective-permute-done.1
  50.5 0.0 collective-permute-done.2
  50.5 2.5 %fusion.5 = bf16[4,66,34,128]{3,2,1,0:T(8,128)(2,1)S(1)} fusion(bf16[4,64,1,128]{3,2,1,0:T(2,128)(2,1)} %collective-permute-done.2, bf16[4,64,32,128]{3,2,1,0:T(8,128)(2,1)S(1)} %constant_dynamic-update-slice_fusion, bf16[4,64,1,128]{3,2,1,0:T(2,128)(2,1)} %collective-permute-done.1), kind=kLoop, calls=%fused_computation.8 | loop fusion | flops 13787136 | bytes 4526080 | tf_op jit(solution)/shard_map/concatenate | solution.py:23
  53.0 1.6 %slice_bitcast_fusion.2 = (bf16[1,4,66,32,128]{4,3,2,1,0:T(8,128)(2,1)S(1)}, bf16[1,4,66,32,128]{4,3,2,1,0:T(8,128)(2,1)S(1)}, bf16[1,4,66,32,128]{4,3,2,1,0:T(8,128)(2,1)S(1)}) fusion(bf16[4,66,34,128]{3,2,1,0:T(8,128)(2,1)S(1)} %fusion.5), kind=kLoop, calls=%fused_computation.15 | loop fusion | bytes 12976128 | tf_op jit(solution)/shard_map/stack | solution.py:172
  54.6 3.2 %pad_maximum_fusion.xs_ref = bf16[3,4,66,32,128]{4,3,2,1,0:T(8,128)(2,1)} fusion(bf16[1,4,66,32,128]{4,3,2,1,0:T(8,128)(2,1)S(1)} %get-tuple-element.4, bf16[1,4,66,32,128]{4,3,2,1,0:T(8,128)(2,1)S(1)} %get-tuple-element.3, bf16[1,4,66,32,128]{4,3,2,1,0:T(8,128)(2,1)S(1)} %get-tuple-element.2), kind=kLoop, calls=%fused_computation.2 | loop fusion | flops 6488064 | bytes 12976128 | tf_op jit(solution)/shard_map/stack | solution.py:172
  57.8 0.0 copy-start.3
  57.8 12.7 %shard_map.59 = bf16[64,32,128]{2,1,0:T(8,128)(2,1)} custom-call(bf16[3,4,66,32,128]{4,3,2,1,0:T(8,128)(2,1)} %pad_maximum_fusion.xs_ref, bf16[9,384,128]{2,1,0:T(8,128)(2,1)} %bitcast.63), custom_call_target="tpu_custom_call" | custom-call | flops 3623878656 | bytes 7897088 | tf_op jit(solution)/shard_map/pallas_call | solution.py:149
  70.5 12.8 %all-to-all-start = ((bf16[1,64,32,128]{3,2,0,1:T(8,128)(2,1)}), bf16[1,64,32,128]{3,2,0,1:T(8,128)(2,1)S(1)}, u32[]{:S(2)}, u32[]{:S(2)}) async-start(bf16[1,64,32,128]{3,2,0,1:T(8,128)(2,1)} %bitcast.64), calls=%async_computation | async-start | bytes 1048576 | tf_op jit(solution)/shard_map/all_to_all | solution.py:175
  83.3 0.0 copy-done.3
  83.3 13.0 %all_gather.7 = bf16[3,128,128]{1,2,0:T(8,128)(2,1)S(1)} all-gather(bf16[3,128,16]{1,2,0:T(8,128)(2,1)S(1)} %copy-done.3), channel_id=1, replica_groups=mesh['tm'=32,'fsdp'=8] {'fsdp'}, dimensions={2}, use_global_device_ids=true | all-gather | bytes 110592 | tf_op jit(solution)/shard_map/all_gather | solution.py:165
  96.3 3.7 %all-to-all-done = bf16[1,64,32,128]{3,2,0,1:T(8,128)(2,1)S(1)} async-done(((bf16[1,64,32,128]{3,2,0,1:T(8,128)(2,1)}), bf16[1,64,32,128]{3,2,0,1:T(8,128)(2,1)S(1)}, u32[]{:S(2)}, u32[]{:S(2)}) %all-to-all-start) | async-done | bytes 524320 | tf_op jit(solution)/shard_map/all_to_all | solution.py:175
  100.0 0.0 copy-done
  100.0 0.3 convolution_bitcast_fusion
  100.3 0.3 convolution_bitcast_fusion.1
  100.7 0.2 pad_slice_fusion
  100.9 0.3 convolution_bitcast_fusion.2
  101.3 0.1 reshape_reshape.3
  101.4 1.0 copy.15
  102.4 18.2 %shard_map.60 = f32[1,192]{1,0:T(1,128)} custom-call(f32[8,32,1,192]{3,2,1,0:T(1,128)} %bitcast.62), custom_call_target="tpu_custom_call" | custom-call | tf_op jit(solution)/shard_map/pallas_call | solution.py:100
  120.6 0.3 convolution_add_fusion.2
  120.9 0.0 copy-start.4
  120.9 0.3 convolution_add_fusion.1
  121.2 1.1 fusion.6
  122.3 0.0 copy-done.4
  122.3 0.6 copy.18
  (1 shorter events, 0.0 us)
Async XLA Ops:
  0.6 99.4 %copy-start = (bf16[32,2,32,128]{3,2,1,0:T(8,128)(2,1)S(1)}, bf16[32,2,32,128]{3,2,1,0:T(8,128)(2,1)}, u32[]{:S(2)}) copy-start(bf16[32,2,32,128]{3,2,1,0:T(8,128)(2,1)} %param.7) | copy-start | bytes 1572868
  0.6 26.3 %copy-start.1 = (bf16[2,64,32,128]{3,2,1,0:T(8,128)(2,1)S(1)}, bf16[2,64,32,128]{3,2,1,0:T(8,128)(2,1)}, u32[]{:S(2)}) copy-start(bf16[2,64,32,128]{3,2,1,0:T(8,128)(2,1)} %param.4) | copy-start | bytes 3145732
  0.7 33.9 %copy-start.2 = (bf16[3,3,3,128,16]{3,4,2,1,0:T(8,128)(2,1)S(1)}, bf16[3,3,3,128,16]{3,4,2,1,0:T(8,128)(2,1)}, u32[]{:S(2)}) copy-start(bf16[3,3,3,128,16]{3,4,2,1,0:T(8,128)(2,1)} %param.5) | copy-start | bytes 331780
  0.7 26.2 %collective-permute-start = (bf16[2,64,32,128]{3,2,1,0:T(8,128)(2,1)}, bf16[2,64,32,128]{3,2,1,0:T(8,128)(2,1)S(1)}, u32[]{:S(2)}, u32[]{:S(2)}) collective-permute-start(bf16[2,64,32,128]{3,2,1,0:T(8,128)(2,1)} %param.4), channel_id=1, source_target_pairs={{0,8},{8,16},{16,24},{24,32},{32,40},{40,48},{48,56},{56,64},{64,7... | collective-permute-start | bytes 3145736 | tf_op jit(solution)/shard_map/ppermute | solution.py:14
  28.0 22.5 %collective-permute-start.1 = (bf16[4,64,1,128]{3,2,1,0:T(2,128)(2,1)}, bf16[4,64,1,128]{3,2,1,0:T(2,128)(2,1)}, u32[]{:S(2)}, u32[]{:S(2)}) collective-permute-start(bf16[4,64,1,128]{3,2,1,0:T(2,128)(2,1)} %get-tuple-element.5), channel_id=1, source_target_pairs={{0,1},{1,2},{2,3},{3,4},{4,5},{5,6},{6,7},{8,9},{9,10},{10,11},{11... | collective-permute-start | bytes 196616 | tf_op jit(solution)/shard_map/ppermute | solution.py:25
  32.6 17.8 %collective-permute-start.2 = (bf16[4,64,1,128]{3,2,1,0:T(2,128)(2,1)}, bf16[4,64,1,128]{3,2,1,0:T(2,128)(2,1)}, u32[]{:S(2)}, u32[]{:S(2)}) collective-permute-start(bf16[4,64,1,128]{3,2,1,0:T(2,128)(2,1)} %get-tuple-element.6), channel_id=1, source_target_pairs={{1,0},{2,1},{3,2},{4,3},{5,4},{6,5},{7,6},{9,8},{10,9},{11,10},{12... | collective-permute-start | bytes 196616 | tf_op jit(solution)/shard_map/ppermute | solution.py:27
  57.8 25.5 %copy-start.3 = (bf16[3,128,16]{1,2,0:T(8,128)(2,1)S(1)}, bf16[3,128,16]{1,2,0:T(8,128)(2,1)}, u32[]{:S(2)}) copy-start(bf16[3,128,16]{1,2,0:T(8,128)(2,1)} %param.6) | copy-start | bytes 36868
  70.5 29.5 %all-to-all-start = ((bf16[1,64,32,128]{3,2,0,1:T(8,128)(2,1)}), bf16[1,64,32,128]{3,2,0,1:T(8,128)(2,1)S(1)}, u32[]{:S(2)}, u32[]{:S(2)}) async-start(bf16[1,64,32,128]{3,2,0,1:T(8,128)(2,1)} %bitcast.64), calls=%async_computation | async-start | bytes 1048576 | tf_op jit(solution)/shard_map/all_to_all | solution.py:175
  120.9 1.4 %copy-start.4 = (f32[1,192]{1,0:T(1,128)S(1)}, f32[1,192]{1,0:T(1,128)}, u32[]{:S(2)}) copy-start(f32[1,192]{1,0:T(1,128)} %shard_map.60) | copy-start | bytes 2308

commit v7 on v6

--- a/solution.py
+++ b/solution.py
@@ -160,10 +160,16 @@
 
 
 def local(frames, conv_weight, mix_weight, cotangent):
-    full_conv, full_mix = (
-        lax.all_gather(conv_weight, "fsdp", axis=4, tiled=True),
-        lax.all_gather(mix_weight, "fsdp", axis=2, tiled=True),
-    )
+    groups = lax.axis_size("fsdp")
+    f = lax.axis_index("fsdp")
+    shards = [conv_weight] + [
+        lax.ppermute(conv_weight, "fsdp", [((g + k) % groups, g) for g in range(groups)])
+        for k in range(1, groups)
+    ]
+    stacked = jnp.stack(shards)
+    order = lax.rem(jnp.arange(groups) - f + groups, groups)
+    full_conv = jnp.concatenate([stacked[order[g]] for g in range(groups)], axis=-1)
+    full_mix = lax.all_gather(mix_weight, "fsdp", axis=2, tiled=True)
     count_frames, height, width, channels = frames.shape
     previous = from_behind(frames, "tm", 1)
     timed = jnp.concatenate([previous, frames], axis=0)

time: 123 us -> 137 us (1.11)
  between operations: 0.8 us -> 16.1 us
  blocking collectives: 27.4 us -> 14 us
  starting transfers between devices: 23.5 us -> 31.5 us
  local copies, waits for them, and re-layouts: 6.1 us -> 9.67 us
    all_gather x2 -> x1, blocking collectives: 27.4 us -> 14 us  [local(): full_mix = lax.all_gather(mix_weight, 'fsdp', axis=2, tiled=True)]
    ppermute x0 -> x7, starting transfers between devices: none -> 9.97 us  [local(): lax.ppermute(conv_weight, 'fsdp', [((g + k) % groups, g) for g in range(g...]
    unnamed x12 -> x26, local copies, waits for them, and re-layouts: 0.66 us -> 2.76 us
  transfers between devices with their start and end apart: 4 -> 11, of which waited for: 2 -> 3; matrix products, arithmetic and copies ran while one was open for 1% -> 3% of each run, Pallas kernels for 0% -> 0%
where the time goes in v7:
time: 137 us; the launch traced here: 136 us
  starting transfers between devices  31.5 us (23%)
  Pallas kernels  30.3 us (22%)
  waiting for transfers between devices  26.2 us (19%)
  between operations  16.1 us (12%)
  blocking collectives  14 us (10%)
  local copies, waits for them, and re-layouts  9.67 us (7%)
  other arithmetic  5.73 us (4%)
  matrix products  2.7 us (2%)
    ppermute x1, waiting for transfers between devices, from_behind(): return lax.ppermute(block, axis, route)  21.7 us
    pallas_call x1, Pallas kernels, scatter_sum(): pl.pallas_call(scatter_kernel, out_shape=jax.ShapeDtypeStruct((1, piece),...  17.6 us
    all_gather x1, blocking collectives, local(): full_mix = lax.all_gather(mix_weight, 'fsdp', axis=2, tiled=True)  14 us
    all_to_all x1, starting transfers between devices, local(): lax.all_to_all(pooled, 'tm', split_axis=1, concat_axis=0, tiled=True)  12.8 us
    pallas_call x1, Pallas kernels, conv_pool(): pl.pallas_call(conv_pool_kernel, out_shape=jax.ShapeDtypeStruct((height,...  12.7 us
    ppermute x7, starting transfers between devices, local(): lax.ppermute(conv_weight, 'fsdp', [((g + k) % groups, g) for g in range(g...  9.97 us
    ppermute x1, starting transfers between devices, with_halo(): lax.ppermute(tail, axis, [(i, (i + 1) % count) for i in range(ends)])  3.37 us
    all_to_all x1, waiting for transfers between devices, local(): lax.all_to_all(pooled, 'tm', split_axis=1, concat_axis=0, tiled=True)  3.34 us
  transfers between devices with their start and end apart: 11, of which 3 were waited for; matrix products, arithmetic and copies ran while one was open for 3% of the time, Pallas kernels for 0%

profile of v7, /device:TPU:1, one launch (start us, length us, event | category | flops | bytes accessed | tf_op | source)
XLA Modules:
  0.0 136.1 jit_solution(16117060858252705196)
XLA Ops:
  0.6 0.0 copy-start
  0.6 3.3 %collective-permute-start.3 = (bf16[3,3,3,128,16]{3,4,2,1,0:T(8,128)(2,1)}, bf16[3,3,3,128,16]{3,4,2,1,0:T(8,128)(2,1)S(1)}, u32[]{:S(2)}, u32[]{:S(2)}) collective-permute-start(bf16[3,3,3,128,16]{3,4,2,1,0:T(8,128)(2,1)} %param.5), channel_id=1, source_target_pairs={{1,0},{2,1},{3,2},{4,3},{5,4},{6,5},{7,6},{0,7},{9,8},{10,9},{11,1... | collective-permute-start | bytes 331784 | tf_op jit(solution)/shard_map/ppermute | solution.py:166
  3.9 1.0 collective-permute-start.4
  4.9 0.7 collective-permute-start.5
  5.6 2.4 %collective-permute-start.6 = (bf16[3,3,3,128,16]{3,4,2,1,0:T(8,128)(2,1)}, bf16[3,3,3,128,16]{3,4,2,1,0:T(8,128)(2,1)S(1)}, u32[]{:S(2)}, u32[]{:S(2)}) collective-permute-start(bf16[3,3,3,128,16]{3,4,2,1,0:T(8,128)(2,1)} %param.5), channel_id=1, source_target_pairs={{4,0},{5,1},{6,2},{7,3},{0,4},{1,5},{2,6},{3,7},{12,8},{13,9},{14,... | collective-permute-start | bytes 331784 | tf_op jit(solution)/shard_map/ppermute | solution.py:166
  8.0 0.8 collective-permute-start.7
  8.8 0.9 bitcast_dynamic-update-slice_fusion.15
  9.7 0.7 fusion.9
  25.5 0.0 copy-start.2
  25.5 0.0 collective-permute-done.3
  25.5 0.8 collective-permute-start.8
  26.4 0.0 collective-permute-done.4
  26.4 1.0 collective-permute-start.9
  27.4 0.0 collective-permute-done.5
  27.4 3.2 %collective-permute-start = (bf16[2,64,32,128]{3,2,1,0:T(8,128)(2,1)}, bf16[2,64,32,128]{3,2,1,0:T(8,128)(2,1)S(1)}, u32[]{:S(2)}, u32[]{:S(2)}) collective-permute-start(bf16[2,64,32,128]{3,2,1,0:T(8,128)(2,1)} %param.4), channel_id=1, source_target_pairs={{0,8},{8,16},{16,24},{24,32},{32,40},{40,48},{48,56},{56,64},{64,7... | collective-permute-start | bytes 3145736 | tf_op jit(solution)/shard_map/ppermute | solution.py:14
  30.6 0.0 collective-permute-done.6
  30.7 0.0 collective-permute-done.7
  30.7 1.2 collective-permute-done.8
  31.9 0.0 collective-permute-done.9
  32.1 21.7 %collective-permute-done = bf16[2,64,32,128]{3,2,1,0:T(8,128)(2,1)S(1)} collective-permute-done((bf16[2,64,32,128]{3,2,1,0:T(8,128)(2,1)}, bf16[2,64,32,128]{3,2,1,0:T(8,128)(2,1)S(1)}, u32[]{:S(2)}, u32[]{:S(2)}) %collective-permute-start) | collective-permute-done | bytes 1048608 | tf_op jit(solution)/shard_map/ppermute | solution.py:14
  53.8 0.1 constant_dynamic-update-slice_fusion.1
  53.9 0.1 constant_dynamic-update-slice_fusion
  54.1 0.9 fusion.8
  55.0 2.2 %collective-permute-start.2 = (bf16[4,64,1,128]{3,2,1,0:T(2,128)(2,1)}, bf16[4,64,1,128]{3,2,1,0:T(2,128)(2,1)}, u32[]{:S(2)}, u32[]{:S(2)}) collective-permute-start(bf16[4,64,1,128]{3,2,1,0:T(2,128)(2,1)} %get-tuple-element.6), channel_id=1, source_target_pairs={{1,0},{2,1},{3,2},{4,3},{5,4},{6,5},{7,6},{9,8},{10,9},{11,10},{12... | collective-permute-start | bytes 196616 | tf_op jit(solution)/shard_map/ppermute | solution.py:27
  57.2 3.4 %collective-permute-start.1 = (bf16[4,64,1,128]{3,2,1,0:T(2,128)(2,1)}, bf16[4,64,1,128]{3,2,1,0:T(2,128)(2,1)}, u32[]{:S(2)}, u32[]{:S(2)}) collective-permute-start(bf16[4,64,1,128]{3,2,1,0:T(2,128)(2,1)} %get-tuple-element.5), channel_id=1, source_target_pairs={{0,1},{1,2},{2,3},{3,4},{4,5},{5,6},{6,7},{8,9},{9,10},{10,11},{11... | collective-permute-start | bytes 196616 | tf_op jit(solution)/shard_map/ppermute | solution.py:25
  60.6 0.9 copy-done.1
  61.5 2.3 %copy.8 = bf16[3,3,3,128,128]{4,3,2,1,0:T(8,128)(2,1)} copy(bf16[3,3,3,128,128]{3,4,1,0,2:T(8,128)(2,1)} %bitcast.101) | data formatting | bytes 1769472 | tf_op jit(solution)/shard_map/transpose | solution.py:179
  63.7 0.0 collective-permute-done.2
  63.7 0.0 collective-permute-done.1
  63.8 2.5 %fusion.5 = bf16[4,66,34,128]{3,2,1,0:T(8,128)(2,1)S(1)} fusion(bf16[4,64,1,128]{3,2,1,0:T(2,128)(2,1)} %collective-permute-done.2, bf16[4,64,32,128]{3,2,1,0:T(8,128)(2,1)S(1)} %constant_dynamic-update-slice_fusion, bf16[4,64,1,128]{3,2,1,0:T(2,128)(2,1)} %collective-permute-done.1), kind=kLoop, calls=%fused_computation.8 | loop fusion | flops 13787136 | bytes 4526080 | tf_op jit(solution)/shard_map/concatenate | solution.py:23
  66.3 1.6 %slice_bitcast_fusion.2 = (bf16[1,4,66,32,128]{4,3,2,1,0:T(8,128)(2,1)S(1)}, bf16[1,4,66,32,128]{4,3,2,1,0:T(8,128)(2,1)S(1)}, bf16[1,4,66,32,128]{4,3,2,1,0:T(8,128)(2,1)S(1)}) fusion(bf16[4,66,34,128]{3,2,1,0:T(8,128)(2,1)S(1)} %fusion.5), kind=kLoop, calls=%fused_computation.15 | loop fusion | bytes 12976128 | tf_op jit(solution)/shard_map/stack | solution.py:178
  67.9 3.2 %pad_maximum_fusion.xs_ref = bf16[3,4,66,32,128]{4,3,2,1,0:T(8,128)(2,1)} fusion(bf16[1,4,66,32,128]{4,3,2,1,0:T(8,128)(2,1)S(1)} %get-tuple-element.4, bf16[1,4,66,32,128]{4,3,2,1,0:T(8,128)(2,1)S(1)} %get-tuple-element.3, bf16[1,4,66,32,128]{4,3,2,1,0:T(8,128)(2,1)S(1)} %get-tuple-element.2), kind=kLoop, calls=%fused_computation.2 | loop fusion | flops 6488064 | bytes 12976128 | tf_op jit(solution)/shard_map/stack | solution.py:178
  71.1 12.7 %shard_map.59 = bf16[64,32,128]{2,1,0:T(8,128)(2,1)} custom-call(bf16[3,4,66,32,128]{4,3,2,1,0:T(8,128)(2,1)} %pad_maximum_fusion.xs_ref, bf16[9,384,128]{2,1,0:T(8,128)(2,1)} %bitcast.103), custom_call_target="tpu_custom_call" | custom-call | flops 3623878656 | bytes 7897088 | tf_op jit(solution)/shard_map/pallas_call | solution.py:149
  83.7 12.8 %all-to-all-start = ((bf16[1,64,32,128]{3,2,0,1:T(8,128)(2,1)}), bf16[1,64,32,128]{3,2,0,1:T(8,128)(2,1)S(1)}, u32[]{:S(2)}, u32[]{:S(2)}) async-start(bf16[1,64,32,128]{3,2,0,1:T(8,128)(2,1)} %bitcast.104), calls=%async_computation | async-start | bytes 1048576 | tf_op jit(solution)/shard_map/all_to_all | solution.py:181
  96.5 14.0 %all_gather.3 = bf16[3,128,128]{1,2,0:T(8,128)(2,1)S(1)} all-gather(bf16[3,128,16]{1,2,0:T(8,128)(2,1)S(1)} %copy-done.3), channel_id=1, replica_groups=mesh['tm'=32,'fsdp'=8] {'fsdp'}, dimensions={2}, use_global_device_ids=true | all-gather | bytes 110592 | tf_op jit(solution)/shard_map/all_gather | solution.py:172
  110.5 3.3 %all-to-all-done = bf16[1,64,32,128]{3,2,0,1:T(8,128)(2,1)S(1)} async-done(((bf16[1,64,32,128]{3,2,0,1:T(8,128)(2,1)}), bf16[1,64,32,128]{3,2,0,1:T(8,128)(2,1)S(1)}, u32[]{:S(2)}, u32[]{:S(2)}) %all-to-all-start) | async-done | bytes 524320 | tf_op jit(solution)/shard_map/all_to_all | solution.py:181
  113.8 0.2 pad_slice_fusion
  114.1 0.0 copy-done
  114.1 0.3 convolution_bitcast_fusion
  114.4 0.3 convolution_bitcast_fusion.1
  114.8 0.3 convolution_add_fusion.2
  115.1 0.3 convolution_bitcast_fusion.2
  115.5 0.1 reshape_reshape.3
  115.6 1.0 copy.14
  116.5 17.6 %shard_map.60 = f32[1,192]{1,0:T(1,128)} custom-call(f32[8,32,1,192]{3,2,1,0:T(1,128)} %bitcast.102), custom_call_target="tpu_custom_call" | custom-call | tf_op jit(solution)/shard_map/pallas_call | solution.py:100
  134.1 0.3 convolution_add_fusion.1
  134.4 1.1 fusion.6
  135.5 0.6 copy.31
  (23 shorter events, 0.3 us)
Async XLA Ops:
  0.6 113.5 %copy-start = (bf16[32,2,32,128]{3,2,1,0:T(8,128)(2,1)S(1)}, bf16[32,2,32,128]{3,2,1,0:T(8,128)(2,1)}, u32[]{:S(2)}) copy-start(bf16[32,2,32,128]{3,2,1,0:T(8,128)(2,1)} %param.7) | copy-start | bytes 1572868
  0.6 24.9 %collective-permute-start.3 = (bf16[3,3,3,128,16]{3,4,2,1,0:T(8,128)(2,1)}, bf16[3,3,3,128,16]{3,4,2,1,0:T(8,128)(2,1)S(1)}, u32[]{:S(2)}, u32[]{:S(2)}) collective-permute-start(bf16[3,3,3,128,16]{3,4,2,1,0:T(8,128)(2,1)} %param.5), channel_id=1, source_target_pairs={{1,0},{2,1},{3,2},{4,3},{5,4},{6,5},{7,6},{0,7},{9,8},{10,9},{11,1... | collective-permute-start | bytes 331784 | tf_op jit(solution)/shard_map/ppermute | solution.py:166
  3.9 22.5 %collective-permute-start.4 = (bf16[3,3,3,128,16]{3,4,2,1,0:T(8,128)(2,1)}, bf16[3,3,3,128,16]{3,4,2,1,0:T(8,128)(2,1)S(1)}, u32[]{:S(2)}, u32[]{:S(2)}) collective-permute-start(bf16[3,3,3,128,16]{3,4,2,1,0:T(8,128)(2,1)} %param.5), channel_id=1, source_target_pairs={{2,0},{3,1},{4,2},{5,3},{6,4},{7,5},{0,6},{1,7},{10,8},{11,9},{12,... | collective-permute-start | bytes 331784 | tf_op jit(solution)/shard_map/ppermute | solution.py:166
  4.9 22.5 %collective-permute-start.5 = (bf16[3,3,3,128,16]{3,4,2,1,0:T(8,128)(2,1)}, bf16[3,3,3,128,16]{3,4,2,1,0:T(8,128)(2,1)S(1)}, u32[]{:S(2)}, u32[]{:S(2)}) collective-permute-start(bf16[3,3,3,128,16]{3,4,2,1,0:T(8,128)(2,1)} %param.5), channel_id=1, source_target_pairs={{3,0},{4,1},{5,2},{6,3},{7,4},{0,5},{1,6},{2,7},{11,8},{12,9},{13,... | collective-permute-start | bytes 331784 | tf_op jit(solution)/shard_map/ppermute | solution.py:166
  5.6 25.0 %collective-permute-start.6 = (bf16[3,3,3,128,16]{3,4,2,1,0:T(8,128)(2,1)}, bf16[3,3,3,128,16]{3,4,2,1,0:T(8,128)(2,1)S(1)}, u32[]{:S(2)}, u32[]{:S(2)}) collective-permute-start(bf16[3,3,3,128,16]{3,4,2,1,0:T(8,128)(2,1)} %param.5), channel_id=1, source_target_pairs={{4,0},{5,1},{6,2},{7,3},{0,4},{1,5},{2,6},{3,7},{12,8},{13,9},{14,... | collective-permute-start | bytes 331784 | tf_op jit(solution)/shard_map/ppermute | solution.py:166
  8.0 22.6 %collective-permute-start.7 = (bf16[3,3,3,128,16]{3,4,2,1,0:T(8,128)(2,1)}, bf16[3,3,3,128,16]{3,4,2,1,0:T(8,128)(2,1)S(1)}, u32[]{:S(2)}, u32[]{:S(2)}) collective-permute-start(bf16[3,3,3,128,16]{3,4,2,1,0:T(8,128)(2,1)} %param.5), channel_id=1, source_target_pairs={{5,0},{6,1},{7,2},{0,3},{1,4},{2,5},{3,6},{4,7},{13,8},{14,9},{15,... | collective-permute-start | bytes 331784 | tf_op jit(solution)/shard_map/ppermute | solution.py:166
  25.5 28.4 %copy-start.2 = (bf16[2,64,32,128]{3,2,1,0:T(8,128)(2,1)S(1)}, bf16[2,64,32,128]{3,2,1,0:T(8,128)(2,1)}, u32[]{:S(2)}) copy-start(bf16[2,64,32,128]{3,2,1,0:T(8,128)(2,1)} %param.4) | copy-start | bytes 3145732
  25.5 6.3 %collective-permute-start.8 = (bf16[3,3,3,128,16]{3,4,2,1,0:T(8,128)(2,1)}, bf16[3,3,3,128,16]{3,4,2,1,0:T(8,128)(2,1)S(1)}, u32[]{:S(2)}, u32[]{:S(2)}) collective-permute-start(bf16[3,3,3,128,16]{3,4,2,1,0:T(8,128)(2,1)} %param.5), channel_id=1, source_target_pairs={{6,0},{7,1},{0,2},{1,3},{2,4},{3,5},{4,6},{5,7},{14,8},{15,9},{8,1... | collective-permute-start | bytes 331784 | tf_op jit(solution)/shard_map/ppermute | solution.py:166
  26.4 5.5 %collective-permute-start.9 = (bf16[3,3,3,128,16]{3,4,2,1,0:T(8,128)(2,1)}, bf16[3,3,3,128,16]{3,4,2,1,0:T(8,128)(2,1)S(1)}, u32[]{:S(2)}, u32[]{:S(2)}) collective-permute-start(bf16[3,3,3,128,16]{3,4,2,1,0:T(8,128)(2,1)} %param.5), channel_id=1, source_target_pairs={{7,0},{0,1},{1,2},{2,3},{3,4},{4,5},{5,6},{6,7},{15,8},{8,9},{9,10... | collective-permute-start | bytes 331784 | tf_op jit(solution)/shard_map/ppermute | solution.py:166
  27.4 26.4 %collective-permute-start = (bf16[2,64,32,128]{3,2,1,0:T(8,128)(2,1)}, bf16[2,64,32,128]{3,2,1,0:T(8,128)(2,1)S(1)}, u32[]{:S(2)}, u32[]{:S(2)}) collective-permute-start(bf16[2,64,32,128]{3,2,1,0:T(8,128)(2,1)} %param.4), channel_id=1, source_target_pairs={{0,8},{8,16},{16,24},{24,32},{32,40},{40,48},{48,56},{56,64},{64,7... | collective-permute-start | bytes 3145736 | tf_op jit(solution)/shard_map/ppermute | solution.py:14
  55.0 8.8 %collective-permute-start.2 = (bf16[4,64,1,128]{3,2,1,0:T(2,128)(2,1)}, bf16[4,64,1,128]{3,2,1,0:T(2,128)(2,1)}, u32[]{:S(2)}, u32[]{:S(2)}) collective-permute-start(bf16[4,64,1,128]{3,2,1,0:T(2,128)(2,1)} %get-tuple-element.6), channel_id=1, source_target_pairs={{1,0},{2,1},{3,2},{4,3},{5,4},{6,5},{7,6},{9,8},{10,9},{11,10},{12... | collective-permute-start | bytes 196616 | tf_op jit(solution)/shard_map/ppermute | solution.py:27
  57.2 6.6 %collective-permute-start.1 = (bf16[4,64,1,128]{3,2,1,0:T(2,128)(2,1)}, bf16[4,64,1,128]{3,2,1,0:T(2,128)(2,1)}, u32[]{:S(2)}, u32[]{:S(2)}) collective-permute-start(bf16[4,64,1,128]{3,2,1,0:T(2,128)(2,1)} %get-tuple-element.5), channel_id=1, source_target_pairs={{0,1},{1,2},{2,3},{3,4},{4,5},{5,6},{6,7},{8,9},{9,10},{10,11},{11... | collective-permute-start | bytes 196616 | tf_op jit(solution)/shard_map/ppermute | solution.py:25
  60.6 0.9 copy-start.1
  71.1 25.4 %copy-start.3 = (bf16[3,128,16]{1,2,0:T(8,128)(2,1)S(1)}, bf16[3,128,16]{1,2,0:T(8,128)(2,1)}, u32[]{:S(2)}) copy-start(bf16[3,128,16]{1,2,0:T(8,128)(2,1)} %param.6) | copy-start | bytes 36868
  83.7 30.1 %all-to-all-start = ((bf16[1,64,32,128]{3,2,0,1:T(8,128)(2,1)}), bf16[1,64,32,128]{3,2,0,1:T(8,128)(2,1)S(1)}, u32[]{:S(2)}, u32[]{:S(2)}) async-start(bf16[1,64,32,128]{3,2,0,1:T(8,128)(2,1)} %bitcast.104), calls=%async_computation | async-start | bytes 1048576 | tf_op jit(solution)/shard_map/all_to_all | solution.py:181
  134.1 1.4 %copy-start.4 = (f32[1,192]{1,0:T(1,128)S(1)}, f32[1,192]{1,0:T(1,128)}, u32[]{:S(2)}) copy-start(f32[1,192]{1,0:T(1,128)} %shard_map.60) | copy-start | bytes 2308

commit v8 on v6

--- a/solution.py
+++ b/solution.py
@@ -159,13 +159,78 @@
     )(shifted, weights)
 
 
+def prologue_kernel(x_ref, w_ref, m_ref, halo_ref, wall_ref, mall_ref, sends, recvs, wsends, wrecvs, msends, mrecvs, lsems):
+    count, groups = lax.axis_size("tm"), lax.axis_size("fsdp")
+    t, f = lax.axis_index("tm"), lax.axis_index("fsdp")
+    t_next, t_prev = lax.rem(t + 1, count), lax.rem(t + count - 1, count)
+    peers = [(t_next, f), (t_prev, f)] + [(t, lax.rem(f + k, groups)) for k in range(1, groups)]
+    barrier = pltpu.get_barrier_semaphore()
+    for dev in peers:
+        pl.semaphore_signal(barrier, inc=1, device_id=dev, device_id_type=MESH)
+    pl.semaphore_wait(barrier, len(peers))
+    copies = [
+        pltpu.make_async_remote_copy(
+            src_ref=x_ref, dst_ref=halo_ref, send_sem=sends.at[0], recv_sem=recvs.at[0],
+            device_id=(t_next, f), device_id_type=MESH,
+        )
+    ]
+    copies[0].start()
+    locals_ = [
+        pltpu.make_async_copy(w_ref, wall_ref.at[f], lsems.at[0]),
+        pltpu.make_async_copy(m_ref, mall_ref.at[f], lsems.at[1]),
+    ]
+    for copy in locals_:
+        copy.start()
+    for k in range(1, groups):
+        dev = (t, lax.rem(f + k, groups))
+        for src, dst, ss, rs in ((w_ref, wall_ref, wsends, wrecvs), (m_ref, mall_ref, msends, mrecvs)):
+            copy = pltpu.make_async_remote_copy(
+                src_ref=src, dst_ref=dst.at[f], send_sem=ss.at[k], recv_sem=rs.at[k],
+                device_id=dev, device_id_type=MESH,
+            )
+            copy.start()
+            copies.append(copy)
+    for copy in locals_:
+        copy.wait()
+    for copy in copies:
+        copy.wait()
+
+
+def prologue(frames, conv_shard, mix_shard):
+    groups = lax.axis_size("fsdp")
+    vmem = pl.BlockSpec(memory_space=pltpu.VMEM)
+    return pl.pallas_call(
+        prologue_kernel,
+        out_shape=(
+            jax.ShapeDtypeStruct(frames.shape, frames.dtype),
+            jax.ShapeDtypeStruct((groups,) + conv_shard.shape, conv_shard.dtype),
+            jax.ShapeDtypeStruct((groups,) + mix_shard.shape, mix_shard.dtype),
+        ),
+        in_specs=[vmem] * 3,
+        out_specs=(vmem,) * 3,
+        scratch_shapes=[
+            pltpu.SemaphoreType.DMA((1,)),
+            pltpu.SemaphoreType.DMA((1,)),
+            pltpu.SemaphoreType.DMA((groups,)),
+            pltpu.SemaphoreType.DMA((groups,)),
+            pltpu.SemaphoreType.DMA((groups,)),
+            pltpu.SemaphoreType.DMA((groups,)),
+            pltpu.SemaphoreType.DMA((2,)),
+        ],
+        compiler_params=pltpu.CompilerParams(collective_id=2, has_side_effects=True),
+    )(frames, conv_shard, mix_shard)
+
+
 def local(frames, conv_weight, mix_weight, cotangent):
-    full_conv, full_mix = (
-        lax.all_gather(conv_weight, "fsdp", axis=4, tiled=True),
-        lax.all_gather(mix_weight, "fsdp", axis=2, tiled=True),
-    )
+    t = lax.axis_index("tm")
     count_frames, height, width, channels = frames.shape
-    previous = from_behind(frames, "tm", 1)
+    part = conv_weight.shape[-1]
+    conv_shard = jnp.swapaxes(conv_weight, 3, 4).reshape(-1, part, channels)
+    mix_shard = jnp.swapaxes(mix_weight, 1, 2)
+    previous, wall, mall = prologue(frames, conv_shard, mix_shard)
+    full_conv = jnp.transpose(wall, (1, 3, 0, 2)).reshape(conv_weight.shape[:-1] + (-1,))
+    full_mix = jnp.transpose(mall, (1, 3, 0, 2)).reshape(mix_weight.shape[:-1] + (-1,))
+    previous = jnp.where(t > 0, previous, jnp.zeros((), previous.dtype))
     timed = jnp.concatenate([previous, frames], axis=0)
     padded = with_halo(timed, (("fsdp", 2),), 1)
     padded = jnp.pad(padded, ((0, 0), (1, 1), (0, 0), (0, 0)))

time: 123 us -> 116 us (0.943)
  Pallas kernels: 30.9 us -> 70.5 us
  blocking collectives: 27.4 us -> 0 us
  starting transfers between devices: 23.5 us -> 9.81 us
  waiting for transfers between devices: 25.7 us -> 18.7 us
  other arithmetic: 5.77 us -> 7.43 us
    pallas_call x0 -> x1, Pallas kernels: none -> 38.6 us  [prologue(): pl.pallas_call(prologue_kernel, out_shape=(jax.ShapeDtypeStruct(frames.sh...]
    all_gather x2 -> x0, blocking collectives: 27.4 us -> none  [the longest x1 14.4 us: local(): lax.all_gather(conv_weight, 'fsdp', axis=4, tiled=True)]
    ppermute x1 -> x0, waiting for transfers between devices: 22.1 us -> none  [from_behind(): return lax.ppermute(block, axis, route)]
    all_to_all x1, waiting for transfers between devices: 3.69 us -> 15.8 us  [local(): lax.all_to_all(pooled, 'tm', split_axis=1, concat_axis=0, tiled=True)]
    all_to_all x1, starting transfers between devices: 12.8 us -> 4.84 us  [local(): lax.all_to_all(pooled, 'tm', split_axis=1, concat_axis=0, tiled=True)]
    ppermute x1 -> x0, starting transfers between devices: 4.14 us -> none  [from_behind(): return lax.ppermute(block, axis, route)]
    ppermute x1, waiting for transfers between devices: 0.01 us -> 2.91 us  [with_halo(): lax.ppermute(head, axis, [((i + 1) % count, i) for i in range(ends)])]
    ppermute x1, starting transfers between devices: 4.63 us -> 3.05 us  [with_halo(): lax.ppermute(tail, axis, [(i, (i + 1) % count) for i in range(ends)])]
  transfers between devices with their start and end apart: 4 -> 3, of which waited for: 2 -> 2; matrix products, arithmetic and copies ran while one was open for 1% -> 2% of each run, Pallas kernels for 0% -> 0%
where the time goes in v8:
time: 116 us; the launch traced here: 115 us
  Pallas kernels  70.5 us (61%)
  waiting for transfers between devices  18.7 us (16%)
  starting transfers between devices  9.81 us (8%)
  other arithmetic  7.43 us (6%)
  local copies, waits for them, and re-layouts  5.25 us (5%)
  matrix products  2.7 us (2%)
    pallas_call x1, Pallas kernels, prologue(): pl.pallas_call(prologue_kernel, out_shape=(jax.ShapeDtypeStruct(frames.sh...  38.6 us
    pallas_call x1, Pallas kernels, scatter_sum(): pl.pallas_call(scatter_kernel, out_shape=jax.ShapeDtypeStruct((1, piece),...  19.3 us
    all_to_all x1, waiting for transfers between devices, local(): lax.all_to_all(pooled, 'tm', split_axis=1, concat_axis=0, tiled=True)  15.8 us
    pallas_call x1, Pallas kernels, conv_pool(): pl.pallas_call(conv_pool_kernel, out_shape=jax.ShapeDtypeStruct((height,...  12.7 us
    all_to_all x1, starting transfers between devices, local(): lax.all_to_all(pooled, 'tm', split_axis=1, concat_axis=0, tiled=True)  4.84 us
    concatenate x1, other arithmetic, with_halo(): jnp.concatenate([lax.ppermute(tail, axis, [(i, (i + 1) % count) for i in...  3.23 us
    another operation x1, other arithmetic, local(): shifted = jnp.stack([padded[:, :, c:c + width] for c in range(3)])  3.2 us
    ppermute x1, starting transfers between devices, with_halo(): lax.ppermute(tail, axis, [(i, (i + 1) % count) for i in range(ends)])  3.05 us
  transfers between devices with their start and end apart: 3, of which 2 were waited for; matrix products, arithmetic and copies ran while one was open for 2% of the time, Pallas kernels for 0%

profile of v8, /device:TPU:1, one launch (start us, length us, event | category | flops | bytes accessed | tf_op | source)
XLA Modules:
  0.0 115.3 jit_solution(4289515030100145753)
XLA Ops:
  0.6 0.0 copy-start
  0.6 0.0 copy-start.1
  0.7 38.6 %shard_map.59 = (bf16[2,64,32,128]{3,2,1,0:T(8,128)(2,1)}, bf16[8,27,16,128]{3,2,1,0:T(8,128)(2,1)}, bf16[8,3,16,128]{3,2,1,0:T(8,128)(2,1)}) custom-call(bf16[2,64,32,128]{3,2,1,0:T(8,128)(2,1)} %x_ref.1, bf16[27,16,128]{2,1,0:T(8,128)(2,1)} %bitcast.75, bf16[3,16,128]{2,1,0:T(8,128)(2,1)} %bitcast.77), custom_call_target="tpu_custom_call" | custom-call | tf_op jit(solution)/shard_map/pallas_call | solution.py:202
  39.2 0.0 copy-start.2
  39.3 0.1 broadcast_select_fusion
  39.4 0.0 copy-done.1
  39.4 0.9 pad_maximum_fusion.3
  40.3 3.1 %collective-permute-start = (bf16[4,64,1,128]{3,2,1,0:T(2,128)(2,1)}, bf16[4,64,1,128]{3,2,1,0:T(2,128)(2,1)}, u32[]{:S(2)}, u32[]{:S(2)}) collective-permute-start(bf16[4,64,1,128]{3,2,1,0:T(2,128)(2,1)} %get-tuple-element.11), channel_id=1, source_target_pairs={{0,1},{1,2},{2,3},{3,4},{4,5},{5,6},{6,7},{8,9},{9,10},{10,11},{11... | collective-permute-start | bytes 196616 | tf_op jit(solution)/shard_map/ppermute | solution.py:25
  43.3 1.9 %collective-permute-start.1 = (bf16[4,64,1,128]{3,2,1,0:T(2,128)(2,1)}, bf16[4,64,1,128]{3,2,1,0:T(2,128)(2,1)}, u32[]{:S(2)}, u32[]{:S(2)}) collective-permute-start(bf16[4,64,1,128]{3,2,1,0:T(2,128)(2,1)} %get-tuple-element.12), channel_id=1, source_target_pairs={{1,0},{2,1},{3,2},{4,3},{5,4},{6,5},{7,6},{9,8},{10,9},{11,10},{12... | collective-permute-start | bytes 196616 | tf_op jit(solution)/shard_map/ppermute | solution.py:27
  45.3 0.0 copy-done.2
  45.3 0.2 copy.9
  45.5 1.5 %copy.10 = bf16[3,3,3,128,128]{4,3,2,1,0:T(8,128)(2,1)} copy(bf16[3,3,3,128,128]{3,4,1,0,2:T(8,128)(2,1)S(1)} %bitcast.64) | data formatting | bytes 1769472 | tf_op jit(solution)/shard_map/transpose | solution.py:238
  47.0 0.0 collective-permute-done
  47.0 2.9 %collective-permute-done.1 = bf16[4,64,1,128]{3,2,1,0:T(2,128)(2,1)} collective-permute-done((bf16[4,64,1,128]{3,2,1,0:T(2,128)(2,1)}, bf16[4,64,1,128]{3,2,1,0:T(2,128)(2,1)}, u32[]{:S(2)}, u32[]{:S(2)}) %collective-permute-start.1) | collective-permute-done | bytes 65568 | tf_op jit(solution)/shard_map/ppermute | solution.py:27
  49.9 3.2 %select_maximum_fusion = bf16[4,66,34,128]{3,2,1,0:T(8,128)(2,1)S(1)} fusion(bf16[4,64,1,128]{3,2,1,0:T(2,128)(2,1)} %collective-permute-done.1, bf16[4,64,1,128]{3,2,1,0:T(2,128)(2,1)} %collective-permute-done, bf16[2,64,32,128]{3,2,1,0:T(8,128)(2,1)S(1)} %copy-done.1, bf16[2,64,32,128]{3,2,1,0:T(8,128)(2,1)S(1)} %broadcast_select_fusion), kind=kLoop, calls=%fused_computation.4 | loop fusion | flops 17233920 | bytes 4526080 | tf_op jit(solution)/shard_map/concatenate | solution.py:23
  53.2 1.6 %slice_bitcast_fusion.2 = (bf16[1,4,66,32,128]{4,3,2,1,0:T(8,128)(2,1)S(1)}, bf16[1,4,66,32,128]{4,3,2,1,0:T(8,128)(2,1)S(1)}, bf16[1,4,66,32,128]{4,3,2,1,0:T(8,128)(2,1)S(1)}) fusion(bf16[4,66,34,128]{3,2,1,0:T(8,128)(2,1)S(1)} %select_maximum_fusion), kind=kLoop, calls=%fused_computation.15 | loop fusion | bytes 12976128 | tf_op jit(solution)/shard_map/stack | solution.py:237
  54.8 3.2 %pad_maximum_fusion.xs_ref = bf16[3,4,66,32,128]{4,3,2,1,0:T(8,128)(2,1)} fusion(bf16[1,4,66,32,128]{4,3,2,1,0:T(8,128)(2,1)S(1)} %get-tuple-element.10, bf16[1,4,66,32,128]{4,3,2,1,0:T(8,128)(2,1)S(1)} %get-tuple-element.9, bf16[1,4,66,32,128]{4,3,2,1,0:T(8,128)(2,1)S(1)} %get-tuple-element.8), kind=kLoop, calls=%fused_computation.2 | loop fusion | flops 6488064 | bytes 12976128 | tf_op jit(solution)/shard_map/stack | solution.py:237
  58.0 0.0 copy-start.3
  58.0 12.7 %shard_map.60 = bf16[64,32,128]{2,1,0:T(8,128)(2,1)} custom-call(bf16[3,4,66,32,128]{4,3,2,1,0:T(8,128)(2,1)} %pad_maximum_fusion.xs_ref, bf16[9,384,128]{2,1,0:T(8,128)(2,1)} %bitcast.68), custom_call_target="tpu_custom_call" | custom-call | flops 3623878656 | bytes 7897088 | tf_op jit(solution)/shard_map/pallas_call | solution.py:149
  70.6 4.8 %all-to-all-start = ((bf16[1,64,32,128]{3,2,0,1:T(8,128)(2,1)}), bf16[1,64,32,128]{3,2,0,1:T(8,128)(2,1)S(1)}, u32[]{:S(2)}, u32[]{:S(2)}) async-start(bf16[1,64,32,128]{3,2,0,1:T(8,128)(2,1)} %bitcast.70), calls=%async_computation | async-start | bytes 1048576 | tf_op jit(solution)/shard_map/all_to_all | solution.py:240
  75.5 0.0 copy-done.3
  75.5 15.8 %all-to-all-done = bf16[1,64,32,128]{3,2,0,1:T(8,128)(2,1)S(1)} async-done(((bf16[1,64,32,128]{3,2,0,1:T(8,128)(2,1)}), bf16[1,64,32,128]{3,2,0,1:T(8,128)(2,1)S(1)}, u32[]{:S(2)}, u32[]{:S(2)}) %all-to-all-start) | async-done | bytes 524320 | tf_op jit(solution)/shard_map/all_to_all | solution.py:240
  91.3 0.0 copy-done
  91.3 0.3 convolution_bitcast_fusion.1
  91.7 0.3 convolution_bitcast_fusion
  92.0 0.2 pad_slice_fusion
  92.3 0.3 convolution_bitcast_fusion.2
  92.7 0.1 reshape_reshape.3
  92.8 1.0 copy.16
  93.7 19.3 %shard_map.61 = f32[1,192]{1,0:T(1,128)} custom-call(f32[8,32,1,192]{3,2,1,0:T(1,128)} %bitcast.67), custom_call_target="tpu_custom_call" | custom-call | tf_op jit(solution)/shard_map/pallas_call | solution.py:100
  113.0 0.3 convolution_add_fusion.2
  113.3 0.0 copy-start.4
  113.3 0.3 convolution_add_fusion.1
  113.6 1.1 fusion.4
  114.7 0.0 copy-done.4
  114.7 0.6 copy.18
  (2 shorter events, 0.0 us)
Async XLA Ops:
  0.6 90.7 %copy-start = (bf16[32,2,32,128]{3,2,1,0:T(8,128)(2,1)S(1)}, bf16[32,2,32,128]{3,2,1,0:T(8,128)(2,1)}, u32[]{:S(2)}) copy-start(bf16[32,2,32,128]{3,2,1,0:T(8,128)(2,1)} %param.7) | copy-start | bytes 1572868
  0.6 38.7 %copy-start.1 = (bf16[2,64,32,128]{3,2,1,0:T(8,128)(2,1)S(1)}, bf16[2,64,32,128]{3,2,1,0:T(8,128)(2,1)}, u32[]{:S(2)}) copy-start(bf16[2,64,32,128]{3,2,1,0:T(8,128)(2,1)} %x_ref.1) | copy-start | bytes 3145732
  39.2 6.0 %copy-start.2 = (bf16[8,27,16,128]{3,2,1,0:T(8,128)(2,1)S(1)}, bf16[8,27,16,128]{3,2,1,0:T(8,128)(2,1)}, u32[]{:S(2)}) copy-start(bf16[8,27,16,128]{3,2,1,0:T(8,128)(2,1)} %get-tuple-element.6) | copy-start | bytes 2654212
  40.3 6.8 %collective-permute-start = (bf16[4,64,1,128]{3,2,1,0:T(2,128)(2,1)}, bf16[4,64,1,128]{3,2,1,0:T(2,128)(2,1)}, u32[]{:S(2)}, u32[]{:S(2)}) collective-permute-start(bf16[4,64,1,128]{3,2,1,0:T(2,128)(2,1)} %get-tuple-element.11), channel_id=1, source_target_pairs={{0,1},{1,2},{2,3},{3,4},{4,5},{5,6},{6,7},{8,9},{9,10},{10,11},{11... | collective-permute-start | bytes 196616 | tf_op jit(solution)/shard_map/ppermute | solution.py:25
  43.3 6.6 %collective-permute-start.1 = (bf16[4,64,1,128]{3,2,1,0:T(2,128)(2,1)}, bf16[4,64,1,128]{3,2,1,0:T(2,128)(2,1)}, u32[]{:S(2)}, u32[]{:S(2)}) collective-permute-start(bf16[4,64,1,128]{3,2,1,0:T(2,128)(2,1)} %get-tuple-element.12), channel_id=1, source_target_pairs={{1,0},{2,1},{3,2},{4,3},{5,4},{6,5},{7,6},{9,8},{10,9},{11,10},{12... | collective-permute-start | bytes 196616 | tf_op jit(solution)/shard_map/ppermute | solution.py:27
  58.0 17.5 %copy-start.3 = (bf16[8,3,16,128]{3,2,1,0:T(8,128)(2,1)S(1)}, bf16[8,3,16,128]{3,2,1,0:T(8,128)(2,1)}, u32[]{:S(2)}) copy-start(bf16[8,3,16,128]{3,2,1,0:T(8,128)(2,1)} %get-tuple-element.7) | copy-start | bytes 294916
  70.6 20.7 %all-to-all-start = ((bf16[1,64,32,128]{3,2,0,1:T(8,128)(2,1)}), bf16[1,64,32,128]{3,2,0,1:T(8,128)(2,1)S(1)}, u32[]{:S(2)}, u32[]{:S(2)}) async-start(bf16[1,64,32,128]{3,2,0,1:T(8,128)(2,1)} %bitcast.70), calls=%async_computation | async-start | bytes 1048576 | tf_op jit(solution)/shard_map/all_to_all | solution.py:240
  113.3 1.4 %copy-start.4 = (f32[1,192]{1,0:T(1,128)S(1)}, f32[1,192]{1,0:T(1,128)}, u32[]{:S(2)}) copy-start(f32[1,192]{1,0:T(1,128)} %shard_map.61) | copy-start | bytes 2308

commit v9 on v8

--- a/solution.py
+++ b/solution.py
@@ -168,13 +168,24 @@
     for dev in peers:
         pl.semaphore_signal(barrier, inc=1, device_id=dev, device_id_type=MESH)
     pl.semaphore_wait(barrier, len(peers))
-    copies = [
+    pieces = sends.shape[0]
+    rows = x_ref.shape[1] // pieces
+    halo = [
         pltpu.make_async_remote_copy(
-            src_ref=x_ref, dst_ref=halo_ref, send_sem=sends.at[0], recv_sem=recvs.at[0],
+            src_ref=x_ref.at[:, pl.ds(i * rows, rows)],
+            dst_ref=halo_ref.at[:, pl.ds(i * rows, rows)],
+            send_sem=sends.at[i], recv_sem=recvs.at[i],
             device_id=(t_next, f), device_id_type=MESH,
         )
+        for i in range(pieces)
     ]
-    copies[0].start()
+
+    @pl.when(t < count - 1)
+    def _():
+        for copy in halo:
+            copy.start()
+
+    copies = []
     locals_ = [
         pltpu.make_async_copy(w_ref, wall_ref.at[f], lsems.at[0]),
         pltpu.make_async_copy(m_ref, mall_ref.at[f], lsems.at[1]),
@@ -195,6 +206,16 @@
     for copy in copies:
         copy.wait()
 
+    @pl.when(t < count - 1)
+    def _():
+        for copy in halo:
+            copy.wait_send()
+
+    @pl.when(t > 0)
+    def _():
+        for copy in halo:
+            copy.wait_recv()
+
 
 def prologue(frames, conv_shard, mix_shard):
     groups = lax.axis_size("fsdp")
@@ -209,8 +230,8 @@
         in_specs=[vmem] * 3,
         out_specs=(vmem,) * 3,
         scratch_shapes=[
-            pltpu.SemaphoreType.DMA((1,)),
-            pltpu.SemaphoreType.DMA((1,)),
+            pltpu.SemaphoreType.DMA((4,)),
+            pltpu.SemaphoreType.DMA((4,)),
             pltpu.SemaphoreType.DMA((groups,)),
             pltpu.SemaphoreType.DMA((groups,)),
             pltpu.SemaphoreType.DMA((groups,)),

time: 116 us -> 116 us (level)
  Pallas kernels: 70.5 us -> 65.6 us
  starting transfers between devices: 9.81 us -> 14.7 us
    pallas_call x1, Pallas kernels: 38.6 us -> 33.7 us  [prologue(): pl.pallas_call(prologue_kernel, out_shape=(jax.ShapeDtypeStruct(frames.sh...]
    all_to_all x1, starting transfers between devices: 4.84 us -> 8.18 us  [local(): lax.all_to_all(pooled, 'tm', split_axis=1, concat_axis=0, tiled=True)]
    ppermute x1, starting transfers between devices: 3.05 us -> 4.63 us  [with_halo(): lax.ppermute(tail, axis, [(i, (i + 1) % count) for i in range(ends)])]
where the time goes in v9:
time: 116 us; the launch traced here: 115 us
  Pallas kernels  65.6 us (57%)
  waiting for transfers between devices  18.7 us (16%)
  starting transfers between devices  14.7 us (13%)
  other arithmetic  7.43 us (6%)
  local copies, waits for them, and re-layouts  5.25 us (5%)
  matrix products  2.7 us (2%)
    pallas_call x1, Pallas kernels, prologue(): pl.pallas_call(prologue_kernel, out_shape=(jax.ShapeDtypeStruct(frames.sh...  33.7 us
    pallas_call x1, Pallas kernels, scatter_sum(): pl.pallas_call(scatter_kernel, out_shape=jax.ShapeDtypeStruct((1, piece),...  19.3 us
    all_to_all x1, waiting for transfers between devices, local(): lax.all_to_all(pooled, 'tm', split_axis=1, concat_axis=0, tiled=True)  15.8 us
    pallas_call x1, Pallas kernels, conv_pool(): pl.pallas_call(conv_pool_kernel, out_shape=jax.ShapeDtypeStruct((height,...  12.7 us
    all_to_all x1, starting transfers between devices, local(): lax.all_to_all(pooled, 'tm', split_axis=1, concat_axis=0, tiled=True)  8.18 us
    ppermute x1, starting transfers between devices, with_halo(): lax.ppermute(tail, axis, [(i, (i + 1) % count) for i in range(ends)])  4.63 us
    concatenate x1, other arithmetic, with_halo(): jnp.concatenate([lax.ppermute(tail, axis, [(i, (i + 1) % count) for i in...  3.23 us
    another operation x1, other arithmetic, local(): shifted = jnp.stack([padded[:, :, c:c + width] for c in range(3)])  3.2 us
  transfers between devices with their start and end apart: 3, of which 2 were waited for; matrix products, arithmetic and copies ran while one was open for 2% of the time, Pallas kernels for 0%

profile of v9, /device:TPU:1, one launch (start us, length us, event | category | flops | bytes accessed | tf_op | source)
XLA Modules:
  0.0 115.3 jit_solution(11613619006615436284)
XLA Ops:
  0.6 0.0 copy-start
  0.6 0.0 copy-start.1
  0.7 33.7 %shard_map.59 = (bf16[2,64,32,128]{3,2,1,0:T(8,128)(2,1)}, bf16[8,27,16,128]{3,2,1,0:T(8,128)(2,1)}, bf16[8,3,16,128]{3,2,1,0:T(8,128)(2,1)}) custom-call(bf16[2,64,32,128]{3,2,1,0:T(8,128)(2,1)} %x_ref.1, bf16[27,16,128]{2,1,0:T(8,128)(2,1)} %bitcast.75, bf16[3,16,128]{2,1,0:T(8,128)(2,1)} %bitcast.77), custom_call_target="tpu_custom_call" | custom-call | tf_op jit(solution)/shard_map/pallas_call | solution.py:223
  34.3 0.0 copy-start.2
  34.3 0.1 broadcast_select_fusion
  34.4 0.0 copy-done.1
  34.5 0.9 pad_maximum_fusion.3
  35.4 4.6 %collective-permute-start = (bf16[4,64,1,128]{3,2,1,0:T(2,128)(2,1)}, bf16[4,64,1,128]{3,2,1,0:T(2,128)(2,1)}, u32[]{:S(2)}, u32[]{:S(2)}) collective-permute-start(bf16[4,64,1,128]{3,2,1,0:T(2,128)(2,1)} %get-tuple-element.11), channel_id=1, source_target_pairs={{0,1},{1,2},{2,3},{3,4},{4,5},{5,6},{6,7},{8,9},{9,10},{10,11},{11... | collective-permute-start | bytes 196616 | tf_op jit(solution)/shard_map/ppermute | solution.py:25
  40.0 1.9 %collective-permute-start.1 = (bf16[4,64,1,128]{3,2,1,0:T(2,128)(2,1)}, bf16[4,64,1,128]{3,2,1,0:T(2,128)(2,1)}, u32[]{:S(2)}, u32[]{:S(2)}) collective-permute-start(bf16[4,64,1,128]{3,2,1,0:T(2,128)(2,1)} %get-tuple-element.12), channel_id=1, source_target_pairs={{1,0},{2,1},{3,2},{4,3},{5,4},{6,5},{7,6},{9,8},{10,9},{11,10},{12... | collective-permute-start | bytes 196616 | tf_op jit(solution)/shard_map/ppermute | solution.py:27
  41.9 0.0 copy-done.2
  41.9 0.2 copy.9
  42.2 1.5 %copy.10 = bf16[3,3,3,128,128]{4,3,2,1,0:T(8,128)(2,1)} copy(bf16[3,3,3,128,128]{3,4,1,0,2:T(8,128)(2,1)S(1)} %bitcast.64) | data formatting | bytes 1769472 | tf_op jit(solution)/shard_map/transpose | solution.py:259
  43.7 0.0 collective-permute-done
  43.7 2.9 %collective-permute-done.1 = bf16[4,64,1,128]{3,2,1,0:T(2,128)(2,1)} collective-permute-done((bf16[4,64,1,128]{3,2,1,0:T(2,128)(2,1)}, bf16[4,64,1,128]{3,2,1,0:T(2,128)(2,1)}, u32[]{:S(2)}, u32[]{:S(2)}) %collective-permute-start.1) | collective-permute-done | bytes 65568 | tf_op jit(solution)/shard_map/ppermute | solution.py:27
  46.6 3.2 %select_maximum_fusion = bf16[4,66,34,128]{3,2,1,0:T(8,128)(2,1)S(1)} fusion(bf16[4,64,1,128]{3,2,1,0:T(2,128)(2,1)} %collective-permute-done.1, bf16[4,64,1,128]{3,2,1,0:T(2,128)(2,1)} %collective-permute-done, bf16[2,64,32,128]{3,2,1,0:T(8,128)(2,1)S(1)} %copy-done.1, bf16[2,64,32,128]{3,2,1,0:T(8,128)(2,1)S(1)} %broadcast_select_fusion), kind=kLoop, calls=%fused_computation.4 | loop fusion | flops 17233920 | bytes 4526080 | tf_op jit(solution)/shard_map/concatenate | solution.py:23
  49.8 1.6 %slice_bitcast_fusion.2 = (bf16[1,4,66,32,128]{4,3,2,1,0:T(8,128)(2,1)S(1)}, bf16[1,4,66,32,128]{4,3,2,1,0:T(8,128)(2,1)S(1)}, bf16[1,4,66,32,128]{4,3,2,1,0:T(8,128)(2,1)S(1)}) fusion(bf16[4,66,34,128]{3,2,1,0:T(8,128)(2,1)S(1)} %select_maximum_fusion), kind=kLoop, calls=%fused_computation.15 | loop fusion | bytes 12976128 | tf_op jit(solution)/shard_map/stack | solution.py:258
  51.4 3.2 %pad_maximum_fusion.xs_ref = bf16[3,4,66,32,128]{4,3,2,1,0:T(8,128)(2,1)} fusion(bf16[1,4,66,32,128]{4,3,2,1,0:T(8,128)(2,1)S(1)} %get-tuple-element.10, bf16[1,4,66,32,128]{4,3,2,1,0:T(8,128)(2,1)S(1)} %get-tuple-element.9, bf16[1,4,66,32,128]{4,3,2,1,0:T(8,128)(2,1)S(1)} %get-tuple-element.8), kind=kLoop, calls=%fused_computation.2 | loop fusion | flops 6488064 | bytes 12976128 | tf_op jit(solution)/shard_map/stack | solution.py:258
  54.6 0.0 copy-start.3
  54.6 12.7 %shard_map.60 = bf16[64,32,128]{2,1,0:T(8,128)(2,1)} custom-call(bf16[3,4,66,32,128]{4,3,2,1,0:T(8,128)(2,1)} %pad_maximum_fusion.xs_ref, bf16[9,384,128]{2,1,0:T(8,128)(2,1)} %bitcast.68), custom_call_target="tpu_custom_call" | custom-call | flops 3623878656 | bytes 7897088 | tf_op jit(solution)/shard_map/pallas_call | solution.py:149
  67.3 8.2 %all-to-all-start = ((bf16[1,64,32,128]{3,2,0,1:T(8,128)(2,1)}), bf16[1,64,32,128]{3,2,0,1:T(8,128)(2,1)S(1)}, u32[]{:S(2)}, u32[]{:S(2)}) async-start(bf16[1,64,32,128]{3,2,0,1:T(8,128)(2,1)} %bitcast.70), calls=%async_computation | async-start | bytes 1048576 | tf_op jit(solution)/shard_map/all_to_all | solution.py:261
  75.5 0.0 copy-done.3
  75.5 15.8 %all-to-all-done = bf16[1,64,32,128]{3,2,0,1:T(8,128)(2,1)S(1)} async-done(((bf16[1,64,32,128]{3,2,0,1:T(8,128)(2,1)}), bf16[1,64,32,128]{3,2,0,1:T(8,128)(2,1)S(1)}, u32[]{:S(2)}, u32[]{:S(2)}) %all-to-all-start) | async-done | bytes 524320 | tf_op jit(solution)/shard_map/all_to_all | solution.py:261
  91.4 0.0 copy-done
  91.4 0.3 convolution_bitcast_fusion.1
  91.7 0.3 convolution_bitcast_fusion
  92.0 0.2 pad_slice_fusion
  92.3 0.3 convolution_bitcast_fusion.2
  92.7 0.1 reshape_reshape.3
  92.8 1.0 copy.16
  93.7 19.3 %shard_map.61 = f32[1,192]{1,0:T(1,128)} custom-call(f32[8,32,1,192]{3,2,1,0:T(1,128)} %bitcast.67), custom_call_target="tpu_custom_call" | custom-call | tf_op jit(solution)/shard_map/pallas_call | solution.py:100
  113.0 0.3 convolution_add_fusion.2
  113.3 0.0 copy-start.4
  113.3 0.3 convolution_add_fusion.1
  113.6 1.1 fusion.4
  114.7 0.0 copy-done.4
  114.7 0.6 copy.18
  (2 shorter events, 0.0 us)
Async XLA Ops:
  0.6 90.7 %copy-start = (bf16[32,2,32,128]{3,2,1,0:T(8,128)(2,1)S(1)}, bf16[32,2,32,128]{3,2,1,0:T(8,128)(2,1)}, u32[]{:S(2)}) copy-start(bf16[32,2,32,128]{3,2,1,0:T(8,128)(2,1)} %param.7) | copy-start | bytes 1572868
  0.6 33.8 %copy-start.1 = (bf16[2,64,32,128]{3,2,1,0:T(8,128)(2,1)S(1)}, bf16[2,64,32,128]{3,2,1,0:T(8,128)(2,1)}, u32[]{:S(2)}) copy-start(bf16[2,64,32,128]{3,2,1,0:T(8,128)(2,1)} %x_ref.1) | copy-start | bytes 3145732
  34.3 7.6 %copy-start.2 = (bf16[8,27,16,128]{3,2,1,0:T(8,128)(2,1)S(1)}, bf16[8,27,16,128]{3,2,1,0:T(8,128)(2,1)}, u32[]{:S(2)}) copy-start(bf16[8,27,16,128]{3,2,1,0:T(8,128)(2,1)} %get-tuple-element.6) | copy-start | bytes 2654212
  35.4 8.3 %collective-permute-start = (bf16[4,64,1,128]{3,2,1,0:T(2,128)(2,1)}, bf16[4,64,1,128]{3,2,1,0:T(2,128)(2,1)}, u32[]{:S(2)}, u32[]{:S(2)}) collective-permute-start(bf16[4,64,1,128]{3,2,1,0:T(2,128)(2,1)} %get-tuple-element.11), channel_id=1, source_target_pairs={{0,1},{1,2},{2,3},{3,4},{4,5},{5,6},{6,7},{8,9},{9,10},{10,11},{11... | collective-permute-start | bytes 196616 | tf_op jit(solution)/shard_map/ppermute | solution.py:25
  40.0 6.6 %collective-permute-start.1 = (bf16[4,64,1,128]{3,2,1,0:T(2,128)(2,1)}, bf16[4,64,1,128]{3,2,1,0:T(2,128)(2,1)}, u32[]{:S(2)}, u32[]{:S(2)}) collective-permute-start(bf16[4,64,1,128]{3,2,1,0:T(2,128)(2,1)} %get-tuple-element.12), channel_id=1, source_target_pairs={{1,0},{2,1},{3,2},{4,3},{5,4},{6,5},{7,6},{9,8},{10,9},{11,10},{12... | collective-permute-start | bytes 196616 | tf_op jit(solution)/shard_map/ppermute | solution.py:27
  54.6 20.9 %copy-start.3 = (bf16[8,3,16,128]{3,2,1,0:T(8,128)(2,1)S(1)}, bf16[8,3,16,128]{3,2,1,0:T(8,128)(2,1)}, u32[]{:S(2)}) copy-start(bf16[8,3,16,128]{3,2,1,0:T(8,128)(2,1)} %get-tuple-element.7) | copy-start | bytes 294916
  67.3 24.0 %all-to-all-start = ((bf16[1,64,32,128]{3,2,0,1:T(8,128)(2,1)}), bf16[1,64,32,128]{3,2,0,1:T(8,128)(2,1)S(1)}, u32[]{:S(2)}, u32[]{:S(2)}) async-start(bf16[1,64,32,128]{3,2,0,1:T(8,128)(2,1)} %bitcast.70), calls=%async_computation | async-start | bytes 1048576 | tf_op jit(solution)/shard_map/all_to_all | solution.py:261
  113.3 1.4 %copy-start.4 = (f32[1,192]{1,0:T(1,128)S(1)}, f32[1,192]{1,0:T(1,128)}, u32[]{:S(2)}) copy-start(f32[1,192]{1,0:T(1,128)} %shard_map.61) | copy-start | bytes 2308

commit v10 on v9

--- a/solution.py
+++ b/solution.py
@@ -118,9 +118,21 @@
     return out.reshape(piece)
 
 
-def conv_pool_kernel(xs_ref, w_ref, o_ref):
+def conv_pool_kernel(p_ref, w_ref, o_ref, xs_ref):
     height, width, channels = o_ref.shape
+    frames = p_ref.shape[0]
     rows = 8
+    band = 8
+
+    def shift(i, carry):
+        q, r = i // (p_ref.shape[1] // band), i % (p_ref.shape[1] // band)
+        top = pl.multiple_of(r * band, band)
+        block = p_ref[q, pl.ds(top, band)].astype(jnp.float32)
+        for c in range(3):
+            xs_ref[c, q, pl.ds(top, band)] = block[:, c : c + width].astype(xs_ref.dtype)
+        return carry
+
+    lax.fori_loop(0, frames * (p_ref.shape[1] // band), shift, 0)
 
     def body(r, carry):
         top = pl.multiple_of(r * rows, rows)
@@ -141,9 +153,9 @@
     lax.fori_loop(0, height // rows, body, 0)
 
 
-def conv_pool(shifted, weights):
-    _, _, rows, width, channels = shifted.shape
-    height = rows - 2
+def conv_pool(padded, weights):
+    frames, rows, wide, channels = padded.shape
+    height, width = rows - 8, wide - 2
     vmem = pl.BlockSpec(memory_space=pltpu.VMEM)
     flops = 2 * 2 * height * width * weights.shape[0] * weights.shape[1] * channels
     return pl.pallas_call(
@@ -151,12 +163,13 @@
         out_shape=jax.ShapeDtypeStruct((height, width, channels), jnp.bfloat16),
         in_specs=[vmem, vmem],
         out_specs=vmem,
+        scratch_shapes=[pltpu.VMEM((3, frames, rows, width, channels), padded.dtype)],
         cost_estimate=pl.CostEstimate(
             flops=flops,
             transcendentals=2 * height * width * channels,
-            bytes_accessed=shifted.size * 2 + weights.size * 2 + height * width * channels * 2,
+            bytes_accessed=padded.size * 2 + weights.size * 2 + height * width * channels * 2,
         ),
-    )(shifted, weights)
+    )(padded, weights)
 
 
 def prologue_kernel(x_ref, w_ref, m_ref, halo_ref, wall_ref, mall_ref, sends, recvs, wsends, wrecvs, msends, mrecvs, lsems):
@@ -254,10 +267,9 @@
     previous = jnp.where(t > 0, previous, jnp.zeros((), previous.dtype))
     timed = jnp.concatenate([previous, frames], axis=0)
     padded = with_halo(timed, (("fsdp", 2),), 1)
-    padded = jnp.pad(padded, ((0, 0), (1, 1), (0, 0), (0, 0)))
-    shifted = jnp.stack([padded[:, :, c : c + width] for c in range(3)])
+    padded = jnp.pad(padded, ((0, 0), (1, 7), (0, 0), (0, 0)))
     weights = jnp.transpose(full_conv, (1, 2, 0, 3, 4)).reshape(9, 3 * channels, -1)
-    pooled = conv_pool(shifted, weights)[None]
+    pooled = conv_pool(padded, weights)[None]
     pooled = lax.all_to_all(pooled, "tm", split_axis=1, concat_axis=0, tiled=True)
     branch = pooled.astype(jnp.float32).reshape(-1, channels)
     flat_cot = cotangent.reshape(-1, channels)

time: 116 us -> 114 us (0.983)
  Pallas kernels: 65.6 us -> 67.5 us
  other arithmetic: 7.43 us -> 5.82 us
  local copies, waits for them, and re-layouts: 5.25 us -> 3.66 us
    another operation x1 -> x0, other arithmetic: 3.2 us -> none  [local(): shifted = jnp.stack([padded[:, :, c:c + width] for c in range(3)])]
    pallas_call x1, Pallas kernels: 12.7 us -> 14.6 us  [conv_pool(): pl.pallas_call(conv_pool_kernel, out_shape=jax.ShapeDtypeStruct((height,...]
    concatenate x1, other arithmetic: 3.23 us -> 4.82 us  [with_halo(): jnp.concatenate([lax.ppermute(tail, axis, [(i, (i + 1) % count) for i in...]
    another operation x1 -> x0, local copies, waits for them, and re-layouts: 1.59 us -> none  [local(): shifted = jnp.stack([padded[:, :, c:c + width] for c in range(3)])]
where the time goes in v10:
time: 114 us
  Pallas kernels  67.5 us (59%)
  waiting for transfers between devices  18.8 us (16%)
  starting transfers between devices  14.7 us (13%)
  other arithmetic  5.82 us (5%)
  local copies, waits for them, and re-layouts  3.66 us (3%)
  matrix products  2.7 us (2%)
    pallas_call x1, Pallas kernels, prologue(): pl.pallas_call(prologue_kernel, out_shape=(jax.ShapeDtypeStruct(frames.sh...  33.6 us
    pallas_call x1, Pallas kernels, scatter_sum(): pl.pallas_call(scatter_kernel, out_shape=jax.ShapeDtypeStruct((1, piece),...  19.3 us
    all_to_all x1, waiting for transfers between devices, local(): lax.all_to_all(pooled, 'tm', split_axis=1, concat_axis=0, tiled=True)  15.8 us
    pallas_call x1, Pallas kernels, conv_pool(): pl.pallas_call(conv_pool_kernel, out_shape=jax.ShapeDtypeStruct((height,...  14.6 us
    all_to_all x1, starting transfers between devices, local(): lax.all_to_all(pooled, 'tm', split_axis=1, concat_axis=0, tiled=True)  8.18 us
    concatenate x1, other arithmetic, with_halo(): jnp.concatenate([lax.ppermute(tail, axis, [(i, (i + 1) % count) for i in...  4.82 us
    ppermute x1, starting transfers between devices, with_halo(): lax.ppermute(tail, axis, [(i, (i + 1) % count) for i in range(ends)])  4.63 us
    ppermute x1, waiting for transfers between devices, with_halo(): lax.ppermute(head, axis, [((i + 1) % count, i) for i in range(ends)])  2.92 us
  transfers between devices with their start and end apart: 3, of which 2 were waited for; matrix products, arithmetic and copies ran while one was open for 2% of the time, Pallas kernels for 0%

profile of v10, /device:TPU:1, one launch (start us, length us, event | category | flops | bytes accessed | tf_op | source)
XLA Modules:
  0.0 114.0 jit_solution(8453373422084251067)
XLA Ops:
  0.6 0.0 copy-start
  0.6 0.0 copy-start.1
  0.7 33.6 %shard_map.59 = (bf16[2,64,32,128]{3,2,1,0:T(8,128)(2,1)}, bf16[8,27,16,128]{3,2,1,0:T(8,128)(2,1)}, bf16[8,3,16,128]{3,2,1,0:T(8,128)(2,1)}) custom-call(bf16[2,64,32,128]{3,2,1,0:T(8,128)(2,1)} %x_ref.1, bf16[27,16,128]{2,1,0:T(8,128)(2,1)} %bitcast.69, bf16[3,16,128]{2,1,0:T(8,128)(2,1)} %bitcast.71), custom_call_target="tpu_custom_call" | custom-call | tf_op jit(solution)/shard_map/pallas_call | solution.py:236
  34.3 0.0 copy-start.2
  34.3 0.1 broadcast_select_fusion
  34.4 0.0 copy-done.1
  34.4 0.9 pad_maximum_fusion.2
  35.3 4.6 %collective-permute-start = (bf16[4,64,1,128]{3,2,1,0:T(2,128)(2,1)}, bf16[4,64,1,128]{3,2,1,0:T(2,128)(2,1)}, u32[]{:S(2)}, u32[]{:S(2)}) collective-permute-start(bf16[4,64,1,128]{3,2,1,0:T(2,128)(2,1)} %get-tuple-element.8), channel_id=1, source_target_pairs={{0,1},{1,2},{2,3},{3,4},{4,5},{5,6},{6,7},{8,9},{9,10},{10,11},{11... | collective-permute-start | bytes 196616 | tf_op jit(solution)/shard_map/ppermute | solution.py:25
  40.0 1.9 %collective-permute-start.1 = (bf16[4,64,1,128]{3,2,1,0:T(2,128)(2,1)}, bf16[4,64,1,128]{3,2,1,0:T(2,128)(2,1)}, u32[]{:S(2)}, u32[]{:S(2)}) collective-permute-start(bf16[4,64,1,128]{3,2,1,0:T(2,128)(2,1)} %get-tuple-element.9), channel_id=1, source_target_pairs={{1,0},{2,1},{3,2},{4,3},{5,4},{6,5},{7,6},{9,8},{10,9},{11,10},{12... | collective-permute-start | bytes 196616 | tf_op jit(solution)/shard_map/ppermute | solution.py:27
  41.9 0.0 copy-done.2
  41.9 0.2 copy.9
  42.1 1.5 %copy.10 = bf16[3,3,3,128,128]{4,3,2,1,0:T(8,128)(2,1)} copy(bf16[3,3,3,128,128]{3,4,1,0,2:T(8,128)(2,1)S(1)} %bitcast.58) | data formatting | bytes 1769472 | tf_op jit(solution)/shard_map/transpose | solution.py:271
  43.6 0.0 collective-permute-done
  43.6 2.9 %collective-permute-done.1 = bf16[4,64,1,128]{3,2,1,0:T(2,128)(2,1)} collective-permute-done((bf16[4,64,1,128]{3,2,1,0:T(2,128)(2,1)}, bf16[4,64,1,128]{3,2,1,0:T(2,128)(2,1)}, u32[]{:S(2)}, u32[]{:S(2)}) %collective-permute-start.1) | collective-permute-done | bytes 65568 | tf_op jit(solution)/shard_map/ppermute | solution.py:27
  46.6 4.8 %select_maximum_fusion.p_ref = bf16[4,72,34,128]{3,2,1,0:T(8,128)(2,1)} fusion(bf16[4,64,1,128]{3,2,1,0:T(2,128)(2,1)} %collective-permute-done.1, bf16[4,64,1,128]{3,2,1,0:T(2,128)(2,1)} %collective-permute-done, bf16[2,64,32,128]{3,2,1,0:T(8,128)(2,1)S(1)} %copy-done.1, bf16[2,64,32,128]{3,2,1,0:T(8,128)(2,1)S(1)} %broadcast_select_fusion), kind=kLoop, calls=%fused_computation.3 | loop fusion | flops 18800640 | bytes 4734976 | tf_op jit(solution)/shard_map/concatenate | solution.py:23
  51.4 0.0 copy-start.3
  51.4 14.6 %shard_map.60 = bf16[64,32,128]{2,1,0:T(8,128)(2,1)} custom-call(bf16[4,72,34,128]{3,2,1,0:T(8,128)(2,1)} %select_maximum_fusion.p_ref, bf16[9,384,128]{2,1,0:T(8,128)(2,1)} %bitcast.63), custom_call_target="tpu_custom_call" | custom-call | flops 3623878656 | bytes 3915776 | tf_op jit(solution)/shard_map/pallas_call | solution.py:161
  66.0 8.2 %all-to-all-start = ((bf16[1,64,32,128]{3,2,0,1:T(8,128)(2,1)}), bf16[1,64,32,128]{3,2,0,1:T(8,128)(2,1)S(1)}, u32[]{:S(2)}, u32[]{:S(2)}) async-start(bf16[1,64,32,128]{3,2,0,1:T(8,128)(2,1)} %bitcast.64), calls=%async_computation | async-start | bytes 1048576 | tf_op jit(solution)/shard_map/all_to_all | solution.py:273
  74.2 0.0 copy-done.3
  74.2 15.8 %all-to-all-done = bf16[1,64,32,128]{3,2,0,1:T(8,128)(2,1)S(1)} async-done(((bf16[1,64,32,128]{3,2,0,1:T(8,128)(2,1)}), bf16[1,64,32,128]{3,2,0,1:T(8,128)(2,1)S(1)}, u32[]{:S(2)}, u32[]{:S(2)}) %all-to-all-start) | async-done | bytes 524320 | tf_op jit(solution)/shard_map/all_to_all | solution.py:273
  90.0 0.0 copy-done
  90.0 0.3 convolution_bitcast_fusion.1
  90.4 0.3 convolution_bitcast_fusion
  90.7 0.2 pad_slice_fusion
  91.0 0.3 convolution_bitcast_fusion.2
  91.3 0.1 reshape_reshape.3
  91.4 1.0 copy.16
  92.4 19.3 %shard_map.61 = f32[1,192]{1,0:T(1,128)} custom-call(f32[8,32,1,192]{3,2,1,0:T(1,128)} %bitcast.61), custom_call_target="tpu_custom_call" | custom-call | tf_op jit(solution)/shard_map/pallas_call | solution.py:100
  111.7 0.0 copy-start.4
  111.7 0.3 convolution_add_fusion.2
  112.0 0.3 convolution_add_fusion.1
  112.3 1.1 fusion.4
  113.4 0.0 copy-done.4
  113.4 0.6 copy.18
  (2 shorter events, 0.0 us)
Async XLA Ops:
  0.6 89.4 %copy-start = (bf16[32,2,32,128]{3,2,1,0:T(8,128)(2,1)S(1)}, bf16[32,2,32,128]{3,2,1,0:T(8,128)(2,1)}, u32[]{:S(2)}) copy-start(bf16[32,2,32,128]{3,2,1,0:T(8,128)(2,1)} %param.7) | copy-start | bytes 1572868
  0.6 33.8 %copy-start.1 = (bf16[2,64,32,128]{3,2,1,0:T(8,128)(2,1)S(1)}, bf16[2,64,32,128]{3,2,1,0:T(8,128)(2,1)}, u32[]{:S(2)}) copy-start(bf16[2,64,32,128]{3,2,1,0:T(8,128)(2,1)} %x_ref.1) | copy-start | bytes 3145732
  34.3 7.6 %copy-start.2 = (bf16[8,27,16,128]{3,2,1,0:T(8,128)(2,1)S(1)}, bf16[8,27,16,128]{3,2,1,0:T(8,128)(2,1)}, u32[]{:S(2)}) copy-start(bf16[8,27,16,128]{3,2,1,0:T(8,128)(2,1)} %get-tuple-element.6) | copy-start | bytes 2654212
  35.3 8.3 %collective-permute-start = (bf16[4,64,1,128]{3,2,1,0:T(2,128)(2,1)}, bf16[4,64,1,128]{3,2,1,0:T(2,128)(2,1)}, u32[]{:S(2)}, u32[]{:S(2)}) collective-permute-start(bf16[4,64,1,128]{3,2,1,0:T(2,128)(2,1)} %get-tuple-element.8), channel_id=1, source_target_pairs={{0,1},{1,2},{2,3},{3,4},{4,5},{5,6},{6,7},{8,9},{9,10},{10,11},{11... | collective-permute-start | bytes 196616 | tf_op jit(solution)/shard_map/ppermute | solution.py:25
  40.0 6.6 %collective-permute-start.1 = (bf16[4,64,1,128]{3,2,1,0:T(2,128)(2,1)}, bf16[4,64,1,128]{3,2,1,0:T(2,128)(2,1)}, u32[]{:S(2)}, u32[]{:S(2)}) collective-permute-start(bf16[4,64,1,128]{3,2,1,0:T(2,128)(2,1)} %get-tuple-element.9), channel_id=1, source_target_pairs={{1,0},{2,1},{3,2},{4,3},{5,4},{6,5},{7,6},{9,8},{10,9},{11,10},{12... | collective-permute-start | bytes 196616 | tf_op jit(solution)/shard_map/ppermute | solution.py:27
  51.4 22.8 %copy-start.3 = (bf16[8,3,16,128]{3,2,1,0:T(8,128)(2,1)S(1)}, bf16[8,3,16,128]{3,2,1,0:T(8,128)(2,1)}, u32[]{:S(2)}) copy-start(bf16[8,3,16,128]{3,2,1,0:T(8,128)(2,1)} %get-tuple-element.7) | copy-start | bytes 294916
  66.0 24.0 %all-to-all-start = ((bf16[1,64,32,128]{3,2,0,1:T(8,128)(2,1)}), bf16[1,64,32,128]{3,2,0,1:T(8,128)(2,1)S(1)}, u32[]{:S(2)}, u32[]{:S(2)}) async-start(bf16[1,64,32,128]{3,2,0,1:T(8,128)(2,1)} %bitcast.64), calls=%async_computation | async-start | bytes 1048576 | tf_op jit(solution)/shard_map/all_to_all | solution.py:273
  111.7 1.7 %copy-start.4 = (f32[1,192]{1,0:T(1,128)S(1)}, f32[1,192]{1,0:T(1,128)}, u32[]{:S(2)}) copy-start(f32[1,192]{1,0:T(1,128)} %shard_map.61) | copy-start | bytes 2308

commit v11 on v10

--- a/solution.py
+++ b/solution.py
@@ -136,17 +136,22 @@
 
     def body(r, carry):
         top = pl.multiple_of(r * rows, rows)
-        hidden = []
-        for j in range(2):
-            acc = jnp.zeros((rows * width, channels), jnp.float32)
-            for b in range(3):
-                for c in range(3):
-                    taps = [xs_ref[c, j + a, pl.ds(top + b, rows)] for a in range(3)]
-                    lhs = jnp.concatenate(taps, axis=-1).reshape(rows * width, 3 * channels)
-                    acc = acc + jnp.dot(lhs, w_ref[b * 3 + c], preferred_element_type=jnp.float32)
-            silu = acc / (1.0 + jnp.exp(-acc))
-            hidden.append(silu.astype(jnp.bfloat16).astype(jnp.float32))
-        pooled = ((hidden[0] + hidden[1]) * 0.5).astype(o_ref.dtype)
+        span = rows * width
+        acc = jnp.zeros((2 * span, channels), jnp.float32)
+        for b in range(3):
+            for c in range(3):
+                lhs = jnp.concatenate(
+                    [
+                        jnp.concatenate(
+                            [xs_ref[c, j + a, pl.ds(top + b, rows)] for a in range(3)], axis=-1
+                        ).reshape(span, 3 * channels)
+                        for j in range(2)
+                    ],
+                    axis=0,
+                )
+                acc = acc + jnp.dot(lhs, w_ref[b * 3 + c], preferred_element_type=jnp.float32)
+        silu = (acc / (1.0 + jnp.exp(-acc))).astype(jnp.bfloat16).astype(jnp.float32)
+        pooled = ((silu[:span] + silu[span:]) * 0.5).astype(o_ref.dtype)
         o_ref[pl.ds(top, rows)] = pooled.reshape(rows, width, channels)
         return carry
 

time: 114 us -> 114 us (level)
  no operation moved by 1% of the time
where the time goes in v11:
time: 114 us
  Pallas kernels  67.6 us (59%)
  waiting for transfers between devices  18.8 us (16%)
  starting transfers between devices  14.7 us (13%)
  other arithmetic  5.82 us (5%)
  local copies, waits for them, and re-layouts  3.66 us (3%)
  matrix products  2.7 us (2%)
    pallas_call x1, Pallas kernels, prologue(): pl.pallas_call(prologue_kernel, out_shape=(jax.ShapeDtypeStruct(frames.sh...  33.6 us
    pallas_call x1, Pallas kernels, scatter_sum(): pl.pallas_call(scatter_kernel, out_shape=jax.ShapeDtypeStruct((1, piece),...  19.3 us
    all_to_all x1, waiting for transfers between devices, local(): lax.all_to_all(pooled, 'tm', split_axis=1, concat_axis=0, tiled=True)  15.8 us
    pallas_call x1, Pallas kernels, conv_pool(): pl.pallas_call(conv_pool_kernel, out_shape=jax.ShapeDtypeStruct((height,...  14.7 us
    all_to_all x1, starting transfers between devices, local(): lax.all_to_all(pooled, 'tm', split_axis=1, concat_axis=0, tiled=True)  8.19 us
    concatenate x1, other arithmetic, with_halo(): jnp.concatenate([lax.ppermute(tail, axis, [(i, (i + 1) % count) for i in...  4.82 us
    ppermute x1, starting transfers between devices, with_halo(): lax.ppermute(tail, axis, [(i, (i + 1) % count) for i in range(ends)])  4.63 us
    ppermute x1, waiting for transfers between devices, with_halo(): lax.ppermute(head, axis, [((i + 1) % count, i) for i in range(ends)])  2.92 us
  transfers between devices with their start and end apart: 3, of which 2 were waited for; matrix products, arithmetic and copies ran while one was open for 2% of the time, Pallas kernels for 0%

profile of v11, /device:TPU:1, one launch (start us, length us, event | category | flops | bytes accessed | tf_op | source)
XLA Modules:
  0.0 114.1 jit_solution(18422255913811263884)
XLA Ops:
  0.6 0.0 copy-start
  0.6 0.0 copy-start.1
  0.7 33.6 %shard_map.59 = (bf16[2,64,32,128]{3,2,1,0:T(8,128)(2,1)}, bf16[8,27,16,128]{3,2,1,0:T(8,128)(2,1)}, bf16[8,3,16,128]{3,2,1,0:T(8,128)(2,1)}) custom-call(bf16[2,64,32,128]{3,2,1,0:T(8,128)(2,1)} %x_ref.1, bf16[27,16,128]{2,1,0:T(8,128)(2,1)} %bitcast.69, bf16[3,16,128]{2,1,0:T(8,128)(2,1)} %bitcast.71), custom_call_target="tpu_custom_call" | custom-call | tf_op jit(solution)/shard_map/pallas_call | solution.py:241
  34.3 0.0 copy-start.2
  34.3 0.1 broadcast_select_fusion
  34.4 0.0 copy-done.1
  34.4 0.9 pad_maximum_fusion.2
  35.3 4.6 %collective-permute-start = (bf16[4,64,1,128]{3,2,1,0:T(2,128)(2,1)}, bf16[4,64,1,128]{3,2,1,0:T(2,128)(2,1)}, u32[]{:S(2)}, u32[]{:S(2)}) collective-permute-start(bf16[4,64,1,128]{3,2,1,0:T(2,128)(2,1)} %get-tuple-element.8), channel_id=1, source_target_pairs={{0,1},{1,2},{2,3},{3,4},{4,5},{5,6},{6,7},{8,9},{9,10},{10,11},{11... | collective-permute-start | bytes 196616 | tf_op jit(solution)/shard_map/ppermute | solution.py:25
  40.0 1.9 %collective-permute-start.1 = (bf16[4,64,1,128]{3,2,1,0:T(2,128)(2,1)}, bf16[4,64,1,128]{3,2,1,0:T(2,128)(2,1)}, u32[]{:S(2)}, u32[]{:S(2)}) collective-permute-start(bf16[4,64,1,128]{3,2,1,0:T(2,128)(2,1)} %get-tuple-element.9), channel_id=1, source_target_pairs={{1,0},{2,1},{3,2},{4,3},{5,4},{6,5},{7,6},{9,8},{10,9},{11,10},{12... | collective-permute-start | bytes 196616 | tf_op jit(solution)/shard_map/ppermute | solution.py:27
  41.9 0.0 copy-done.2
  41.9 0.2 copy.9
  42.1 1.5 %copy.10 = bf16[3,3,3,128,128]{4,3,2,1,0:T(8,128)(2,1)} copy(bf16[3,3,3,128,128]{3,4,1,0,2:T(8,128)(2,1)S(1)} %bitcast.58) | data formatting | bytes 1769472 | tf_op jit(solution)/shard_map/transpose | solution.py:276
  43.6 0.0 collective-permute-done
  43.6 2.9 %collective-permute-done.1 = bf16[4,64,1,128]{3,2,1,0:T(2,128)(2,1)} collective-permute-done((bf16[4,64,1,128]{3,2,1,0:T(2,128)(2,1)}, bf16[4,64,1,128]{3,2,1,0:T(2,128)(2,1)}, u32[]{:S(2)}, u32[]{:S(2)}) %collective-permute-start.1) | collective-permute-done | bytes 65568 | tf_op jit(solution)/shard_map/ppermute | solution.py:27
  46.6 4.8 %select_maximum_fusion.p_ref = bf16[4,72,34,128]{3,2,1,0:T(8,128)(2,1)} fusion(bf16[4,64,1,128]{3,2,1,0:T(2,128)(2,1)} %collective-permute-done.1, bf16[4,64,1,128]{3,2,1,0:T(2,128)(2,1)} %collective-permute-done, bf16[2,64,32,128]{3,2,1,0:T(8,128)(2,1)S(1)} %copy-done.1, bf16[2,64,32,128]{3,2,1,0:T(8,128)(2,1)S(1)} %broadcast_select_fusion), kind=kLoop, calls=%fused_computation.3 | loop fusion | flops 18800640 | bytes 4734976 | tf_op jit(solution)/shard_map/concatenate | solution.py:23
  51.4 0.0 copy-start.3
  51.4 14.7 %shard_map.60 = bf16[64,32,128]{2,1,0:T(8,128)(2,1)} custom-call(bf16[4,72,34,128]{3,2,1,0:T(8,128)(2,1)} %select_maximum_fusion.p_ref, bf16[9,384,128]{2,1,0:T(8,128)(2,1)} %bitcast.63), custom_call_target="tpu_custom_call" | custom-call | flops 3623878656 | bytes 3915776 | tf_op jit(solution)/shard_map/pallas_call | solution.py:166
  66.1 8.2 %all-to-all-start = ((bf16[1,64,32,128]{3,2,0,1:T(8,128)(2,1)}), bf16[1,64,32,128]{3,2,0,1:T(8,128)(2,1)S(1)}, u32[]{:S(2)}, u32[]{:S(2)}) async-start(bf16[1,64,32,128]{3,2,0,1:T(8,128)(2,1)} %bitcast.64), calls=%async_computation | async-start | bytes 1048576 | tf_op jit(solution)/shard_map/all_to_all | solution.py:278
  74.3 0.0 copy-done.3
  74.3 15.8 %all-to-all-done = bf16[1,64,32,128]{3,2,0,1:T(8,128)(2,1)S(1)} async-done(((bf16[1,64,32,128]{3,2,0,1:T(8,128)(2,1)}), bf16[1,64,32,128]{3,2,0,1:T(8,128)(2,1)S(1)}, u32[]{:S(2)}, u32[]{:S(2)}) %all-to-all-start) | async-done | bytes 524320 | tf_op jit(solution)/shard_map/all_to_all | solution.py:278
  90.2 0.0 copy-done
  90.2 0.3 convolution_bitcast_fusion.1
  90.5 0.3 convolution_bitcast_fusion
  90.9 0.2 pad_slice_fusion
  91.1 0.3 convolution_bitcast_fusion.2
  91.5 0.1 reshape_reshape.3
  91.6 1.0 copy.16
  92.6 19.3 %shard_map.61 = f32[1,192]{1,0:T(1,128)} custom-call(f32[8,32,1,192]{3,2,1,0:T(1,128)} %bitcast.61), custom_call_target="tpu_custom_call" | custom-call | tf_op jit(solution)/shard_map/pallas_call | solution.py:100
  111.8 0.0 copy-start.4
  111.8 0.3 convolution_add_fusion.2
  112.1 0.3 convolution_add_fusion.1
  112.4 1.1 fusion.4
  113.5 0.0 copy-done.4
  113.5 0.6 copy.18
  (2 shorter events, 0.0 us)
Async XLA Ops:
  0.6 89.5 %copy-start = (bf16[32,2,32,128]{3,2,1,0:T(8,128)(2,1)S(1)}, bf16[32,2,32,128]{3,2,1,0:T(8,128)(2,1)}, u32[]{:S(2)}) copy-start(bf16[32,2,32,128]{3,2,1,0:T(8,128)(2,1)} %param.7) | copy-start | bytes 1572868
  0.6 33.8 %copy-start.1 = (bf16[2,64,32,128]{3,2,1,0:T(8,128)(2,1)S(1)}, bf16[2,64,32,128]{3,2,1,0:T(8,128)(2,1)}, u32[]{:S(2)}) copy-start(bf16[2,64,32,128]{3,2,1,0:T(8,128)(2,1)} %x_ref.1) | copy-start | bytes 3145732
  34.3 7.6 %copy-start.2 = (bf16[8,27,16,128]{3,2,1,0:T(8,128)(2,1)S(1)}, bf16[8,27,16,128]{3,2,1,0:T(8,128)(2,1)}, u32[]{:S(2)}) copy-start(bf16[8,27,16,128]{3,2,1,0:T(8,128)(2,1)} %get-tuple-element.6) | copy-start | bytes 2654212
  35.3 8.3 %collective-permute-start = (bf16[4,64,1,128]{3,2,1,0:T(2,128)(2,1)}, bf16[4,64,1,128]{3,2,1,0:T(2,128)(2,1)}, u32[]{:S(2)}, u32[]{:S(2)}) collective-permute-start(bf16[4,64,1,128]{3,2,1,0:T(2,128)(2,1)} %get-tuple-element.8), channel_id=1, source_target_pairs={{0,1},{1,2},{2,3},{3,4},{4,5},{5,6},{6,7},{8,9},{9,10},{10,11},{11... | collective-permute-start | bytes 196616 | tf_op jit(solution)/shard_map/ppermute | solution.py:25
  40.0 6.6 %collective-permute-start.1 = (bf16[4,64,1,128]{3,2,1,0:T(2,128)(2,1)}, bf16[4,64,1,128]{3,2,1,0:T(2,128)(2,1)}, u32[]{:S(2)}, u32[]{:S(2)}) collective-permute-start(bf16[4,64,1,128]{3,2,1,0:T(2,128)(2,1)} %get-tuple-element.9), channel_id=1, source_target_pairs={{1,0},{2,1},{3,2},{4,3},{5,4},{6,5},{7,6},{9,8},{10,9},{11,10},{12... | collective-permute-start | bytes 196616 | tf_op jit(solution)/shard_map/ppermute | solution.py:27
  51.4 22.9 %copy-start.3 = (bf16[8,3,16,128]{3,2,1,0:T(8,128)(2,1)S(1)}, bf16[8,3,16,128]{3,2,1,0:T(8,128)(2,1)}, u32[]{:S(2)}) copy-start(bf16[8,3,16,128]{3,2,1,0:T(8,128)(2,1)} %get-tuple-element.7) | copy-start | bytes 294916
  66.1 24.1 %all-to-all-start = ((bf16[1,64,32,128]{3,2,0,1:T(8,128)(2,1)}), bf16[1,64,32,128]{3,2,0,1:T(8,128)(2,1)S(1)}, u32[]{:S(2)}, u32[]{:S(2)}) async-start(bf16[1,64,32,128]{3,2,0,1:T(8,128)(2,1)} %bitcast.64), calls=%async_computation | async-start | bytes 1048576 | tf_op jit(solution)/shard_map/all_to_all | solution.py:278
  111.8 1.7 %copy-start.4 = (f32[1,192]{1,0:T(1,128)S(1)}, f32[1,192]{1,0:T(1,128)}, u32[]{:S(2)}) copy-start(f32[1,192]{1,0:T(1,128)} %shard_map.61) | copy-start | bytes 2308

commit v12 on v11

--- a/solution.py
+++ b/solution.py
@@ -40,81 +40,63 @@
     return jnp.pad(block, ((offset, 0), (0, 0), (0, 0), (0, 0)))[: block.shape[0]]
 
 
-def scatter_kernel(p_ref, o_ref, first, second, summed, s1, r1, s2, r2, l1, l2):
-    groups, count = first.shape[0], second.shape[0]
-    f, t = lax.axis_index("fsdp"), lax.axis_index("tm")
+def scatter_kernel(p_ref, o_ref, held, sends, recvs, local_sem):
+    groups, total = lax.axis_size("fsdp"), held.shape[0]
+    me = lax.axis_index("tm") * groups + lax.axis_index("fsdp")
+
+    def device(k):
+        peer = lax.rem(me + k, total)
+        return (peer // groups, lax.rem(peer, groups))
+
+    def copy_of(k):
+        return pltpu.make_async_remote_copy(
+            src_ref=p_ref.at[lax.rem(me + k, total)],
+            dst_ref=held.at[me],
+            send_sem=sends.at[k],
+            recv_sem=recvs.at[k],
+            device_id=device(k),
+            device_id_type=MESH,
+        )
+
     barrier = pltpu.get_barrier_semaphore()
-    for k in range(1, groups):
-        pl.semaphore_signal(
-            barrier, inc=1, device_id={"fsdp": lax.rem(f + k, groups)}, device_id_type=MESH
-        )
-    for k in range(1, count):
-        pl.semaphore_signal(
-            barrier, inc=1, device_id={"tm": lax.rem(t + k, count)}, device_id_type=MESH
-        )
-    pl.semaphore_wait(barrier, groups - 1 + count - 1)
-    local = pltpu.make_async_copy(p_ref.at[f], first.at[f], l1)
+
+    @pl.loop(1, total)
+    def _(k):
+        pl.semaphore_signal(barrier, inc=1, device_id=device(k), device_id_type=MESH)
+
+    pl.semaphore_wait(barrier, total - 1)
+    local = pltpu.make_async_copy(p_ref.at[me], held.at[me], local_sem)
     local.start()
-    copies = []
-    for k in range(1, groups):
-        peer = lax.rem(f + k, groups)
-        copy = pltpu.make_async_remote_copy(
-            src_ref=p_ref.at[peer],
-            dst_ref=first.at[f],
-            send_sem=s1.at[k],
-            recv_sem=r1.at[k],
-            device_id={"fsdp": peer},
-            device_id_type=MESH,
-        )
-        copy.start()
-        copies.append(copy)
+
+    @pl.loop(1, total)
+    def _(k):
+        copy_of(k).start()
+
     local.wait()
-    for copy in copies:
-        copy.wait()
-    summed[...] = jnp.sum(first[...], axis=0)
-    local = pltpu.make_async_copy(summed.at[t], second.at[t], l2)
-    local.start()
-    copies = []
-    for k in range(1, count):
-        peer = lax.rem(t + k, count)
-        copy = pltpu.make_async_remote_copy(
-            src_ref=summed.at[peer],
-            dst_ref=second.at[t],
-            send_sem=s2.at[k],
-            recv_sem=r2.at[k],
-            device_id={"tm": peer},
-            device_id_type=MESH,
-        )
-        copy.start()
-        copies.append(copy)
-    local.wait()
-    for copy in copies:
-        copy.wait()
-    o_ref[...] = jnp.sum(second[...], axis=0)
+
+    @pl.loop(1, total)
+    def _(k):
+        copy_of(k).wait()
+
+    o_ref[...] = jnp.sum(held[...], axis=0)
 
 
 def scatter_sum(partial):
-    groups, count = lax.axis_size("fsdp"), lax.axis_size("tm")
-    piece = partial.size // (groups * count)
-    arranged = jnp.transpose(partial.reshape(count, groups, 1, piece), (1, 0, 2, 3))
+    total = lax.axis_size("fsdp") * lax.axis_size("tm")
+    piece = partial.size // total
     out = pl.pallas_call(
         scatter_kernel,
         out_shape=jax.ShapeDtypeStruct((1, piece), jnp.float32),
         in_specs=[pl.BlockSpec(memory_space=pltpu.VMEM)],
         out_specs=pl.BlockSpec(memory_space=pltpu.VMEM),
         scratch_shapes=[
-            pltpu.VMEM((groups, count, 1, piece), jnp.float32),
-            pltpu.VMEM((count, 1, piece), jnp.float32),
-            pltpu.VMEM((count, 1, piece), jnp.float32),
-            pltpu.SemaphoreType.DMA((groups,)),
-            pltpu.SemaphoreType.DMA((groups,)),
-            pltpu.SemaphoreType.DMA((count,)),
-            pltpu.SemaphoreType.DMA((count,)),
-            pltpu.SemaphoreType.DMA,
+            pltpu.VMEM((total, 1, piece), jnp.float32),
+            pltpu.SemaphoreType.DMA((total,)),
+            pltpu.SemaphoreType.DMA((total,)),
             pltpu.SemaphoreType.DMA,
         ],
         compiler_params=pltpu.CompilerParams(collective_id=1, has_side_effects=True),
-    )(arranged)
+    )(partial.reshape(total, 1, piece))
     return out.reshape(piece)
 
 

time: 114 us -> 125 us (1.096)
  Pallas kernels: 67.6 us -> 77.7 us
    pallas_call x1, Pallas kernels: 19.3 us -> 29.4 us  [scatter_sum(): pl.pallas_call(scatter_kernel, out_shape=jax.ShapeDtypeStruct((1, piece),...]
  transfers between devices with their start and end apart: 3 -> 3, of which waited for: 2 -> 2; matrix products, arithmetic and copies ran while one was open for 2% -> 1% of each run, Pallas kernels for 0% -> 0%
where the time goes in v12:
time: 125 us; the launch traced here: 124 us
  Pallas kernels  77.7 us (62%)
  waiting for transfers between devices  18.8 us (15%)
  starting transfers between devices  14.7 us (12%)
  other arithmetic  5.82 us (5%)
  local copies, waits for them, and re-layouts  3.72 us (3%)
  matrix products  2.71 us (2%)
    pallas_call x1, Pallas kernels, prologue(): pl.pallas_call(prologue_kernel, out_shape=(jax.ShapeDtypeStruct(frames.sh...  33.6 us
    pallas_call x1, Pallas kernels, scatter_sum(): pl.pallas_call(scatter_kernel, out_shape=jax.ShapeDtypeStruct((1, piece),...  29.4 us
    all_to_all x1, waiting for transfers between devices, local(): lax.all_to_all(pooled, 'tm', split_axis=1, concat_axis=0, tiled=True)  15.8 us
    pallas_call x1, Pallas kernels, conv_pool(): pl.pallas_call(conv_pool_kernel, out_shape=jax.ShapeDtypeStruct((height,...  14.7 us
    all_to_all x1, starting transfers between devices, local(): lax.all_to_all(pooled, 'tm', split_axis=1, concat_axis=0, tiled=True)  8.19 us
    concatenate x1, other arithmetic, with_halo(): jnp.concatenate([lax.ppermute(tail, axis, [(i, (i + 1) % count) for i in...  4.82 us
    ppermute x1, starting transfers between devices, with_halo(): lax.ppermute(tail, axis, [(i, (i + 1) % count) for i in range(ends)])  4.63 us
    ppermute x1, waiting for transfers between devices, with_halo(): lax.ppermute(head, axis, [((i + 1) % count, i) for i in range(ends)])  2.92 us
  transfers between devices with their start and end apart: 3, of which 2 were waited for; matrix products, arithmetic and copies ran while one was open for 1% of the time, Pallas kernels for 0%

profile of v12, /device:TPU:1, one launch (start us, length us, event | category | flops | bytes accessed | tf_op | source)
XLA Modules:
  0.0 124.3 jit_solution(10163514050874682978)
XLA Ops:
  0.6 0.0 copy-start
  0.6 0.0 copy-start.1
  0.7 33.6 %shard_map.59 = (bf16[2,64,32,128]{3,2,1,0:T(8,128)(2,1)}, bf16[8,27,16,128]{3,2,1,0:T(8,128)(2,1)}, bf16[8,3,16,128]{3,2,1,0:T(8,128)(2,1)}) custom-call(bf16[2,64,32,128]{3,2,1,0:T(8,128)(2,1)} %x_ref.1, bf16[27,16,128]{2,1,0:T(8,128)(2,1)} %bitcast.65, bf16[3,16,128]{2,1,0:T(8,128)(2,1)} %bitcast.67), custom_call_target="tpu_custom_call" | custom-call | tf_op jit(solution)/shard_map/pallas_call | solution.py:223
  34.3 0.0 copy-start.2
  34.3 0.1 broadcast_select_fusion
  34.4 0.0 copy-done.1
  34.4 0.9 pad_maximum_fusion.2
  35.3 4.6 %collective-permute-start = (bf16[4,64,1,128]{3,2,1,0:T(2,128)(2,1)}, bf16[4,64,1,128]{3,2,1,0:T(2,128)(2,1)}, u32[]{:S(2)}, u32[]{:S(2)}) collective-permute-start(bf16[4,64,1,128]{3,2,1,0:T(2,128)(2,1)} %get-tuple-element.8), channel_id=1, source_target_pairs={{0,1},{1,2},{2,3},{3,4},{4,5},{5,6},{6,7},{8,9},{9,10},{10,11},{11... | collective-permute-start | bytes 196616 | tf_op jit(solution)/shard_map/ppermute | solution.py:25
  40.0 1.9 %collective-permute-start.1 = (bf16[4,64,1,128]{3,2,1,0:T(2,128)(2,1)}, bf16[4,64,1,128]{3,2,1,0:T(2,128)(2,1)}, u32[]{:S(2)}, u32[]{:S(2)}) collective-permute-start(bf16[4,64,1,128]{3,2,1,0:T(2,128)(2,1)} %get-tuple-element.9), channel_id=1, source_target_pairs={{1,0},{2,1},{3,2},{4,3},{5,4},{6,5},{7,6},{9,8},{10,9},{11,10},{12... | collective-permute-start | bytes 196616 | tf_op jit(solution)/shard_map/ppermute | solution.py:27
  41.9 0.0 copy-done.2
  41.9 0.2 copy.9
  42.1 1.5 %copy.10 = bf16[3,3,3,128,128]{4,3,2,1,0:T(8,128)(2,1)} copy(bf16[3,3,3,128,128]{3,4,1,0,2:T(8,128)(2,1)S(1)} %bitcast.55) | data formatting | bytes 1769472 | tf_op jit(solution)/shard_map/transpose | solution.py:258
  43.6 0.0 collective-permute-done
  43.6 2.9 %collective-permute-done.1 = bf16[4,64,1,128]{3,2,1,0:T(2,128)(2,1)} collective-permute-done((bf16[4,64,1,128]{3,2,1,0:T(2,128)(2,1)}, bf16[4,64,1,128]{3,2,1,0:T(2,128)(2,1)}, u32[]{:S(2)}, u32[]{:S(2)}) %collective-permute-start.1) | collective-permute-done | bytes 65568 | tf_op jit(solution)/shard_map/ppermute | solution.py:27
  46.6 4.8 %select_maximum_fusion.p_ref = bf16[4,72,34,128]{3,2,1,0:T(8,128)(2,1)} fusion(bf16[4,64,1,128]{3,2,1,0:T(2,128)(2,1)} %collective-permute-done.1, bf16[4,64,1,128]{3,2,1,0:T(2,128)(2,1)} %collective-permute-done, bf16[2,64,32,128]{3,2,1,0:T(8,128)(2,1)S(1)} %copy-done.1, bf16[2,64,32,128]{3,2,1,0:T(8,128)(2,1)S(1)} %broadcast_select_fusion), kind=kLoop, calls=%fused_computation.3 | loop fusion | flops 18800640 | bytes 4734976 | tf_op jit(solution)/shard_map/concatenate | solution.py:23
  51.4 0.0 copy-start.3
  51.4 14.7 %shard_map.60 = bf16[64,32,128]{2,1,0:T(8,128)(2,1)} custom-call(bf16[4,72,34,128]{3,2,1,0:T(8,128)(2,1)} %select_maximum_fusion.p_ref, bf16[9,384,128]{2,1,0:T(8,128)(2,1)} %bitcast.59), custom_call_target="tpu_custom_call" | custom-call | flops 3623878656 | bytes 3915776 | tf_op jit(solution)/shard_map/pallas_call | solution.py:148
  66.1 8.2 %all-to-all-start = ((bf16[1,64,32,128]{3,2,0,1:T(8,128)(2,1)}), bf16[1,64,32,128]{3,2,0,1:T(8,128)(2,1)S(1)}, u32[]{:S(2)}, u32[]{:S(2)}) async-start(bf16[1,64,32,128]{3,2,0,1:T(8,128)(2,1)} %bitcast.60), calls=%async_computation | async-start | bytes 1048576 | tf_op jit(solution)/shard_map/all_to_all | solution.py:260
  74.3 0.0 copy-done.3
  74.3 15.8 %all-to-all-done = bf16[1,64,32,128]{3,2,0,1:T(8,128)(2,1)S(1)} async-done(((bf16[1,64,32,128]{3,2,0,1:T(8,128)(2,1)}), bf16[1,64,32,128]{3,2,0,1:T(8,128)(2,1)S(1)}, u32[]{:S(2)}, u32[]{:S(2)}) %all-to-all-start) | async-done | bytes 524320 | tf_op jit(solution)/shard_map/all_to_all | solution.py:260
  90.2 0.0 copy-done
  90.2 0.3 convolution_bitcast_fusion.1
  90.5 0.3 convolution_bitcast_fusion
  90.9 0.2 pad_slice_fusion
  91.1 0.3 convolution_bitcast_fusion.2
  91.5 1.1 reshape_reshape.4.p_ref
  92.6 29.4 %shard_map.61 = f32[1,192]{1,0:T(1,128)} custom-call(f32[256,1,192]{2,1,0:T(1,128)} %reshape_reshape.4.p_ref), custom_call_target="tpu_custom_call" | custom-call | tf_op jit(solution)/shard_map/pallas_call | solution.py:87
  122.0 0.0 copy-start.4
  122.0 0.3 convolution_add_fusion.2
  122.3 0.3 convolution_add_fusion.1
  122.6 1.1 fusion.4
  123.7 0.0 copy-done.4
  123.7 0.6 copy.16
  (2 shorter events, 0.0 us)
Async XLA Ops:
  0.6 89.5 %copy-start = (bf16[32,2,32,128]{3,2,1,0:T(8,128)(2,1)S(1)}, bf16[32,2,32,128]{3,2,1,0:T(8,128)(2,1)}, u32[]{:S(2)}) copy-start(bf16[32,2,32,128]{3,2,1,0:T(8,128)(2,1)} %param.7) | copy-start | bytes 1572868
  0.6 33.8 %copy-start.1 = (bf16[2,64,32,128]{3,2,1,0:T(8,128)(2,1)S(1)}, bf16[2,64,32,128]{3,2,1,0:T(8,128)(2,1)}, u32[]{:S(2)}) copy-start(bf16[2,64,32,128]{3,2,1,0:T(8,128)(2,1)} %x_ref.1) | copy-start | bytes 3145732
  34.3 7.6 %copy-start.2 = (bf16[8,27,16,128]{3,2,1,0:T(8,128)(2,1)S(1)}, bf16[8,27,16,128]{3,2,1,0:T(8,128)(2,1)}, u32[]{:S(2)}) copy-start(bf16[8,27,16,128]{3,2,1,0:T(8,128)(2,1)} %get-tuple-element.6) | copy-start | bytes 2654212
  35.3 8.3 %collective-permute-start = (bf16[4,64,1,128]{3,2,1,0:T(2,128)(2,1)}, bf16[4,64,1,128]{3,2,1,0:T(2,128)(2,1)}, u32[]{:S(2)}, u32[]{:S(2)}) collective-permute-start(bf16[4,64,1,128]{3,2,1,0:T(2,128)(2,1)} %get-tuple-element.8), channel_id=1, source_target_pairs={{0,1},{1,2},{2,3},{3,4},{4,5},{5,6},{6,7},{8,9},{9,10},{10,11},{11... | collective-permute-start | bytes 196616 | tf_op jit(solution)/shard_map/ppermute | solution.py:25
  40.0 6.6 %collective-permute-start.1 = (bf16[4,64,1,128]{3,2,1,0:T(2,128)(2,1)}, bf16[4,64,1,128]{3,2,1,0:T(2,128)(2,1)}, u32[]{:S(2)}, u32[]{:S(2)}) collective-permute-start(bf16[4,64,1,128]{3,2,1,0:T(2,128)(2,1)} %get-tuple-element.9), channel_id=1, source_target_pairs={{1,0},{2,1},{3,2},{4,3},{5,4},{6,5},{7,6},{9,8},{10,9},{11,10},{12... | collective-permute-start | bytes 196616 | tf_op jit(solution)/shard_map/ppermute | solution.py:27
  51.4 22.9 %copy-start.3 = (bf16[8,3,16,128]{3,2,1,0:T(8,128)(2,1)S(1)}, bf16[8,3,16,128]{3,2,1,0:T(8,128)(2,1)}, u32[]{:S(2)}) copy-start(bf16[8,3,16,128]{3,2,1,0:T(8,128)(2,1)} %get-tuple-element.7) | copy-start | bytes 294916
  66.1 24.1 %all-to-all-start = ((bf16[1,64,32,128]{3,2,0,1:T(8,128)(2,1)}), bf16[1,64,32,128]{3,2,0,1:T(8,128)(2,1)S(1)}, u32[]{:S(2)}, u32[]{:S(2)}) async-start(bf16[1,64,32,128]{3,2,0,1:T(8,128)(2,1)} %bitcast.60), calls=%async_computation | async-start | bytes 1048576 | tf_op jit(solution)/shard_map/all_to_all | solution.py:260
  122.0 1.7 %copy-start.4 = (f32[1,192]{1,0:T(1,128)S(1)}, f32[1,192]{1,0:T(1,128)}, u32[]{:S(2)}) copy-start(f32[1,192]{1,0:T(1,128)} %shard_map.61) | copy-start | bytes 2308

commit v13 on v11

--- a/solution.py
+++ b/solution.py
@@ -118,21 +118,41 @@
     return out.reshape(piece)
 
 
-def conv_pool_kernel(p_ref, w_ref, o_ref, xs_ref):
+def conv_pool_kernel(h_ref, x_ref, l_ref, r_ref, w_ref, o_ref, xs_ref):
     height, width, channels = o_ref.shape
-    frames = p_ref.shape[0]
+    depth = x_ref.shape[0]
+    groups = lax.axis_size("fsdp")
+    t, f = lax.axis_index("tm"), lax.axis_index("fsdp")
     rows = 8
-    band = 8
-
-    def shift(i, carry):
-        q, r = i // (p_ref.shape[1] // band), i % (p_ref.shape[1] // band)
-        top = pl.multiple_of(r * band, band)
-        block = p_ref[q, pl.ds(top, band)].astype(jnp.float32)
-        for c in range(3):
-            xs_ref[c, q, pl.ds(top, band)] = block[:, c : c + width].astype(xs_ref.dtype)
+    zero_rows = jnp.zeros((3, 2 * depth, 1, width, channels), xs_ref.dtype)
+    xs_ref[:, :, pl.ds(0, 1)] = zero_rows
+    xs_ref[:, :, pl.ds(height + 1, 1)] = zero_rows
+    col = lax.broadcasted_iota(jnp.int32, (rows, width, channels), 1)
+
+    def shift(r, carry):
+        top = pl.multiple_of(r * rows, rows)
+        for q in range(2 * depth):
+            earlier = q < depth
+            src = h_ref if earlier else x_ref
+            block = src[q % depth, pl.ds(top, rows)].astype(jnp.float32)
+            lft = l_ref[q, pl.ds(top, rows)].astype(jnp.float32)[:, None, :]
+            rgt = r_ref[q, pl.ds(top, rows)].astype(jnp.float32)[:, None, :]
+            lok, rok = f > 0, f < groups - 1
+            if earlier:
+                block = jnp.where(t > 0, block, 0.0)
+                lok, rok = lok & (t > 0), rok & (t > 0)
+            lft = jnp.where(lok, lft, 0.0)
+            rgt = jnp.where(rok, rgt, 0.0)
+            moved = [
+                jnp.where(col == 0, lft, pltpu.roll(block, 1, 1)),
+                block,
+                jnp.where(col == width - 1, rgt, pltpu.roll(block, width - 1, 1)),
+            ]
+            for c in range(3):
+                xs_ref[c, q, pl.ds(top + 1, rows)] = moved[c].astype(xs_ref.dtype)
         return carry
 
-    lax.fori_loop(0, frames * (p_ref.shape[1] // band), shift, 0)
+    lax.fori_loop(0, height // rows, shift, 0)
 
     def body(r, carry):
         top = pl.multiple_of(r * rows, rows)
@@ -158,30 +178,31 @@
     lax.fori_loop(0, height // rows, body, 0)
 
 
-def conv_pool(padded, weights):
-    frames, rows, wide, channels = padded.shape
-    height, width = rows - 8, wide - 2
+def conv_pool(halo, frames, left, right, weights):
+    depth, height, width, channels = frames.shape
     vmem = pl.BlockSpec(memory_space=pltpu.VMEM)
     flops = 2 * 2 * height * width * weights.shape[0] * weights.shape[1] * channels
     return pl.pallas_call(
         conv_pool_kernel,
         out_shape=jax.ShapeDtypeStruct((height, width, channels), jnp.bfloat16),
-        in_specs=[vmem, vmem],
+        in_specs=[vmem] * 5,
         out_specs=vmem,
-        scratch_shapes=[pltpu.VMEM((3, frames, rows, width, channels), padded.dtype)],
+        scratch_shapes=[pltpu.VMEM((3, 2 * depth, height + 8, width, channels), frames.dtype)],
         cost_estimate=pl.CostEstimate(
             flops=flops,
             transcendentals=2 * height * width * channels,
-            bytes_accessed=padded.size * 2 + weights.size * 2 + height * width * channels * 2,
+            bytes_accessed=4 * frames.size + weights.size * 2 + height * width * channels * 2,
         ),
-    )(padded, weights)
-
-
-def prologue_kernel(x_ref, w_ref, m_ref, halo_ref, wall_ref, mall_ref, sends, recvs, wsends, wrecvs, msends, mrecvs, lsems):
+    )(halo, frames, left, right, weights)
+
+
+def prologue_kernel(x_ref, w_ref, m_ref, lcol_ref, rcol_ref, halo_ref, wall_ref, mall_ref, left_ref, right_ref, sends, recvs, wsends, wrecvs, msends, mrecvs, lsems, esends, erecvs):
     count, groups = lax.axis_size("tm"), lax.axis_size("fsdp")
     t, f = lax.axis_index("tm"), lax.axis_index("fsdp")
     t_next, t_prev = lax.rem(t + 1, count), lax.rem(t + count - 1, count)
+    f_next, f_prev = lax.rem(f + 1, groups), lax.rem(f + groups - 1, groups)
     peers = [(t_next, f), (t_prev, f)] + [(t, lax.rem(f + k, groups)) for k in range(1, groups)]
+    peers += [(a, b) for a in (t_next, t_prev) for b in (f_next, f_prev)]
     barrier = pltpu.get_barrier_semaphore()
     for dev in peers:
         pl.semaphore_signal(barrier, inc=1, device_id=dev, device_id_type=MESH)
@@ -197,6 +218,24 @@
         )
         for i in range(pieces)
     ]
+
+    depth = x_ref.shape[0]
+    edges = [
+        (rcol_ref, left_ref.at[pl.ds(depth, depth)], (t, f_next)),
+        (lcol_ref, right_ref.at[pl.ds(depth, depth)], (t, f_prev)),
+        (rcol_ref, left_ref.at[pl.ds(0, depth)], (t_next, f_next)),
+        (lcol_ref, right_ref.at[pl.ds(0, depth)], (t_next, f_prev)),
+    ]
+    edges = [
+        pltpu.make_async_remote_copy(
+            src_ref=src, dst_ref=dst, send_sem=esends.at[i], recv_sem=erecvs.at[i],
+            device_id=dev, device_id_type=MESH,
+        )
+        for i, (src, dst, dev) in enumerate(edges)
+    ]
+    for copy in edges[:2]:
+        copy.start()
+    halo = halo + edges[2:]
 
     @pl.when(t < count - 1)
     def _():
@@ -221,7 +260,7 @@
             copies.append(copy)
     for copy in locals_:
         copy.wait()
-    for copy in copies:
+    for copy in copies + edges[:2]:
         copy.wait()
 
     @pl.when(t < count - 1)
@@ -237,6 +276,10 @@
 
 def prologue(frames, conv_shard, mix_shard):
     groups = lax.axis_size("fsdp")
+    depth, height, width, channels = frames.shape
+    lcol = frames[:, :, 0, :]
+    rcol = frames[:, :, width - 1, :]
+    edge = jax.ShapeDtypeStruct((2 * depth, height, channels), frames.dtype)
     vmem = pl.BlockSpec(memory_space=pltpu.VMEM)
     return pl.pallas_call(
         prologue_kernel,
@@ -244,9 +287,11 @@
             jax.ShapeDtypeStruct(frames.shape, frames.dtype),
             jax.ShapeDtypeStruct((groups,) + conv_shard.shape, conv_shard.dtype),
             jax.ShapeDtypeStruct((groups,) + mix_shard.shape, mix_shard.dtype),
+            edge,
+            edge,
         ),
-        in_specs=[vmem] * 3,
-        out_specs=(vmem,) * 3,
+        in_specs=[vmem] * 5,
+        out_specs=(vmem,) * 5,
         scratch_shapes=[
             pltpu.SemaphoreType.DMA((4,)),
             pltpu.SemaphoreType.DMA((4,)),
@@ -255,9 +300,11 @@
             pltpu.SemaphoreType.DMA((groups,)),
             pltpu.SemaphoreType.DMA((groups,)),
             pltpu.SemaphoreType.DMA((2,)),
+            pltpu.SemaphoreType.DMA((4,)),
+            pltpu.SemaphoreType.DMA((4,)),
         ],
         compiler_params=pltpu.CompilerParams(collective_id=2, has_side_effects=True),
-    )(frames, conv_shard, mix_shard)
+    )(frames, conv_shard, mix_shard, lcol, rcol)
 
 
 def local(frames, conv_weight, mix_weight, cotangent):
@@ -266,15 +313,11 @@
     part = conv_weight.shape[-1]
     conv_shard = jnp.swapaxes(conv_weight, 3, 4).reshape(-1, part, channels)
     mix_shard = jnp.swapaxes(mix_weight, 1, 2)
-    previous, wall, mall = prologue(frames, conv_shard, mix_shard)
+    previous, wall, mall, left, right = prologue(frames, conv_shard, mix_shard)
     full_conv = jnp.transpose(wall, (1, 3, 0, 2)).reshape(conv_weight.shape[:-1] + (-1,))
     full_mix = jnp.transpose(mall, (1, 3, 0, 2)).reshape(mix_weight.shape[:-1] + (-1,))
-    previous = jnp.where(t > 0, previous, jnp.zeros((), previous.dtype))
-    timed = jnp.concatenate([previous, frames], axis=0)
-    padded = with_halo(timed, (("fsdp", 2),), 1)
-    padded = jnp.pad(padded, ((0, 0), (1, 7), (0, 0), (0, 0)))
     weights = jnp.transpose(full_conv, (1, 2, 0, 3, 4)).reshape(9, 3 * channels, -1)
-    pooled = conv_pool(padded, weights)[None]
+    pooled = conv_pool(previous, frames, left, right, weights)[None]
     pooled = lax.all_to_all(pooled, "tm", split_axis=1, concat_axis=0, tiled=True)
     branch = pooled.astype(jnp.float32).reshape(-1, channels)
     flat_cot = cotangent.reshape(-1, channels)

time: 114 us -> 104 us (0.912)
  starting transfers between devices: 14.7 us -> 8.18 us
  other arithmetic: 5.82 us -> 0.02 us
  local copies, waits for them, and re-layouts: 3.66 us -> 7.32 us
  waiting for transfers between devices: 18.8 us -> 16.5 us
    ppermute x2 -> x0, starting transfers between devices: 6.55 us -> none  [the longest x1 4.63 us: with_halo(): lax.ppermute(tail, axis, [(i, (i + 1) % count) for i in range(ends)])]
    concatenate x1 -> x0, other arithmetic: 4.82 us -> none  [with_halo(): jnp.concatenate([lax.ppermute(tail, axis, [(i, (i + 1) % count) for i in...]
    ppermute x2 -> x0, waiting for transfers between devices: 2.92 us -> none  [the longest x1 2.92 us: with_halo(): lax.ppermute(head, axis, [((i + 1) % count, i) for i in range(ends)])]
    pallas_call x1, Pallas kernels: 33.6 us -> 36.2 us  [prologue(): pl.pallas_call(prologue_kernel, out_shape=(jax.ShapeDtypeStruct(frames.sh...]
    pallas_call x1, Pallas kernels: 14.7 us -> 13 us  [conv_pool(): pl.pallas_call(conv_pool_kernel, out_shape=jax.ShapeDtypeStruct((height,...]
    slice x0 -> x1, local copies, waits for them, and re-layouts: none -> 1.2 us  [prologue(): rcol = frames[:, :, width - 1, :]]
    transpose x1, local copies, waits for them, and re-layouts: 0.24 us -> 1.41 us  [local(): jnp.transpose(wall, (1, 3, 0, 2)).reshape(conv_weight.shape[:-1] + (-1,))]
  transfers between devices with their start and end apart: 3 -> 1, of which waited for: 2 -> 1; matrix products, arithmetic and copies ran while one was open for 2% -> 0% of each run, Pallas kernels for 0% -> 0%
where the time goes in v13:
time: 104 us; the launch traced here: 103 us
  Pallas kernels  67.9 us (65%)
  waiting for transfers between devices  16.5 us (16%)
  starting transfers between devices  8.18 us (8%)
  local copies, waits for them, and re-layouts  7.32 us (7%)
  matrix products  2.69 us (3%)
    pallas_call x1, Pallas kernels, prologue(): pl.pallas_call(prologue_kernel, out_shape=(jax.ShapeDtypeStruct(frames.sh...  36.2 us
    pallas_call x1, Pallas kernels, scatter_sum(): pl.pallas_call(scatter_kernel, out_shape=jax.ShapeDtypeStruct((1, piece),...  18.7 us
    all_to_all x1, waiting for transfers between devices, local(): lax.all_to_all(pooled, 'tm', split_axis=1, concat_axis=0, tiled=True)  16.5 us
    pallas_call x1, Pallas kernels, conv_pool(): pl.pallas_call(conv_pool_kernel, out_shape=jax.ShapeDtypeStruct((height,...  13 us
    all_to_all x1, starting transfers between devices, local(): lax.all_to_all(pooled, 'tm', split_axis=1, concat_axis=0, tiled=True)  8.18 us
  transfers between devices with their start and end apart: 1, of which 1 were waited for; matrix products, arithmetic and copies ran while one was open for 0% of the time, Pallas kernels for 0%

profile of v13, /device:TPU:1, one launch (start us, length us, event | category | flops | bytes accessed | tf_op | source)
XLA Modules:
  0.0 103.4 jit_solution(9396314986564158706)
XLA Ops:
  0.6 0.0 copy-start
  0.6 1.2 %fusion.1 = (bf16[2,64,1,128]{3,2,1,0:T(2,128)(2,1)S(1)}, bf16[2,64,1,128]{3,2,1,0:T(2,128)(2,1)S(1)}) fusion(bf16[2,64,32,128]{3,2,1,0:T(8,128)(2,1)} %x_ref.3), kind=kLoop, calls=%fused_computation.13 | loop fusion | bytes 131072 | tf_op jit(solution)/shard_map/slice | solution.py:281
  1.9 0.6 copy_bitcast_fusion.1
  2.5 36.2 %shard_map.59 = (bf16[2,64,32,128]{3,2,1,0:T(8,128)(2,1)}, bf16[8,27,16,128]{3,2,1,0:T(8,128)(2,1)}, bf16[8,3,16,128]{3,2,1,0:T(8,128)(2,1)}, bf16[4,64,128]{2,1,0:T(8,128)(2,1)}, bf16[4,64,128]{2,1,0:T(8,128)(2,1)}) custom-call(bf16[2,64,32,128]{3,2,1,0:T(8,128)(2,1)} %x_ref.3, bf16[27,16,128]{2,1,0:T(8,128)(2,1)} %bitcast.73, ...), custom_call_target="tpu_custom_call" | custom-call | tf_op jit(solution)/shard_map/pallas_call | solution.py:284
  38.6 1.4 %copy.15 = bf16[27,128,8,16]{1,3,2,0:T(8,128)(2,1)S(1)} copy(bf16[27,128,8,16]{1,3,0,2:T(8,128)(2,1)} %bitcast.66) | data formatting | bytes 1769472 | tf_op jit(solution)/shard_map/transpose | solution.py:317
  40.1 1.5 %copy.16 = bf16[3,3,3,128,128]{4,3,2,1,0:T(8,128)(2,1)} copy(bf16[3,3,3,128,128]{3,4,1,0,2:T(8,128)(2,1)S(1)} %bitcast.62) | data formatting | bytes 1769472 | tf_op jit(solution)/shard_map/transpose | solution.py:319
  41.6 13.0 %shard_map.60 = bf16[64,32,128]{2,1,0:T(8,128)(2,1)} custom-call(bf16[2,64,32,128]{3,2,1,0:T(8,128)(2,1)} %get-tuple-element.7.h_ref, bf16[2,64,32,128]{3,2,1,0:T(8,128)(2,1)} %x_ref.3, bf16[4,64,128]{2,1,0:T(8,128)(2,1)} %get-tuple-element.8.l_ref, bf16[4,64,128]{2,1,0:T(8,128)(2,1)} %get-tuple-element.9.r_ref, bf16[9,384,128]{2,1,0:T(8,128)(2,1)} %bitcast.67), custom_call_target="tpu_custom_call" | custom-call | flops 3623878656 | bytes 3506176 | tf_op jit(solution)/shard_map/pallas_call | solution.py:185
  54.6 0.0 copy-start.1
  54.6 8.2 %all-to-all-start = ((bf16[1,64,32,128]{3,2,0,1:T(8,128)(2,1)}), bf16[1,64,32,128]{3,2,0,1:T(8,128)(2,1)S(1)}, u32[]{:S(2)}, u32[]{:S(2)}) async-start(bf16[1,64,32,128]{3,2,0,1:T(8,128)(2,1)} %bitcast.68), calls=%async_computation | async-start | bytes 1048576 | tf_op jit(solution)/shard_map/all_to_all | solution.py:321
  62.8 0.0 copy-done.1
  62.8 16.5 %all-to-all-done = bf16[1,64,32,128]{3,2,0,1:T(8,128)(2,1)S(1)} async-done(((bf16[1,64,32,128]{3,2,0,1:T(8,128)(2,1)}), bf16[1,64,32,128]{3,2,0,1:T(8,128)(2,1)S(1)}, u32[]{:S(2)}, u32[]{:S(2)}) %all-to-all-start) | async-done | bytes 524320 | tf_op jit(solution)/shard_map/all_to_all | solution.py:321
  79.3 0.0 copy-done
  79.3 0.3 convolution_bitcast_fusion.1
  79.7 0.3 convolution_bitcast_fusion
  80.0 0.2 pad_slice_fusion
  80.3 0.3 convolution_bitcast_fusion.2
  80.6 0.1 reshape_reshape.3
  80.7 1.0 copy.26
  81.7 18.7 %shard_map.61 = f32[1,192]{1,0:T(1,128)} custom-call(f32[8,32,1,192]{3,2,1,0:T(1,128)} %bitcast.65), custom_call_target="tpu_custom_call" | custom-call | tf_op jit(solution)/shard_map/pallas_call | solution.py:100
  100.5 0.3 convolution_add_fusion.2
  100.8 0.3 convolution_add_fusion.1
  101.1 1.1 %fusion = bf16[2048,128]{1,0:T(8,128)(2,1)} fusion(f32[2048,128]{1,0:T(8,128)S(1)} %convolution_add_fusion.1, bf16[2048,128]{1,0:T(8,128)(2,1)S(1)} %bitcast.63, bf16[128,128]{0,1:T(8,128)(2,1)S(1)} %bitcast.70), kind=kOutput, calls=%fused_computation.3 | convolution fusion | flops 67633152 | bytes 2129920 | tf_op jit(solution)/shard_map/dot_general | solution.py:327
  102.2 0.0 copy-start.2
  102.2 0.7 copy-done.2
  102.8 0.6 copy.28
  (2 shorter events, 0.0 us)
Async XLA Ops:
  0.6 78.7 %copy-start = (bf16[32,2,32,128]{3,2,1,0:T(8,128)(2,1)S(1)}, bf16[32,2,32,128]{3,2,1,0:T(8,128)(2,1)}, u32[]{:S(2)}) copy-start(bf16[32,2,32,128]{3,2,1,0:T(8,128)(2,1)} %param.7) | copy-start | bytes 1572868
  54.6 8.2 %copy-start.1 = (bf16[8,3,16,128]{3,2,1,0:T(8,128)(2,1)S(1)}, bf16[8,3,16,128]{3,2,1,0:T(8,128)(2,1)}, u32[]{:S(2)}) copy-start(bf16[8,3,16,128]{3,2,1,0:T(8,128)(2,1)} %get-tuple-element.11) | copy-start | bytes 294916
  54.6 24.7 %all-to-all-start = ((bf16[1,64,32,128]{3,2,0,1:T(8,128)(2,1)}), bf16[1,64,32,128]{3,2,0,1:T(8,128)(2,1)S(1)}, u32[]{:S(2)}, u32[]{:S(2)}) async-start(bf16[1,64,32,128]{3,2,0,1:T(8,128)(2,1)} %bitcast.68), calls=%async_computation | async-start | bytes 1048576 | tf_op jit(solution)/shard_map/all_to_all | solution.py:321
  102.2 0.7 copy-start.2

commit v14 on v13

--- a/solution.py
+++ b/solution.py
@@ -118,8 +118,15 @@
     return out.reshape(piece)
 
 
-def conv_pool_kernel(h_ref, x_ref, l_ref, r_ref, w_ref, o_ref, xs_ref):
-    height, width, channels = o_ref.shape
+def conv_pool_kernel(h_ref, x_ref, l_ref, r_ref, w_ref, o_ref, xs_ref, pooled_ref, sends, recvs, local_sem):
+    height, width, channels = pooled_ref.shape
+    count, per_dev = o_ref.shape[0], o_ref.shape[1]
+    me = lax.axis_index("tm")
+    barrier = pltpu.get_barrier_semaphore()
+    for k in range(1, count):
+        pl.semaphore_signal(
+            barrier, inc=1, device_id={"tm": lax.rem(me + k, count)}, device_id_type=MESH
+        )
     depth = x_ref.shape[0]
     groups = lax.axis_size("fsdp")
     t, f = lax.axis_index("tm"), lax.axis_index("fsdp")
@@ -153,6 +160,7 @@
         return carry
 
     lax.fori_loop(0, height // rows, shift, 0)
+    pl.semaphore_wait(barrier, count - 1)
 
     def body(r, carry):
         top = pl.multiple_of(r * rows, rows)
@@ -172,27 +180,63 @@
                 acc = acc + jnp.dot(lhs, w_ref[b * 3 + c], preferred_element_type=jnp.float32)
         silu = (acc / (1.0 + jnp.exp(-acc))).astype(jnp.bfloat16).astype(jnp.float32)
         pooled = ((silu[:span] + silu[span:]) * 0.5).astype(o_ref.dtype)
-        o_ref[pl.ds(top, rows)] = pooled.reshape(rows, width, channels)
+        pooled_ref[pl.ds(top, rows)] = pooled.reshape(rows, width, channels)
+        for i in range(rows // per_dev):
+            dest = r * (rows // per_dev) + i
+            src = pooled_ref.at[pl.ds(top + i * per_dev, per_dev)]
+
+            @pl.when(dest != me)
+            def _():
+                pltpu.make_async_remote_copy(
+                    src_ref=src, dst_ref=o_ref.at[me], send_sem=sends.at[dest],
+                    recv_sem=recvs.at[me], device_id={"tm": dest}, device_id_type=MESH,
+                ).start()
+
+            @pl.when(dest == me)
+            def _():
+                local = pltpu.make_async_copy(src, o_ref.at[me], local_sem)
+                local.start()
+                local.wait()
+
         return carry
 
     lax.fori_loop(0, height // rows, body, 0)
+
+    @pl.loop(1, count)
+    def _(k):
+        peer = lax.rem(me + k, count)
+        copy = pltpu.make_async_remote_copy(
+            src_ref=pooled_ref.at[pl.ds(0, per_dev)], dst_ref=o_ref.at[peer],
+            send_sem=sends.at[peer], recv_sem=recvs.at[peer],
+            device_id={"tm": peer}, device_id_type=MESH,
+        )
+        copy.wait_send()
+        copy.wait_recv()
 
 
 def conv_pool(halo, frames, left, right, weights):
     depth, height, width, channels = frames.shape
+    count = lax.axis_size("tm")
     vmem = pl.BlockSpec(memory_space=pltpu.VMEM)
     flops = 2 * 2 * height * width * weights.shape[0] * weights.shape[1] * channels
     return pl.pallas_call(
         conv_pool_kernel,
-        out_shape=jax.ShapeDtypeStruct((height, width, channels), jnp.bfloat16),
+        out_shape=jax.ShapeDtypeStruct((count, height // count, width, channels), jnp.bfloat16),
         in_specs=[vmem] * 5,
         out_specs=vmem,
-        scratch_shapes=[pltpu.VMEM((3, 2 * depth, height + 8, width, channels), frames.dtype)],
+        scratch_shapes=[
+            pltpu.VMEM((3, 2 * depth, height + 8, width, channels), frames.dtype),
+            pltpu.VMEM((height, width, channels), jnp.bfloat16),
+            pltpu.SemaphoreType.DMA((count,)),
+            pltpu.SemaphoreType.DMA((count,)),
+            pltpu.SemaphoreType.DMA,
+        ],
         cost_estimate=pl.CostEstimate(
             flops=flops,
             transcendentals=2 * height * width * channels,
             bytes_accessed=4 * frames.size + weights.size * 2 + height * width * channels * 2,
         ),
+        compiler_params=pltpu.CompilerParams(collective_id=3, has_side_effects=True),
     )(halo, frames, left, right, weights)
 
 
@@ -317,8 +361,7 @@
     full_conv = jnp.transpose(wall, (1, 3, 0, 2)).reshape(conv_weight.shape[:-1] + (-1,))
     full_mix = jnp.transpose(mall, (1, 3, 0, 2)).reshape(mix_weight.shape[:-1] + (-1,))
     weights = jnp.transpose(full_conv, (1, 2, 0, 3, 4)).reshape(9, 3 * channels, -1)
-    pooled = conv_pool(previous, frames, left, right, weights)[None]
-    pooled = lax.all_to_all(pooled, "tm", split_axis=1, concat_axis=0, tiled=True)
+    pooled = conv_pool(previous, frames, left, right, weights)
     branch = pooled.astype(jnp.float32).reshape(-1, channels)
     flat_cot = cotangent.reshape(-1, channels)
     grad_terms = []

time: 104 us -> 97.6 us (0.938)
  Pallas kernels: 67.9 us -> 84.6 us
  waiting for transfers between devices: 16.5 us -> 0 us
  starting transfers between devices: 8.18 us -> 0 us
  matrix products: 2.69 us -> 3.8 us
    all_to_all x1 -> x0, waiting for transfers between devices: 16.5 us -> none  [local(): lax.all_to_all(pooled, 'tm', split_axis=1, concat_axis=0, tiled=True)]
    pallas_call x1, Pallas kernels: 13 us -> 27.9 us  [conv_pool(): pl.pallas_call(conv_pool_kernel, out_shape=jax.ShapeDtypeStruct((count, h...]
    all_to_all x1 -> x0, starting transfers between devices: 8.18 us -> none  [local(): lax.all_to_all(pooled, 'tm', split_axis=1, concat_axis=0, tiled=True)]
    pallas_call x1, Pallas kernels: 18.7 us -> 20.5 us  [scatter_sum(): pl.pallas_call(scatter_kernel, out_shape=jax.ShapeDtypeStruct((1, piece),...]
    dot_general x3, matrix products: 1.01 us -> 2.12 us  [local(): lax.dot_general(lagged, flat_cot, (((0,), (0,)), ((), ())), preferred_ele...]
  transfers between devices with their start and end apart: 1 -> 0, of which waited for: 1 -> 0; matrix products, arithmetic and copies ran while one was open for 0% -> 0% of each run, Pallas kernels for 0% -> 0%
where the time goes in v14:
time: 97.6 us; the launch traced here: 97.3 us
  Pallas kernels  84.6 us (87%)
  local copies, waits for them, and re-layouts  8.11 us (8%)
  matrix products  3.8 us (4%)
    pallas_call x1, Pallas kernels, prologue(): pl.pallas_call(prologue_kernel, out_shape=(jax.ShapeDtypeStruct(frames.sh...  36.2 us
    pallas_call x1, Pallas kernels, conv_pool(): pl.pallas_call(conv_pool_kernel, out_shape=jax.ShapeDtypeStruct((count, h...  27.9 us
    pallas_call x1, Pallas kernels, scatter_sum(): pl.pallas_call(scatter_kernel, out_shape=jax.ShapeDtypeStruct((1, piece),...  20.5 us
    dot_general x3, matrix products, local(): lax.dot_general(lagged, flat_cot, (((0,), (0,)), ((), ())), preferred_ele...  2.12 us

profile of v14, /device:TPU:1, one launch (start us, length us, event | category | flops | bytes accessed | tf_op | source)
XLA Modules:
  0.0 97.3 jit_solution(9750589589530060969)
XLA Ops:
  0.6 0.0 copy-start
  0.6 1.2 %fusion.1 = (bf16[2,64,1,128]{3,2,1,0:T(2,128)(2,1)S(1)}, bf16[2,64,1,128]{3,2,1,0:T(2,128)(2,1)S(1)}) fusion(bf16[2,64,32,128]{3,2,1,0:T(8,128)(2,1)} %x_ref.3), kind=kLoop, calls=%fused_computation.13 | loop fusion | bytes 131072 | tf_op jit(solution)/shard_map/slice | solution.py:325
  1.9 0.6 copy_bitcast_fusion.1
  2.5 36.2 %shard_map.59 = (bf16[2,64,32,128]{3,2,1,0:T(8,128)(2,1)}, bf16[8,27,16,128]{3,2,1,0:T(8,128)(2,1)}, bf16[8,3,16,128]{3,2,1,0:T(8,128)(2,1)}, bf16[4,64,128]{2,1,0:T(8,128)(2,1)}, bf16[4,64,128]{2,1,0:T(8,128)(2,1)}) custom-call(bf16[2,64,32,128]{3,2,1,0:T(8,128)(2,1)} %x_ref.3, bf16[27,16,128]{2,1,0:T(8,128)(2,1)} %bitcast.66, ...), custom_call_target="tpu_custom_call" | custom-call | tf_op jit(solution)/shard_map/pallas_call | solution.py:328
  38.7 0.8 fusion.2
  39.5 1.4 %copy.10 = bf16[27,128,8,16]{1,3,2,0:T(8,128)(2,1)S(1)} copy(bf16[27,128,8,16]{1,3,0,2:T(8,128)(2,1)} %bitcast.60) | data formatting | bytes 1769472 | tf_op jit(solution)/shard_map/transpose | solution.py:361
  40.9 1.5 %copy.11 = bf16[3,3,3,128,128]{4,3,2,1,0:T(8,128)(2,1)} copy(bf16[3,3,3,128,128]{3,4,1,0,2:T(8,128)(2,1)S(1)} %bitcast.55) | data formatting | bytes 1769472 | tf_op jit(solution)/shard_map/transpose | solution.py:363
  42.4 27.9 %shard_map.60 = bf16[32,2,32,128]{3,2,1,0:T(8,128)(2,1)} custom-call(bf16[2,64,32,128]{3,2,1,0:T(8,128)(2,1)} %get-tuple-element.7.h_ref, bf16[2,64,32,128]{3,2,1,0:T(8,128)(2,1)} %x_ref.3, bf16[4,64,128]{2,1,0:T(8,128)(2,1)} %get-tuple-element.8.l_ref, bf16[4,64,128]{2,1,0:T(8,128)(2,1)} %get-tuple-element.9.r_ref, bf16[9,384,128]{2,1,0:T(8,128)(2,1)} %bitcast.61), custom_call_target="tpu_custom_call" | custom-call | flops 3623878656 | bytes 3506176 | tf_op jit(solution)/shard_map/pallas_call | solution.py:222
  70.3 0.0 copy-done
  70.3 0.0 copy-start.1
  70.3 1.4 %convolution_bitcast_fusion.1 = f32[1,128,128]{2,1,0:T(8,128)S(1)} fusion(bf16[32,2,32,128]{3,2,1,0:T(8,128)(2,1)} %shard_map.60, bf16[32,2,32,128]{3,2,1,0:T(8,128)(2,1)S(1)} %copy-done), kind=kOutput, calls=%fused_computation.5 | convolution fusion | flops 65011712 | bytes 1114112 | tf_op jit(solution)/shard_map/dot_general | solution.py:372
  71.8 0.0 copy-done.1
  71.8 0.3 convolution_bitcast_fusion.2
  72.1 0.3 convolution_bitcast_fusion
  72.5 0.1 reshape_reshape.3
  72.6 1.0 %copy.21 = f32[32,8,1,192]{3,2,0,1:T(1,128)} copy(f32[32,8,1,192]{3,1,0,2:T(8,128)S(1)} %reshape_reshape.3) | data formatting | bytes 393216 | tf_op jit(solution)/shard_map/reshape;reshape | solution.py:99
  73.6 20.5 %shard_map.61 = f32[1,192]{1,0:T(1,128)} custom-call(f32[8,32,1,192]{3,2,1,0:T(1,128)} %bitcast.59), custom_call_target="tpu_custom_call" | custom-call | tf_op jit(solution)/shard_map/pallas_call | solution.py:100
  94.1 0.3 convolution_add_fusion.2
  94.4 0.2 pad_slice_fusion
  94.7 0.3 convolution_add_fusion.1
  95.0 1.1 %fusion = bf16[2048,128]{1,0:T(8,128)(2,1)} fusion(f32[2048,128]{1,0:T(8,128)S(1)} %convolution_add_fusion.1, bf16[2048,128]{1,0:T(8,128)(2,1)S(1)} %bitcast.57, bf16[128,128]{0,1:T(8,128)(2,1)S(1)} %bitcast.63), kind=kOutput, calls=%fused_computation.3 | convolution fusion | flops 67633152 | bytes 2129920 | tf_op jit(solution)/shard_map/dot_general | solution.py:370
  96.1 0.0 copy-start.2
  96.1 0.7 copy-done.2
  96.7 0.6 copy.23
  (1 shorter events, 0.0 us)
Async XLA Ops:
  0.6 69.7 %copy-start = (bf16[32,2,32,128]{3,2,1,0:T(8,128)(2,1)S(1)}, bf16[32,2,32,128]{3,2,1,0:T(8,128)(2,1)}, u32[]{:S(2)}) copy-start(bf16[32,2,32,128]{3,2,1,0:T(8,128)(2,1)} %param.7) | copy-start | bytes 1572868
  70.3 1.5 %copy-start.1 = (bf16[32,2,32,128]{3,2,1,0:T(8,128)(2,1)S(1)}, bf16[32,2,32,128]{3,2,1,0:T(8,128)(2,1)}, u32[]{:S(2)}) copy-start(bf16[32,2,32,128]{3,2,1,0:T(8,128)(2,1)} %shard_map.60) | copy-start | bytes 1572868
  96.1 0.7 copy-start.2

commit v15 on v14

--- a/solution.py
+++ b/solution.py
@@ -177,7 +177,10 @@
                     ],
                     axis=0,
                 )
-                acc = acc + jnp.dot(lhs, w_ref[b * 3 + c], preferred_element_type=jnp.float32)
+                acc = acc + lax.dot_general(
+                    lhs, w_ref[b * 3 + c], (((1,), (1,)), ((), ())),
+                    preferred_element_type=jnp.float32,
+                )
         silu = (acc / (1.0 + jnp.exp(-acc))).astype(jnp.bfloat16).astype(jnp.float32)
         pooled = ((silu[:span] + silu[span:]) * 0.5).astype(o_ref.dtype)
         pooled_ref[pl.ds(top, rows)] = pooled.reshape(rows, width, channels)
@@ -218,7 +221,7 @@
     depth, height, width, channels = frames.shape
     count = lax.axis_size("tm")
     vmem = pl.BlockSpec(memory_space=pltpu.VMEM)
-    flops = 2 * 2 * height * width * weights.shape[0] * weights.shape[1] * channels
+    flops = 2 * 2 * height * width * weights.shape[0] * weights.shape[2] * channels
     return pl.pallas_call(
         conv_pool_kernel,
         out_shape=jax.ShapeDtypeStruct((count, height // count, width, channels), jnp.bfloat16),
@@ -358,9 +361,10 @@
     conv_shard = jnp.swapaxes(conv_weight, 3, 4).reshape(-1, part, channels)
     mix_shard = jnp.swapaxes(mix_weight, 1, 2)
     previous, wall, mall, left, right = prologue(frames, conv_shard, mix_shard)
-    full_conv = jnp.transpose(wall, (1, 3, 0, 2)).reshape(conv_weight.shape[:-1] + (-1,))
     full_mix = jnp.transpose(mall, (1, 3, 0, 2)).reshape(mix_weight.shape[:-1] + (-1,))
-    weights = jnp.transpose(full_conv, (1, 2, 0, 3, 4)).reshape(9, 3 * channels, -1)
+    groups = wall.shape[0]
+    weights = wall.reshape(groups, 3, 9, part, channels)
+    weights = jnp.transpose(weights, (2, 0, 3, 1, 4)).reshape(9, groups * part, 3 * channels)
     pooled = conv_pool(previous, frames, left, right, weights)
     branch = pooled.astype(jnp.float32).reshape(-1, channels)
     flat_cot = cotangent.reshape(-1, channels)

time: 97.6 us -> 97.9 us (level)
    reshape x0 -> x2, local copies, waits for them, and re-layouts: none -> 3.75 us  [the longest x1 1.96 us: local(): jnp.transpose(weights, (2, 0, 3, 1, 4))]
    transpose x2 -> x0, local copies, waits for them, and re-layouts: 2.91 us -> none  [the longest x1 1.51 us: local(): jnp.transpose(full_conv, (1, 2, 0, 3, 4)).reshape(9, 3 * channels, -1)]
where the time goes in v15:
time: 97.9 us; the launch traced here: 97.5 us
  Pallas kernels  84.7 us (87%)
  local copies, waits for them, and re-layouts  8.29 us (8%)
  matrix products  3.79 us (4%)
    pallas_call x1, Pallas kernels, prologue(): pl.pallas_call(prologue_kernel, out_shape=(jax.ShapeDtypeStruct(frames.sh...  36.2 us
    pallas_call x1, Pallas kernels, conv_pool(): pl.pallas_call(conv_pool_kernel, out_shape=jax.ShapeDtypeStruct((count, h...  28 us
    pallas_call x1, Pallas kernels, scatter_sum(): pl.pallas_call(scatter_kernel, out_shape=jax.ShapeDtypeStruct((1, piece),...  20.5 us
    dot_general x3, matrix products, local(): lax.dot_general(lagged, flat_cot, (((0,), (0,)), ((), ())), preferred_ele...  2.11 us
    reshape x1, local copies, waits for them, and re-layouts, local(): jnp.transpose(weights, (2, 0, 3, 1, 4))  1.96 us

profile of v15, /device:TPU:1, one launch (start us, length us, event | category | flops | bytes accessed | tf_op | source)
XLA Modules:
  0.0 97.5 jit_solution(4952209787594488179)
XLA Ops:
  0.6 0.0 copy-start
  0.6 1.2 %fusion.1 = (bf16[2,64,1,128]{3,2,1,0:T(2,128)(2,1)S(1)}, bf16[2,64,1,128]{3,2,1,0:T(2,128)(2,1)S(1)}) fusion(bf16[2,64,32,128]{3,2,1,0:T(8,128)(2,1)} %x_ref.3), kind=kLoop, calls=%fused_computation.14 | loop fusion | bytes 131072 | tf_op jit(solution)/shard_map/slice | solution.py:328
  1.9 0.6 copy_bitcast_fusion.2
  2.5 36.2 %shard_map.59 = (bf16[2,64,32,128]{3,2,1,0:T(8,128)(2,1)}, bf16[8,27,16,128]{3,2,1,0:T(8,128)(2,1)}, bf16[8,3,16,128]{3,2,1,0:T(8,128)(2,1)}, bf16[4,64,128]{2,1,0:T(8,128)(2,1)}, bf16[4,64,128]{2,1,0:T(8,128)(2,1)}) custom-call(bf16[2,64,32,128]{3,2,1,0:T(8,128)(2,1)} %x_ref.3, bf16[27,16,128]{2,1,0:T(8,128)(2,1)} %bitcast.64, ...), custom_call_target="tpu_custom_call" | custom-call | tf_op jit(solution)/shard_map/pallas_call | solution.py:331
  38.7 0.8 fusion.2
  39.5 1.8 %copy.22 = bf16[8,3,9,16,128]{4,1,3,0,2:T(4,128)(2,1)S(1)} copy(bf16[8,3,9,16,128]{4,3,2,1,0:T(8,128)(2,1)} %bitcast.59) | data formatting | bytes 1769472 | tf_op jit(solution)/shard_map/reshape | solution.py:366
  41.3 2.0 %reshape.42.w_ref = bf16[9,128,384]{2,1,0:T(8,128)(2,1)} reshape(bf16[9,8,16,3,128]{4,3,2,1,0:T(4,128)(2,1)S(1)} %bitcast.54) | data formatting | bytes 1769472 | tf_op jit(solution)/shard_map/reshape | solution.py:367
  43.2 28.0 %shard_map.60 = bf16[32,2,32,128]{3,2,1,0:T(8,128)(2,1)} custom-call(bf16[2,64,32,128]{3,2,1,0:T(8,128)(2,1)} %get-tuple-element.7.h_ref, bf16[2,64,32,128]{3,2,1,0:T(8,128)(2,1)} %x_ref.3, bf16[4,64,128]{2,1,0:T(8,128)(2,1)} %get-tuple-element.8.l_ref, bf16[4,64,128]{2,1,0:T(8,128)(2,1)} %get-tuple-element.9.r_ref, bf16[9,128,384]{2,1,0:T(8,128)(2,1)} %reshape.42.w_ref), custom_call_target="tpu_custom_call" | custom-call | flops 3623878656 | bytes 3506176 | tf_op jit(solution)/shard_map/pallas_call | solution.py:225
  71.3 0.0 copy-start.1
  71.3 0.0 copy-done
  71.3 1.4 %convolution_bitcast_fusion.1 = f32[1,128,128]{2,1,0:T(8,128)S(1)} fusion(bf16[32,2,32,128]{3,2,1,0:T(8,128)(2,1)} %shard_map.60, bf16[32,2,32,128]{3,2,1,0:T(8,128)(2,1)S(1)} %copy-done), kind=kOutput, calls=%fused_computation.6 | convolution fusion | flops 65011712 | bytes 1114112 | tf_op jit(solution)/shard_map/dot_general | solution.py:376
  72.7 0.0 copy-done.1
  72.7 0.3 convolution_bitcast_fusion.2
  73.1 0.3 convolution_bitcast_fusion
  73.4 0.1 reshape_reshape.3
  73.5 1.0 copy.23
  74.5 20.5 %shard_map.61 = f32[1,192]{1,0:T(1,128)} custom-call(f32[8,32,1,192]{3,2,1,0:T(1,128)} %bitcast.58), custom_call_target="tpu_custom_call" | custom-call | tf_op jit(solution)/shard_map/pallas_call | solution.py:100
  95.0 0.3 convolution_add_fusion.2
  95.3 0.2 pad_slice_fusion
  95.6 0.3 convolution_add_fusion.1
  95.9 0.0 copy-start.2
  95.9 1.1 %fusion = bf16[2048,128]{1,0:T(8,128)(2,1)} fusion(f32[2048,128]{1,0:T(8,128)S(1)} %convolution_add_fusion.1, bf16[2048,128]{1,0:T(8,128)(2,1)S(1)} %bitcast.56, bf16[128,128]{0,1:T(8,128)(2,1)S(1)} %bitcast.61), kind=kOutput, calls=%fused_computation.3 | convolution fusion | flops 67633152 | bytes 2129920 | tf_op jit(solution)/shard_map/dot_general | solution.py:374
  97.0 0.0 copy-done.2
  97.0 0.6 copy.25
  (1 shorter events, 0.0 us)
Async XLA Ops:
  0.6 70.6 %copy-start = (bf16[32,2,32,128]{3,2,1,0:T(8,128)(2,1)S(1)}, bf16[32,2,32,128]{3,2,1,0:T(8,128)(2,1)}, u32[]{:S(2)}) copy-start(bf16[32,2,32,128]{3,2,1,0:T(8,128)(2,1)} %param.7) | copy-start | bytes 1572868
  71.3 1.5 %copy-start.1 = (bf16[32,2,32,128]{3,2,1,0:T(8,128)(2,1)S(1)}, bf16[32,2,32,128]{3,2,1,0:T(8,128)(2,1)}, u32[]{:S(2)}) copy-start(bf16[32,2,32,128]{3,2,1,0:T(8,128)(2,1)} %shard_map.60) | copy-start | bytes 1572868
  95.9 1.1 %copy-start.2 = (f32[1,192]{1,0:T(1,128)S(1)}, f32[1,192]{1,0:T(1,128)}, u32[]{:S(2)}) copy-start(f32[1,192]{1,0:T(1,128)} %shard_map.61) | copy-start | bytes 2308

commit v16 on v14

--- a/solution.py
+++ b/solution.py
@@ -41,30 +41,26 @@
 
 
 def scatter_kernel(p_ref, o_ref, first, second, summed, s1, r1, s2, r2, l1, l2):
-    groups, count = first.shape[0], second.shape[0]
-    f, t = lax.axis_index("fsdp"), lax.axis_index("tm")
+    count, groups = first.shape[0], second.shape[0]
+    t, f = lax.axis_index("tm"), lax.axis_index("fsdp")
     barrier = pltpu.get_barrier_semaphore()
+    for k in range(1, count):
+        pl.semaphore_signal(
+            barrier, inc=1, device_id={"tm": lax.rem(t + k, count)}, device_id_type=MESH
+        )
     for k in range(1, groups):
         pl.semaphore_signal(
             barrier, inc=1, device_id={"fsdp": lax.rem(f + k, groups)}, device_id_type=MESH
         )
-    for k in range(1, count):
-        pl.semaphore_signal(
-            barrier, inc=1, device_id={"tm": lax.rem(t + k, count)}, device_id_type=MESH
-        )
     pl.semaphore_wait(barrier, groups - 1 + count - 1)
-    local = pltpu.make_async_copy(p_ref.at[f], first.at[f], l1)
+    local = pltpu.make_async_copy(p_ref.at[t], first.at[t], l1)
     local.start()
     copies = []
-    for k in range(1, groups):
-        peer = lax.rem(f + k, groups)
+    for k in range(1, count):
+        peer = lax.rem(t + k, count)
         copy = pltpu.make_async_remote_copy(
-            src_ref=p_ref.at[peer],
-            dst_ref=first.at[f],
-            send_sem=s1.at[k],
-            recv_sem=r1.at[k],
-            device_id={"fsdp": peer},
-            device_id_type=MESH,
+            src_ref=p_ref.at[peer], dst_ref=first.at[t], send_sem=s1.at[k], recv_sem=r1.at[k],
+            device_id={"tm": peer}, device_id_type=MESH,
         )
         copy.start()
         copies.append(copy)
@@ -72,18 +68,14 @@
     for copy in copies:
         copy.wait()
     summed[...] = jnp.sum(first[...], axis=0)
-    local = pltpu.make_async_copy(summed.at[t], second.at[t], l2)
+    local = pltpu.make_async_copy(summed, second.at[f], l2)
     local.start()
     copies = []
-    for k in range(1, count):
-        peer = lax.rem(t + k, count)
+    for k in range(1, groups):
+        peer = lax.rem(f + k, groups)
         copy = pltpu.make_async_remote_copy(
-            src_ref=summed.at[peer],
-            dst_ref=second.at[t],
-            send_sem=s2.at[k],
-            recv_sem=r2.at[k],
-            device_id={"tm": peer},
-            device_id_type=MESH,
+            src_ref=summed, dst_ref=second.at[f], send_sem=s2.at[k], recv_sem=r2.at[k],
+            device_id={"fsdp": peer}, device_id_type=MESH,
         )
         copy.start()
         copies.append(copy)
@@ -95,27 +87,27 @@
 
 def scatter_sum(partial):
     groups, count = lax.axis_size("fsdp"), lax.axis_size("tm")
-    piece = partial.size // (groups * count)
-    arranged = jnp.transpose(partial.reshape(count, groups, 1, piece), (1, 0, 2, 3))
+    rows = partial.size // (count * 128)
     out = pl.pallas_call(
         scatter_kernel,
-        out_shape=jax.ShapeDtypeStruct((1, piece), jnp.float32),
+        out_shape=jax.ShapeDtypeStruct((rows, 128), jnp.float32),
         in_specs=[pl.BlockSpec(memory_space=pltpu.VMEM)],
         out_specs=pl.BlockSpec(memory_space=pltpu.VMEM),
         scratch_shapes=[
-            pltpu.VMEM((groups, count, 1, piece), jnp.float32),
-            pltpu.VMEM((count, 1, piece), jnp.float32),
-            pltpu.VMEM((count, 1, piece), jnp.float32),
-            pltpu.SemaphoreType.DMA((groups,)),
-            pltpu.SemaphoreType.DMA((groups,)),
+            pltpu.VMEM((count, rows, 128), jnp.float32),
+            pltpu.VMEM((groups, rows, 128), jnp.float32),
+            pltpu.VMEM((rows, 128), jnp.float32),
             pltpu.SemaphoreType.DMA((count,)),
             pltpu.SemaphoreType.DMA((count,)),
+            pltpu.SemaphoreType.DMA((groups,)),
+            pltpu.SemaphoreType.DMA((groups,)),
             pltpu.SemaphoreType.DMA,
             pltpu.SemaphoreType.DMA,
         ],
         compiler_params=pltpu.CompilerParams(collective_id=1, has_side_effects=True),
-    )(arranged)
-    return out.reshape(piece)
+    )(partial.reshape(count, rows, 128))
+    piece = partial.size // (count * groups)
+    return lax.dynamic_slice_in_dim(out.reshape(-1), lax.axis_index("fsdp") * piece, piece)
 
 
 def conv_pool_kernel(h_ref, x_ref, l_ref, r_ref, w_ref, o_ref, xs_ref, pooled_ref, sends, recvs, local_sem):

time: 97.6 us -> 97.1 us (level)
  local copies, waits for them, and re-layouts: 8.11 us -> 7.07 us
    dynamic_slice x0 -> x1, local copies, waits for them, and re-layouts: none -> 1.34 us  [scatter_sum(): lax.dynamic_slice_in_dim(out.reshape(-1), lax.axis_index('fsdp') * piece,...]
    unnamed x7 -> x6, local copies, waits for them, and re-layouts: 1.24 us -> 0.02 us
where the time goes in v16:
time: 97.1 us; the launch traced here: 96.8 us
  Pallas kernels  85.2 us (88%)
  local copies, waits for them, and re-layouts  7.07 us (7%)
  matrix products  3.79 us (4%)
    pallas_call x1, Pallas kernels, prologue(): pl.pallas_call(prologue_kernel, out_shape=(jax.ShapeDtypeStruct(frames.sh...  36.2 us
    pallas_call x1, Pallas kernels, conv_pool(): pl.pallas_call(conv_pool_kernel, out_shape=jax.ShapeDtypeStruct((count, h...  27.9 us
    pallas_call x1, Pallas kernels, scatter_sum(): pl.pallas_call(scatter_kernel, out_shape=jax.ShapeDtypeStruct((rows, 128)...  21.1 us
    dot_general x3, matrix products, local(): lax.dot_general(lagged, flat_cot, (((0,), (0,)), ((), ())), preferred_ele...  2.1 us

profile of v16, /device:TPU:1, one launch (start us, length us, event | category | flops | bytes accessed | tf_op | source)
XLA Modules:
  0.0 96.8 jit_solution(6078693186754239948)
XLA Ops:
  0.6 0.0 copy-start
  0.6 1.2 %fusion.1 = (bf16[2,64,1,128]{3,2,1,0:T(2,128)(2,1)S(1)}, bf16[2,64,1,128]{3,2,1,0:T(2,128)(2,1)S(1)}) fusion(bf16[2,64,32,128]{3,2,1,0:T(8,128)(2,1)} %x_ref.3), kind=kLoop, calls=%fused_computation.12 | loop fusion | bytes 131072 | tf_op jit(solution)/shard_map/slice | solution.py:317
  1.9 0.6 copy_bitcast_fusion
  2.5 36.2 %shard_map.59 = (bf16[2,64,32,128]{3,2,1,0:T(8,128)(2,1)}, bf16[8,27,16,128]{3,2,1,0:T(8,128)(2,1)}, bf16[8,3,16,128]{3,2,1,0:T(8,128)(2,1)}, bf16[4,64,128]{2,1,0:T(8,128)(2,1)}, bf16[4,64,128]{2,1,0:T(8,128)(2,1)}) custom-call(bf16[2,64,32,128]{3,2,1,0:T(8,128)(2,1)} %x_ref.3, bf16[27,16,128]{2,1,0:T(8,128)(2,1)} %bitcast.62, ...), custom_call_target="tpu_custom_call" | custom-call | tf_op jit(solution)/shard_map/pallas_call | solution.py:320
  38.7 1.4 %copy.10 = bf16[27,128,8,16]{1,3,2,0:T(8,128)(2,1)S(1)} copy(bf16[27,128,8,16]{1,3,0,2:T(8,128)(2,1)} %bitcast.56) | data formatting | bytes 1769472 | tf_op jit(solution)/shard_map/transpose | solution.py:353
  40.1 1.5 %copy.11 = bf16[3,3,3,128,128]{4,3,2,1,0:T(8,128)(2,1)} copy(bf16[3,3,3,128,128]{3,4,1,0,2:T(8,128)(2,1)S(1)} %bitcast.52) | data formatting | bytes 1769472 | tf_op jit(solution)/shard_map/transpose | solution.py:355
  41.6 27.9 %shard_map.60 = bf16[32,2,32,128]{3,2,1,0:T(8,128)(2,1)} custom-call(bf16[2,64,32,128]{3,2,1,0:T(8,128)(2,1)} %get-tuple-element.7.h_ref, bf16[2,64,32,128]{3,2,1,0:T(8,128)(2,1)} %x_ref.3, bf16[4,64,128]{2,1,0:T(8,128)(2,1)} %get-tuple-element.8.l_ref, bf16[4,64,128]{2,1,0:T(8,128)(2,1)} %get-tuple-element.9.r_ref, bf16[9,384,128]{2,1,0:T(8,128)(2,1)} %bitcast.57), custom_call_target="tpu_custom_call" | custom-call | flops 3623878656 | bytes 3506176 | tf_op jit(solution)/shard_map/pallas_call | solution.py:214
  69.5 0.0 copy-done
  69.6 0.0 copy-start.1
  69.6 1.4 %convolution_bitcast_fusion = f32[1,128,128]{2,1,0:T(8,128)S(1)} fusion(bf16[32,2,32,128]{3,2,1,0:T(8,128)(2,1)} %shard_map.60, bf16[32,2,32,128]{3,2,1,0:T(8,128)(2,1)S(1)} %copy-done), kind=kOutput, calls=%fused_computation.4 | convolution fusion | flops 62914560 | bytes 1114112 | tf_op jit(solution)/shard_map/dot_general | solution.py:364
  71.0 0.0 copy-done.1
  71.0 0.3 convolution_bitcast_fusion.1
  71.3 0.3 convolution_bitcast_fusion.2
  71.7 0.7 reshape_reshape.3.p_ref
  72.4 0.0 copy-start.2
  72.4 21.1 %shard_map.61 = f32[12,128]{1,0:T(8,128)} custom-call(f32[32,12,128]{2,1,0:T(8,128)} %reshape_reshape.3.p_ref), custom_call_target="tpu_custom_call" | custom-call | tf_op jit(solution)/shard_map/pallas_call | solution.py:91
  93.5 1.3 %dynamic_slice.3 = f32[192]{0:T(256)} dynamic-slice(f32[1536]{0:T(1024)} %bitcast.65, s32[]{:T(128)S(6)} %select_n.3), dynamic_slice_sizes={192} | dynamic-slice | bytes 1540 | tf_op jit(solution)/shard_map/dynamic_slice | solution.py:110
  94.9 0.0 copy-done.2
  94.9 0.3 convolution_add_fusion.2
  95.2 0.2 pad_slice_fusion
  95.4 0.3 convolution_add_fusion.1
  95.7 1.1 %fusion = bf16[2048,128]{1,0:T(8,128)(2,1)} fusion(f32[2048,128]{1,0:T(8,128)S(1)} %convolution_add_fusion.1, bf16[2048,128]{1,0:T(8,128)(2,1)S(1)} %bitcast.54, bf16[128,128]{0,1:T(8,128)(2,1)S(1)} %bitcast.59), kind=kOutput, calls=%fused_computation.3 | convolution fusion | flops 67633152 | bytes 2129920 | tf_op jit(solution)/shard_map/dot_general | solution.py:362
  (2 shorter events, 0.0 us)
Async XLA Ops:
  0.6 68.9 %copy-start = (bf16[32,2,32,128]{3,2,1,0:T(8,128)(2,1)S(1)}, bf16[32,2,32,128]{3,2,1,0:T(8,128)(2,1)}, u32[]{:S(2)}) copy-start(bf16[32,2,32,128]{3,2,1,0:T(8,128)(2,1)} %param.7) | copy-start | bytes 1572868
  69.6 1.4 %copy-start.1 = (bf16[32,2,32,128]{3,2,1,0:T(8,128)(2,1)S(1)}, bf16[32,2,32,128]{3,2,1,0:T(8,128)(2,1)}, u32[]{:S(2)}) copy-start(bf16[32,2,32,128]{3,2,1,0:T(8,128)(2,1)} %shard_map.60) | copy-start | bytes 1572868
  72.4 22.4 %copy-start.2 = (bf16[8,3,16,128]{3,2,1,0:T(8,128)(2,1)S(1)}, bf16[8,3,16,128]{3,2,1,0:T(8,128)(2,1)}, u32[]{:S(2)}) copy-start(bf16[8,3,16,128]{3,2,1,0:T(8,128)(2,1)} %get-tuple-element.11) | copy-start | bytes 294916

commit v17 on v16

--- a/solution.py
+++ b/solution.py
@@ -154,7 +154,10 @@
     lax.fori_loop(0, height // rows, shift, 0)
     pl.semaphore_wait(barrier, count - 1)
 
-    def body(r, carry):
+    chunks, spread = height // rows, rows // per_dev
+
+    def body(step, carry):
+        r = lax.rem(step + me // spread + 1, chunks)
         top = pl.multiple_of(r * rows, rows)
         span = rows * width
         acc = jnp.zeros((2 * span, channels), jnp.float32)

time: 97.1 us -> 95.5 us (0.984)
  Pallas kernels: 85.2 us -> 83.6 us
    pallas_call x1, Pallas kernels: 21.1 us -> 19.7 us  [scatter_sum(): pl.pallas_call(scatter_kernel, out_shape=jax.ShapeDtypeStruct((rows, 128)...]
where the time goes in v17:
time: 95.5 us; the launch traced here: 95.3 us
  Pallas kernels  83.6 us (88%)
  local copies, waits for them, and re-layouts  7.07 us (7%)
  matrix products  3.79 us (4%)
    pallas_call x1, Pallas kernels, prologue(): pl.pallas_call(prologue_kernel, out_shape=(jax.ShapeDtypeStruct(frames.sh...  36.2 us
    pallas_call x1, Pallas kernels, conv_pool(): pl.pallas_call(conv_pool_kernel, out_shape=jax.ShapeDtypeStruct((count, h...  27.8 us
    pallas_call x1, Pallas kernels, scatter_sum(): pl.pallas_call(scatter_kernel, out_shape=jax.ShapeDtypeStruct((rows, 128)...  19.7 us
    dot_general x3, matrix products, local(): lax.dot_general(lagged, flat_cot, (((0,), (0,)), ((), ())), preferred_ele...  2.1 us

profile of v17, /device:TPU:1, one launch (start us, length us, event | category | flops | bytes accessed | tf_op | source)
XLA Modules:
  0.0 95.3 jit_solution(17965925179090050749)
XLA Ops:
  0.6 0.0 copy-start
  0.6 1.2 %fusion.1 = (bf16[2,64,1,128]{3,2,1,0:T(2,128)(2,1)S(1)}, bf16[2,64,1,128]{3,2,1,0:T(2,128)(2,1)S(1)}) fusion(bf16[2,64,32,128]{3,2,1,0:T(8,128)(2,1)} %x_ref.3), kind=kLoop, calls=%fused_computation.12 | loop fusion | bytes 131072 | tf_op jit(solution)/shard_map/slice | solution.py:320
  1.9 0.6 copy_bitcast_fusion
  2.5 36.2 %shard_map.59 = (bf16[2,64,32,128]{3,2,1,0:T(8,128)(2,1)}, bf16[8,27,16,128]{3,2,1,0:T(8,128)(2,1)}, bf16[8,3,16,128]{3,2,1,0:T(8,128)(2,1)}, bf16[4,64,128]{2,1,0:T(8,128)(2,1)}, bf16[4,64,128]{2,1,0:T(8,128)(2,1)}) custom-call(bf16[2,64,32,128]{3,2,1,0:T(8,128)(2,1)} %x_ref.3, bf16[27,16,128]{2,1,0:T(8,128)(2,1)} %bitcast.62, ...), custom_call_target="tpu_custom_call" | custom-call | tf_op jit(solution)/shard_map/pallas_call | solution.py:323
  38.7 1.4 %copy.10 = bf16[27,128,8,16]{1,3,2,0:T(8,128)(2,1)S(1)} copy(bf16[27,128,8,16]{1,3,0,2:T(8,128)(2,1)} %bitcast.56) | data formatting | bytes 1769472 | tf_op jit(solution)/shard_map/transpose | solution.py:356
  40.1 1.5 %copy.11 = bf16[3,3,3,128,128]{4,3,2,1,0:T(8,128)(2,1)} copy(bf16[3,3,3,128,128]{3,4,1,0,2:T(8,128)(2,1)S(1)} %bitcast.52) | data formatting | bytes 1769472 | tf_op jit(solution)/shard_map/transpose | solution.py:358
  41.6 27.8 %shard_map.60 = bf16[32,2,32,128]{3,2,1,0:T(8,128)(2,1)} custom-call(bf16[2,64,32,128]{3,2,1,0:T(8,128)(2,1)} %get-tuple-element.7.h_ref, bf16[2,64,32,128]{3,2,1,0:T(8,128)(2,1)} %x_ref.3, bf16[4,64,128]{2,1,0:T(8,128)(2,1)} %get-tuple-element.8.l_ref, bf16[4,64,128]{2,1,0:T(8,128)(2,1)} %get-tuple-element.9.r_ref, bf16[9,384,128]{2,1,0:T(8,128)(2,1)} %bitcast.57), custom_call_target="tpu_custom_call" | custom-call | flops 3623878656 | bytes 3506176 | tf_op jit(solution)/shard_map/pallas_call | solution.py:217
  69.4 0.0 copy-done
  69.4 0.0 copy-start.1
  69.4 1.4 %convolution_bitcast_fusion = f32[1,128,128]{2,1,0:T(8,128)S(1)} fusion(bf16[32,2,32,128]{3,2,1,0:T(8,128)(2,1)} %shard_map.60, bf16[32,2,32,128]{3,2,1,0:T(8,128)(2,1)S(1)} %copy-done), kind=kOutput, calls=%fused_computation.4 | convolution fusion | flops 62914560 | bytes 1114112 | tf_op jit(solution)/shard_map/dot_general | solution.py:367
  70.8 0.0 copy-done.1
  70.8 0.3 convolution_bitcast_fusion.1
  71.2 0.3 convolution_bitcast_fusion.2
  71.6 0.7 reshape_reshape.3.p_ref
  72.3 0.0 copy-start.2
  72.3 19.7 %shard_map.61 = f32[12,128]{1,0:T(8,128)} custom-call(f32[32,12,128]{2,1,0:T(8,128)} %reshape_reshape.3.p_ref), custom_call_target="tpu_custom_call" | custom-call | tf_op jit(solution)/shard_map/pallas_call | solution.py:91
  91.9 1.3 %dynamic_slice.3 = f32[192]{0:T(256)} dynamic-slice(f32[1536]{0:T(1024)} %bitcast.65, s32[]{:T(128)S(6)} %select_n.3), dynamic_slice_sizes={192} | dynamic-slice | bytes 1540 | tf_op jit(solution)/shard_map/dynamic_slice | solution.py:110
  93.3 0.0 copy-done.2
  93.3 0.3 convolution_add_fusion.2
  93.6 0.2 pad_slice_fusion
  93.9 0.3 convolution_add_fusion.1
  94.2 1.1 %fusion = bf16[2048,128]{1,0:T(8,128)(2,1)} fusion(f32[2048,128]{1,0:T(8,128)S(1)} %convolution_add_fusion.1, bf16[2048,128]{1,0:T(8,128)(2,1)S(1)} %bitcast.54, bf16[128,128]{0,1:T(8,128)(2,1)S(1)} %bitcast.59), kind=kOutput, calls=%fused_computation.3 | convolution fusion | flops 67633152 | bytes 2129920 | tf_op jit(solution)/shard_map/dot_general | solution.py:365
  (2 shorter events, 0.0 us)
Async XLA Ops:
  0.6 68.8 %copy-start = (bf16[32,2,32,128]{3,2,1,0:T(8,128)(2,1)S(1)}, bf16[32,2,32,128]{3,2,1,0:T(8,128)(2,1)}, u32[]{:S(2)}) copy-start(bf16[32,2,32,128]{3,2,1,0:T(8,128)(2,1)} %param.7) | copy-start | bytes 1572868
  69.4 1.4 %copy-start.1 = (bf16[32,2,32,128]{3,2,1,0:T(8,128)(2,1)S(1)}, bf16[32,2,32,128]{3,2,1,0:T(8,128)(2,1)}, u32[]{:S(2)}) copy-start(bf16[32,2,32,128]{3,2,1,0:T(8,128)(2,1)} %shard_map.60) | copy-start | bytes 1572868
  72.3 21.0 %copy-start.2 = (bf16[8,3,16,128]{3,2,1,0:T(8,128)(2,1)S(1)}, bf16[8,3,16,128]{3,2,1,0:T(8,128)(2,1)}, u32[]{:S(2)}) copy-start(bf16[8,3,16,128]{3,2,1,0:T(8,128)(2,1)} %get-tuple-element.11) | copy-start | bytes 294916

commit v18 on v17

--- a/solution.py
+++ b/solution.py
@@ -110,7 +110,7 @@
     return lax.dynamic_slice_in_dim(out.reshape(-1), lax.axis_index("fsdp") * piece, piece)
 
 
-def conv_pool_kernel(h_ref, x_ref, l_ref, r_ref, w_ref, o_ref, xs_ref, pooled_ref, sends, recvs, local_sem):
+def conv_pool_kernel(h_ref, x_ref, l_ref, r_ref, wall_ref, o_ref, xs_ref, pooled_ref, w_ref, sends, recvs, local_sem):
     height, width, channels = pooled_ref.shape
     count, per_dev = o_ref.shape[0], o_ref.shape[1]
     me = lax.axis_index("tm")
@@ -121,6 +121,10 @@
         )
     depth = x_ref.shape[0]
     groups = lax.axis_size("fsdp")
+    for tap in range(9):
+        w_ref[tap] = jnp.concatenate(
+            [wall_ref[:, a * 9 + tap].reshape(w_ref.shape[1], channels) for a in range(3)], axis=-1
+        )
     t, f = lax.axis_index("tm"), lax.axis_index("fsdp")
     rows = 8
     zero_rows = jnp.zeros((3, 2 * depth, 1, width, channels), xs_ref.dtype)
@@ -172,7 +176,10 @@
                     ],
                     axis=0,
                 )
-                acc = acc + jnp.dot(lhs, w_ref[b * 3 + c], preferred_element_type=jnp.float32)
+                acc = acc + lax.dot_general(
+                    lhs, w_ref[b * 3 + c], (((1,), (1,)), ((), ())),
+                    preferred_element_type=jnp.float32,
+                )
         silu = (acc / (1.0 + jnp.exp(-acc))).astype(jnp.bfloat16).astype(jnp.float32)
         pooled = ((silu[:span] + silu[span:]) * 0.5).astype(o_ref.dtype)
         pooled_ref[pl.ds(top, rows)] = pooled.reshape(rows, width, channels)
@@ -209,11 +216,12 @@
         copy.wait_recv()
 
 
-def conv_pool(halo, frames, left, right, weights):
+def conv_pool(halo, frames, left, right, wall):
     depth, height, width, channels = frames.shape
     count = lax.axis_size("tm")
     vmem = pl.BlockSpec(memory_space=pltpu.VMEM)
-    flops = 2 * 2 * height * width * weights.shape[0] * weights.shape[1] * channels
+    cout = wall.shape[0] * wall.shape[2]
+    flops = 2 * 2 * height * width * 27 * channels * cout
     return pl.pallas_call(
         conv_pool_kernel,
         out_shape=jax.ShapeDtypeStruct((count, height // count, width, channels), jnp.bfloat16),
@@ -222,6 +230,7 @@
         scratch_shapes=[
             pltpu.VMEM((3, 2 * depth, height + 8, width, channels), frames.dtype),
             pltpu.VMEM((height, width, channels), jnp.bfloat16),
+            pltpu.VMEM((9, cout, 3 * channels), wall.dtype),
             pltpu.SemaphoreType.DMA((count,)),
             pltpu.SemaphoreType.DMA((count,)),
             pltpu.SemaphoreType.DMA,
@@ -229,10 +238,10 @@
         cost_estimate=pl.CostEstimate(
             flops=flops,
             transcendentals=2 * height * width * channels,
-            bytes_accessed=4 * frames.size + weights.size * 2 + height * width * channels * 2,
+            bytes_accessed=4 * frames.size + wall.size * 2 + height * width * channels * 2,
         ),
         compiler_params=pltpu.CompilerParams(collective_id=3, has_side_effects=True),
-    )(halo, frames, left, right, weights)
+    )(halo, frames, left, right, wall)
 
 
 def prologue_kernel(x_ref, w_ref, m_ref, lcol_ref, rcol_ref, halo_ref, wall_ref, mall_ref, left_ref, right_ref, sends, recvs, wsends, wrecvs, msends, mrecvs, lsems, esends, erecvs):
@@ -353,10 +362,8 @@
     conv_shard = jnp.swapaxes(conv_weight, 3, 4).reshape(-1, part, channels)
     mix_shard = jnp.swapaxes(mix_weight, 1, 2)
     previous, wall, mall, left, right = prologue(frames, conv_shard, mix_shard)
-    full_conv = jnp.transpose(wall, (1, 3, 0, 2)).reshape(conv_weight.shape[:-1] + (-1,))
     full_mix = jnp.transpose(mall, (1, 3, 0, 2)).reshape(mix_weight.shape[:-1] + (-1,))
-    weights = jnp.transpose(full_conv, (1, 2, 0, 3, 4)).reshape(9, 3 * channels, -1)
-    pooled = conv_pool(previous, frames, left, right, weights)
+    pooled = conv_pool(previous, frames, left, right, wall)
     branch = pooled.astype(jnp.float32).reshape(-1, channels)
     flat_cot = cotangent.reshape(-1, channels)
     grad_terms = []

time: 95.5 us -> 92.9 us (0.973)
  local copies, waits for them, and re-layouts: 7.07 us -> 4.16 us
    transpose x2 -> x0, local copies, waits for them, and re-layouts: 2.91 us -> none  [the longest x1 1.51 us: local(): jnp.transpose(full_conv, (1, 2, 0, 3, 4)).reshape(9, 3 * channels, -1)]
    dot_general x3, matrix products: 1.69 us -> 2.94 us  [local(): jnp.dot(lagged, full_mix[offset], preferred_element_type=jnp.float32)]
    dot_general x3, matrix products: 2.1 us -> 1.01 us  [local(): lax.dot_general(lagged, flat_cot, (((0,), (0,)), ((), ())), preferred_ele...]
where the time goes in v18:
time: 92.9 us; the launch traced here: 92.7 us
  Pallas kernels  83.8 us (90%)
  local copies, waits for them, and re-layouts  4.16 us (4%)
  matrix products  3.95 us (4%)
    pallas_call x1, Pallas kernels, prologue(): pl.pallas_call(prologue_kernel, out_shape=(jax.ShapeDtypeStruct(frames.sh...  36.2 us
    pallas_call x1, Pallas kernels, conv_pool(): pl.pallas_call(conv_pool_kernel, out_shape=jax.ShapeDtypeStruct((count, h...  28 us
    pallas_call x1, Pallas kernels, scatter_sum(): pl.pallas_call(scatter_kernel, out_shape=jax.ShapeDtypeStruct((rows, 128)...  19.6 us
    dot_general x3, matrix products, local(): jnp.dot(lagged, full_mix[offset], preferred_element_type=jnp.float32)  2.94 us

profile of v18, /device:TPU:1, one launch (start us, length us, event | category | flops | bytes accessed | tf_op | source)
XLA Modules:
  0.0 92.7 jit_solution(2003528784283310947)
XLA Ops:
  0.6 0.0 copy-start
  0.6 1.2 %fusion.1 = (bf16[2,64,1,128]{3,2,1,0:T(2,128)(2,1)S(1)}, bf16[2,64,1,128]{3,2,1,0:T(2,128)(2,1)S(1)}) fusion(bf16[2,64,32,128]{3,2,1,0:T(8,128)(2,1)} %x_ref.3), kind=kLoop, calls=%fused_computation.12 | loop fusion | bytes 131072 | tf_op jit(solution)/shard_map/slice | solution.py:329
  1.9 0.6 copy_bitcast_fusion
  2.5 36.2 %shard_map.59 = (bf16[2,64,32,128]{3,2,1,0:T(8,128)(2,1)}, bf16[8,27,16,128]{3,2,1,0:T(8,128)(2,1)}, bf16[8,3,16,128]{3,2,1,0:T(8,128)(2,1)}, bf16[4,64,128]{2,1,0:T(8,128)(2,1)}, bf16[4,64,128]{2,1,0:T(8,128)(2,1)}) custom-call(bf16[2,64,32,128]{3,2,1,0:T(8,128)(2,1)} %x_ref.3, bf16[27,16,128]{2,1,0:T(8,128)(2,1)} %bitcast.54, ...), custom_call_target="tpu_custom_call" | custom-call | tf_op jit(solution)/shard_map/pallas_call | solution.py:332
  38.7 0.0 copy-start.2
  38.7 28.0 %shard_map.60 = bf16[32,2,32,128]{3,2,1,0:T(8,128)(2,1)} custom-call(bf16[2,64,32,128]{3,2,1,0:T(8,128)(2,1)} %get-tuple-element.7.h_ref, bf16[2,64,32,128]{3,2,1,0:T(8,128)(2,1)} %x_ref.3, bf16[4,64,128]{2,1,0:T(8,128)(2,1)} %get-tuple-element.8.l_ref, bf16[4,64,128]{2,1,0:T(8,128)(2,1)} %get-tuple-element.9.r_ref, ...), custom_call_target="tpu_custom_call" | custom-call | flops 3623878656 | bytes 3506176 | tf_op jit(solution)/shard_map/pallas_call | solution.py:225
  66.7 0.0 copy-done.2
  66.7 0.0 copy-start.1
  66.7 1.5 %convolution_add_fusion.2 = f32[2048,128]{1,0:T(8,128)S(1)} fusion(bf16[2048,128]{1,0:T(8,128)(2,1)} %bitcast.47, bf16[128,128]{0,1:T(8,128)(2,1)S(1)} %bitcast.52), kind=kOutput, calls=%fused_computation.2 | convolution fusion | flops 67633152 | bytes 1605632 | tf_op jit(solution)/shard_map/dot_general | solution.py:372
  68.3 0.0 copy-done.1
  68.3 0.2 pad_slice_fusion
  68.5 0.3 convolution_add_fusion.1
  68.8 1.1 %fusion = bf16[2048,128]{1,0:T(8,128)(2,1)} fusion(f32[2048,128]{1,0:T(8,128)S(1)} %convolution_add_fusion.1, bf16[2048,128]{1,0:T(8,128)(2,1)S(1)} %bitcast.48, bf16[128,128]{0,1:T(8,128)(2,1)S(1)} %bitcast.51), kind=kOutput, calls=%fused_computation.3 | convolution fusion | flops 67633152 | bytes 2129920 | tf_op jit(solution)/shard_map/dot_general | solution.py:372
  69.9 0.0 copy-done
  69.9 0.3 convolution_bitcast_fusion
  70.3 0.3 convolution_bitcast_fusion.1
  70.6 0.3 convolution_bitcast_fusion.2
  71.0 0.7 reshape_reshape.3.p_ref
  71.7 19.6 %shard_map.61 = f32[12,128]{1,0:T(8,128)} custom-call(f32[32,12,128]{2,1,0:T(8,128)} %reshape_reshape.3.p_ref), custom_call_target="tpu_custom_call" | custom-call | tf_op jit(solution)/shard_map/pallas_call | solution.py:91
  91.3 1.3 %dynamic_slice.3 = f32[192]{0:T(256)} dynamic-slice(f32[1536]{0:T(1024)} %bitcast.57, s32[]{:T(128)S(6)} %select_n.3), dynamic_slice_sizes={192} | dynamic-slice | bytes 1540 | tf_op jit(solution)/shard_map/dynamic_slice | solution.py:110
  (2 shorter events, 0.0 us)
Async XLA Ops:
  0.6 69.3 %copy-start = (bf16[32,2,32,128]{3,2,1,0:T(8,128)(2,1)S(1)}, bf16[32,2,32,128]{3,2,1,0:T(8,128)(2,1)}, u32[]{:S(2)}) copy-start(bf16[32,2,32,128]{3,2,1,0:T(8,128)(2,1)} %param.7) | copy-start | bytes 1572868
  38.7 28.0 %copy-start.2 = (bf16[8,3,16,128]{3,2,1,0:T(8,128)(2,1)S(1)}, bf16[8,3,16,128]{3,2,1,0:T(8,128)(2,1)}, u32[]{:S(2)}) copy-start(bf16[8,3,16,128]{3,2,1,0:T(8,128)(2,1)} %get-tuple-element.11) | copy-start | bytes 294916
  66.7 1.6 %copy-start.1 = (bf16[32,2,32,128]{3,2,1,0:T(8,128)(2,1)S(1)}, bf16[32,2,32,128]{3,2,1,0:T(8,128)(2,1)}, u32[]{:S(2)}) copy-start(bf16[32,2,32,128]{3,2,1,0:T(8,128)(2,1)} %shard_map.60) | copy-start | bytes 1572868

commit v19 on v18

--- a/solution.py
+++ b/solution.py
@@ -40,7 +40,7 @@
     return jnp.pad(block, ((offset, 0), (0, 0), (0, 0), (0, 0)))[: block.shape[0]]
 
 
-def scatter_kernel(p_ref, o_ref, first, second, summed, s1, r1, s2, r2, l1, l2):
+def scatter_kernel(p_ref, x_ref, m_ref, o_ref, e_ref, first, second, summed, branch, s1, r1, s2, r2, l1, l2):
     count, groups = first.shape[0], second.shape[0]
     t, f = lax.axis_index("tm"), lax.axis_index("fsdp")
     barrier = pltpu.get_barrier_semaphore()
@@ -52,6 +52,16 @@
         pl.semaphore_signal(
             barrier, inc=1, device_id={"fsdp": lax.rem(f + k, groups)}, device_id_type=MESH
         )
+    total = x_ref.shape[0]
+    lag = total // count
+    branch[...] = x_ref[...].astype(jnp.float32) + jnp.dot(
+        x_ref[...], m_ref[0], preferred_element_type=jnp.float32
+    )
+    for k in (1, 2):
+        branch[pl.ds(k * lag, total - k * lag)] += jnp.dot(
+            x_ref[pl.ds(0, total - k * lag)], m_ref[k], preferred_element_type=jnp.float32
+        )
+    e_ref[...] = branch[...].astype(e_ref.dtype)
     pl.semaphore_wait(barrier, groups - 1 + count - 1)
     local = pltpu.make_async_copy(p_ref.at[t], first.at[t], l1)
     local.start()
@@ -85,18 +95,23 @@
     o_ref[...] = jnp.sum(second[...], axis=0)
 
 
-def scatter_sum(partial):
+def scatter_sum(partial, pooled, mix):
     groups, count = lax.axis_size("fsdp"), lax.axis_size("tm")
     rows = partial.size // (count * 128)
-    out = pl.pallas_call(
+    vmem = pl.BlockSpec(memory_space=pltpu.VMEM)
+    out, encoded = pl.pallas_call(
         scatter_kernel,
-        out_shape=jax.ShapeDtypeStruct((rows, 128), jnp.float32),
-        in_specs=[pl.BlockSpec(memory_space=pltpu.VMEM)],
-        out_specs=pl.BlockSpec(memory_space=pltpu.VMEM),
+        out_shape=(
+            jax.ShapeDtypeStruct((rows, 128), jnp.float32),
+            jax.ShapeDtypeStruct(pooled.shape, pooled.dtype),
+        ),
+        in_specs=[vmem] * 3,
+        out_specs=(vmem, vmem),
         scratch_shapes=[
             pltpu.VMEM((count, rows, 128), jnp.float32),
             pltpu.VMEM((groups, rows, 128), jnp.float32),
             pltpu.VMEM((rows, 128), jnp.float32),
+            pltpu.VMEM(pooled.shape, jnp.float32),
             pltpu.SemaphoreType.DMA((count,)),
             pltpu.SemaphoreType.DMA((count,)),
             pltpu.SemaphoreType.DMA((groups,)),
@@ -105,9 +120,9 @@
             pltpu.SemaphoreType.DMA,
         ],
         compiler_params=pltpu.CompilerParams(collective_id=1, has_side_effects=True),
-    )(partial.reshape(count, rows, 128))
+    )(partial.reshape(count, rows, 128), pooled, mix)
     piece = partial.size // (count * groups)
-    return lax.dynamic_slice_in_dim(out.reshape(-1), lax.axis_index("fsdp") * piece, piece)
+    return lax.dynamic_slice_in_dim(out.reshape(-1), lax.axis_index("fsdp") * piece, piece), encoded
 
 
 def conv_pool_kernel(h_ref, x_ref, l_ref, r_ref, wall_ref, o_ref, xs_ref, pooled_ref, w_ref, sends, recvs, local_sem):
@@ -364,19 +379,19 @@
     previous, wall, mall, left, right = prologue(frames, conv_shard, mix_shard)
     full_mix = jnp.transpose(mall, (1, 3, 0, 2)).reshape(mix_weight.shape[:-1] + (-1,))
     pooled = conv_pool(previous, frames, left, right, wall)
-    branch = pooled.astype(jnp.float32).reshape(-1, channels)
     flat_cot = cotangent.reshape(-1, channels)
     grad_terms = []
     for offset in range(3):
         lagged = delayed(pooled, offset).reshape(-1, channels)
-        branch = branch + jnp.dot(lagged, full_mix[offset], preferred_element_type=jnp.float32)
         grad_terms.append(
             lax.dot_general(
                 lagged, flat_cot, (((0,), (0,)), ((), ())), preferred_element_type=jnp.float32
             )
         )
-    encoded = branch.astype(jnp.bfloat16).reshape(pooled.shape)
-    mix_grad = scatter_sum(jnp.stack(grad_terms).reshape(-1))
+    mix_grad, encoded = scatter_sum(
+        jnp.stack(grad_terms).reshape(-1), pooled.reshape(-1, channels), full_mix
+    )
+    encoded = encoded.reshape(pooled.shape)
     return (encoded, mix_grad)
 
 

time: 92.9 us -> 93.9 us (1.011)
  local copies, waits for them, and re-layouts: 4.16 us -> 6.69 us
  matrix products: 3.95 us -> 2.1 us
    dot_general x3 -> x0, matrix products: 2.94 us -> none  [local(): jnp.dot(lagged, full_mix[offset], preferred_element_type=jnp.float32)]
    unnamed x6 -> x7, local copies, waits for them, and re-layouts: 0.02 us -> 2.05 us
    dot_general x3, matrix products: 1.01 us -> 2.1 us  [local(): lax.dot_general(lagged, flat_cot, (((0,), (0,)), ((), ())), preferred_ele...]
where the time goes in v19:
time: 93.9 us; the launch traced here: 93.6 us
  Pallas kernels  84 us (89%)
  local copies, waits for them, and re-layouts  6.69 us (7%)
  matrix products  2.1 us (2%)
    pallas_call x1, Pallas kernels, prologue(): pl.pallas_call(prologue_kernel, out_shape=(jax.ShapeDtypeStruct(frames.sh...  36.2 us
    pallas_call x1, Pallas kernels, conv_pool(): pl.pallas_call(conv_pool_kernel, out_shape=jax.ShapeDtypeStruct((count, h...  27.9 us
    pallas_call x1, Pallas kernels, scatter_sum(): pl.pallas_call(scatter_kernel, out_shape=(jax.ShapeDtypeStruct((rows, 128...  19.9 us
    dot_general x3, matrix products, local(): lax.dot_general(lagged, flat_cot, (((0,), (0,)), ((), ())), preferred_ele...  2.1 us
    unnamed x7, local copies, waits for them, and re-layouts  2.05 us

profile of v19, /device:TPU:1, one launch (start us, length us, event | category | flops | bytes accessed | tf_op | source)
XLA Modules:
  0.0 93.6 jit_solution(12034005260785010019)
XLA Ops:
  0.6 0.0 copy-start
  0.6 1.2 %fusion = (bf16[2,64,1,128]{3,2,1,0:T(2,128)(2,1)S(1)}, bf16[2,64,1,128]{3,2,1,0:T(2,128)(2,1)S(1)}) fusion(bf16[2,64,32,128]{3,2,1,0:T(8,128)(2,1)} %x_ref.3), kind=kLoop, calls=%fused_computation.6 | loop fusion | bytes 131072 | tf_op jit(solution)/shard_map/slice | solution.py:344
  1.9 0.6 copy_bitcast_fusion
  2.5 36.2 %shard_map.59 = (bf16[2,64,32,128]{3,2,1,0:T(8,128)(2,1)}, bf16[8,27,16,128]{3,2,1,0:T(8,128)(2,1)}, bf16[8,3,16,128]{3,2,1,0:T(8,128)(2,1)}, bf16[4,64,128]{2,1,0:T(8,128)(2,1)}, bf16[4,64,128]{2,1,0:T(8,128)(2,1)}) custom-call(bf16[2,64,32,128]{3,2,1,0:T(8,128)(2,1)} %x_ref.3, bf16[27,16,128]{2,1,0:T(8,128)(2,1)} %bitcast.40, ...), custom_call_target="tpu_custom_call" | custom-call | tf_op jit(solution)/shard_map/pallas_call | solution.py:347
  38.7 27.9 %shard_map.60 = bf16[32,2,32,128]{3,2,1,0:T(8,128)(2,1)} custom-call(bf16[2,64,32,128]{3,2,1,0:T(8,128)(2,1)} %get-tuple-element.9.h_ref, bf16[2,64,32,128]{3,2,1,0:T(8,128)(2,1)} %x_ref.3, bf16[4,64,128]{2,1,0:T(8,128)(2,1)} %get-tuple-element.10.l_ref, bf16[4,64,128]{2,1,0:T(8,128)(2,1)} %get-tuple-element.11.r_ref, ...), custom_call_target="tpu_custom_call" | custom-call | flops 3623878656 | bytes 3506176 | tf_op jit(solution)/shard_map/pallas_call | solution.py:240
  66.6 0.0 copy-done
  66.6 0.0 copy-start.1
  66.7 1.4 %convolution_bitcast_fusion = f32[1,128,128]{2,1,0:T(8,128)S(1)} fusion(bf16[32,2,32,128]{3,2,1,0:T(8,128)(2,1)} %shard_map.60, bf16[32,2,32,128]{3,2,1,0:T(8,128)(2,1)S(1)} %copy-done), kind=kOutput, calls=%fused_computation | convolution fusion | flops 62914560 | bytes 1114112 | tf_op jit(solution)/shard_map/dot_general | solution.py:387
  68.1 0.0 copy-done.1
  68.1 0.3 convolution_bitcast_fusion.1
  68.4 0.3 convolution_bitcast_fusion.2
  68.8 0.0 copy-start.2
  68.8 0.7 reshape_reshape.3.p_ref
  69.5 0.2 copy-done.2
  69.7 0.7 copy.12.m_ref
  70.5 19.9 %shard_map.61 = (f32[12,128]{1,0:T(8,128)}, bf16[2048,128]{1,0:T(8,128)(2,1)}) custom-call(f32[32,12,128]{2,1,0:T(8,128)} %reshape_reshape.3.p_ref, bf16[2048,128]{1,0:T(8,128)(2,1)} %bitcast.37, bf16[3,128,128]{2,1,0:T(8,128)(2,1)} %copy.12.m_ref), custom_call_target="tpu_custom_call" | custom-call | tf_op jit(solution)/shard_map/pallas_call | solution.py:102
  90.4 1.3 %dynamic_slice.3 = f32[192]{0:T(256)} dynamic-slice(f32[1536]{0:T(1024)} %bitcast.43, s32[]{:T(128)S(6)} %select_n.3), dynamic_slice_sizes={192} | dynamic-slice | bytes 1540 | tf_op jit(solution)/shard_map/dynamic_slice | solution.py:125
  91.7 1.9 %copy.21 = bf16[32,2,32,128]{3,2,1,0:T(8,128)(2,1)} copy(bf16[32,2,32,128]{3,2,1,0:T(8,128)(2,1)} %bitcast.38) | data formatting | bytes 1048576
  (2 shorter events, 0.0 us)
Async XLA Ops:
  0.6 66.0 %copy-start = (bf16[32,2,32,128]{3,2,1,0:T(8,128)(2,1)S(1)}, bf16[32,2,32,128]{3,2,1,0:T(8,128)(2,1)}, u32[]{:S(2)}) copy-start(bf16[32,2,32,128]{3,2,1,0:T(8,128)(2,1)} %param.7) | copy-start | bytes 1572868
  66.6 1.4 %copy-start.1 = (bf16[32,2,32,128]{3,2,1,0:T(8,128)(2,1)S(1)}, bf16[32,2,32,128]{3,2,1,0:T(8,128)(2,1)}, u32[]{:S(2)}) copy-start(bf16[32,2,32,128]{3,2,1,0:T(8,128)(2,1)} %shard_map.60) | copy-start | bytes 1572868
  68.8 0.9 copy-start.2

commit v20 on v18

--- a/solution.py
+++ b/solution.py
@@ -82,15 +82,20 @@
     local.wait()
     for copy in copies:
         copy.wait()
-    o_ref[...] = jnp.sum(second[...], axis=0)
+    summed[...] = jnp.sum(second[...], axis=0)
+    per = o_ref.shape[0]
+    o_ref[...] = summed[pl.ds(pl.multiple_of(f * per, per), per)]
 
 
 def scatter_sum(partial):
     groups, count = lax.axis_size("fsdp"), lax.axis_size("tm")
-    rows = partial.size // (count * 128)
+    piece = partial.size // (count * groups)
+    wide = -(-piece // 128) * 128
+    arranged = jnp.pad(partial.reshape(count, groups, piece), ((0, 0), (0, 0), (0, wide - piece)))
+    rows = groups * wide // 128
     out = pl.pallas_call(
         scatter_kernel,
-        out_shape=jax.ShapeDtypeStruct((rows, 128), jnp.float32),
+        out_shape=jax.ShapeDtypeStruct((wide // 128, 128), jnp.float32),
         in_specs=[pl.BlockSpec(memory_space=pltpu.VMEM)],
         out_specs=pl.BlockSpec(memory_space=pltpu.VMEM),
         scratch_shapes=[
@@ -105,9 +110,8 @@
             pltpu.SemaphoreType.DMA,
         ],
         compiler_params=pltpu.CompilerParams(collective_id=1, has_side_effects=True),
-    )(partial.reshape(count, rows, 128))
-    piece = partial.size // (count * groups)
-    return lax.dynamic_slice_in_dim(out.reshape(-1), lax.axis_index("fsdp") * piece, piece)
+    )(arranged.reshape(count, rows, 128))
+    return out.reshape(-1)[:piece]
 
 
 def conv_pool_kernel(h_ref, x_ref, l_ref, r_ref, wall_ref, o_ref, xs_ref, pooled_ref, w_ref, sends, recvs, local_sem):

time: 92.9 us -> 93.9 us (1.011)
  Pallas kernels: 83.8 us -> 84.8 us
    dynamic_slice x1 -> x0, local copies, waits for them, and re-layouts: 1.34 us -> none  [scatter_sum(): lax.dynamic_slice_in_dim(out.reshape(-1), lax.axis_index('fsdp') * piece,...]
    unnamed x6 -> x9, local copies, waits for them, and re-layouts: 0.02 us -> 1.2 us
    pallas_call x1, Pallas kernels: 19.6 us -> 20.7 us  [scatter_sum(): pl.pallas_call(scatter_kernel, out_shape=jax.ShapeDtypeStruct((wide // 12...]
where the time goes in v20:
time: 93.9 us; the launch traced here: 93.7 us
  Pallas kernels  84.8 us (90%)
  local copies, waits for them, and re-layouts  4.12 us (4%)
  matrix products  3.96 us (4%)
    pallas_call x1, Pallas kernels, prologue(): pl.pallas_call(prologue_kernel, out_shape=(jax.ShapeDtypeStruct(frames.sh...  36.2 us
    pallas_call x1, Pallas kernels, conv_pool(): pl.pallas_call(conv_pool_kernel, out_shape=jax.ShapeDtypeStruct((count, h...  28 us
    pallas_call x1, Pallas kernels, scatter_sum(): pl.pallas_call(scatter_kernel, out_shape=jax.ShapeDtypeStruct((wide // 12...  20.7 us
    dot_general x3, matrix products, local(): jnp.dot(lagged, full_mix[offset], preferred_element_type=jnp.float32)  2.95 us

profile of v20, /device:TPU:1, one launch (start us, length us, event | category | flops | bytes accessed | tf_op | source)
XLA Modules:
  0.0 93.7 jit_solution(1637037236859414573)
XLA Ops:
  0.6 0.0 copy-start
  0.6 1.2 %fusion.1 = (bf16[2,64,1,128]{3,2,1,0:T(2,128)(2,1)S(1)}, bf16[2,64,1,128]{3,2,1,0:T(2,128)(2,1)S(1)}) fusion(bf16[2,64,32,128]{3,2,1,0:T(8,128)(2,1)} %x_ref.3), kind=kLoop, calls=%fused_computation.12 | loop fusion | bytes 131072 | tf_op jit(solution)/shard_map/slice | solution.py:333
  1.9 0.6 copy_bitcast_fusion
  2.5 36.2 %shard_map.59 = (bf16[2,64,32,128]{3,2,1,0:T(8,128)(2,1)}, bf16[8,27,16,128]{3,2,1,0:T(8,128)(2,1)}, bf16[8,3,16,128]{3,2,1,0:T(8,128)(2,1)}, bf16[4,64,128]{2,1,0:T(8,128)(2,1)}, bf16[4,64,128]{2,1,0:T(8,128)(2,1)}) custom-call(bf16[2,64,32,128]{3,2,1,0:T(8,128)(2,1)} %x_ref.3, bf16[27,16,128]{2,1,0:T(8,128)(2,1)} %bitcast.55, ...), custom_call_target="tpu_custom_call" | custom-call | tf_op jit(solution)/shard_map/pallas_call | solution.py:336
  38.7 0.0 copy-start.2
  38.7 28.0 %shard_map.60 = bf16[32,2,32,128]{3,2,1,0:T(8,128)(2,1)} custom-call(bf16[2,64,32,128]{3,2,1,0:T(8,128)(2,1)} %get-tuple-element.7.h_ref, bf16[2,64,32,128]{3,2,1,0:T(8,128)(2,1)} %x_ref.3, bf16[4,64,128]{2,1,0:T(8,128)(2,1)} %get-tuple-element.8.l_ref, bf16[4,64,128]{2,1,0:T(8,128)(2,1)} %get-tuple-element.9.r_ref, ...), custom_call_target="tpu_custom_call" | custom-call | flops 3623878656 | bytes 3506176 | tf_op jit(solution)/shard_map/pallas_call | solution.py:229
  66.6 0.0 copy-done.2
  66.7 0.0 copy-start.1
  66.7 1.6 %convolution_add_fusion.2 = f32[2048,128]{1,0:T(8,128)S(1)} fusion(bf16[2048,128]{1,0:T(8,128)(2,1)} %bitcast.48, bf16[128,128]{0,1:T(8,128)(2,1)S(1)} %bitcast.53), kind=kOutput, calls=%fused_computation.2 | convolution fusion | flops 67633152 | bytes 1605632 | tf_op jit(solution)/shard_map/dot_general | solution.py:376
  68.2 0.0 copy-done.1
  68.2 0.2 pad_slice_fusion
  68.5 0.3 convolution_add_fusion.1
  68.8 1.1 %fusion = bf16[2048,128]{1,0:T(8,128)(2,1)} fusion(f32[2048,128]{1,0:T(8,128)S(1)} %convolution_add_fusion.1, bf16[2048,128]{1,0:T(8,128)(2,1)S(1)} %bitcast.49, bf16[128,128]{0,1:T(8,128)(2,1)S(1)} %bitcast.52), kind=kOutput, calls=%fused_computation.3 | convolution fusion | flops 67633152 | bytes 2129920 | tf_op jit(solution)/shard_map/dot_general | solution.py:376
  69.9 0.0 copy-done
  69.9 0.3 convolution_bitcast_fusion
  70.2 0.3 convolution_bitcast_fusion.1
  70.6 0.3 convolution_bitcast_fusion.2
  71.0 0.1 reshape_reshape.3
  71.1 0.7 reshape.43.p_ref
  71.8 20.7 %shard_map.61 = f32[2,128]{1,0:T(2,128)} custom-call(f32[32,16,128]{2,1,0:T(8,128)} %reshape.43.p_ref), custom_call_target="tpu_custom_call" | custom-call | tf_op jit(solution)/shard_map/pallas_call | solution.py:96
  92.5 0.0 copy-start.3
  92.5 0.6 copy-done.3
  93.1 0.6 copy.16
  (3 shorter events, 0.0 us)
Async XLA Ops:
  0.6 69.3 %copy-start = (bf16[32,2,32,128]{3,2,1,0:T(8,128)(2,1)S(1)}, bf16[32,2,32,128]{3,2,1,0:T(8,128)(2,1)}, u32[]{:S(2)}) copy-start(bf16[32,2,32,128]{3,2,1,0:T(8,128)(2,1)} %param.7) | copy-start | bytes 1572868
  38.7 28.0 %copy-start.2 = (bf16[8,3,16,128]{3,2,1,0:T(8,128)(2,1)S(1)}, bf16[8,3,16,128]{3,2,1,0:T(8,128)(2,1)}, u32[]{:S(2)}) copy-start(bf16[8,3,16,128]{3,2,1,0:T(8,128)(2,1)} %get-tuple-element.11) | copy-start | bytes 294916
  66.7 1.6 %copy-start.1 = (bf16[32,2,32,128]{3,2,1,0:T(8,128)(2,1)S(1)}, bf16[32,2,32,128]{3,2,1,0:T(8,128)(2,1)}, u32[]{:S(2)}) copy-start(bf16[32,2,32,128]{3,2,1,0:T(8,128)(2,1)} %shard_map.60) | copy-start | bytes 1572868
  92.5 0.6 copy-start.3

commit v21 on v18

--- a/solution.py
+++ b/solution.py
@@ -244,7 +244,9 @@
     )(halo, frames, left, right, wall)
 
 
-def prologue_kernel(x_ref, w_ref, m_ref, lcol_ref, rcol_ref, halo_ref, wall_ref, mall_ref, left_ref, right_ref, sends, recvs, wsends, wrecvs, msends, mrecvs, lsems, esends, erecvs):
+def prologue_kernel(x_ref, w_ref, m_ref, halo_ref, wall_ref, mall_ref, left_ref, right_ref, lcol_ref, rcol_ref, sends, recvs, wsends, wrecvs, msends, mrecvs, lsems, esends, erecvs):
+    lcol_ref[...] = x_ref[:, :, 0, :]
+    rcol_ref[...] = x_ref[:, :, x_ref.shape[2] - 1, :]
     count, groups = lax.axis_size("tm"), lax.axis_size("fsdp")
     t, f = lax.axis_index("tm"), lax.axis_index("fsdp")
     t_next, t_prev = lax.rem(t + 1, count), lax.rem(t + count - 1, count)
@@ -325,8 +327,6 @@
 def prologue(frames, conv_shard, mix_shard):
     groups = lax.axis_size("fsdp")
     depth, height, width, channels = frames.shape
-    lcol = frames[:, :, 0, :]
-    rcol = frames[:, :, width - 1, :]
     edge = jax.ShapeDtypeStruct((2 * depth, height, channels), frames.dtype)
     vmem = pl.BlockSpec(memory_space=pltpu.VMEM)
     return pl.pallas_call(
@@ -338,9 +338,11 @@
             edge,
             edge,
         ),
-        in_specs=[vmem] * 5,
+        in_specs=[vmem] * 3,
         out_specs=(vmem,) * 5,
         scratch_shapes=[
+            pltpu.VMEM((depth, height, channels), frames.dtype),
+            pltpu.VMEM((depth, height, channels), frames.dtype),
             pltpu.SemaphoreType.DMA((4,)),
             pltpu.SemaphoreType.DMA((4,)),
             pltpu.SemaphoreType.DMA((groups,)),
@@ -352,7 +354,7 @@
             pltpu.SemaphoreType.DMA((4,)),
         ],
         compiler_params=pltpu.CompilerParams(collective_id=2, has_side_effects=True),
-    )(frames, conv_shard, mix_shard, lcol, rcol)
+    )(frames, conv_shard, mix_shard)
 
 
 def local(frames, conv_weight, mix_weight, cotangent):

time: 92.9 us -> 91.3 us (0.983)
  local copies, waits for them, and re-layouts: 4.16 us -> 2.33 us
    slice x1 -> x0, local copies, waits for them, and re-layouts: 1.2 us -> none  [prologue(): rcol = frames[:, :, width - 1, :]]
where the time goes in v21:
time: 91.3 us; the launch traced here: 91.1 us
  Pallas kernels  84.1 us (92%)
  matrix products  3.96 us (4%)
  local copies, waits for them, and re-layouts  2.33 us (3%)
    pallas_call x1, Pallas kernels, prologue(): pl.pallas_call(prologue_kernel, out_shape=(jax.ShapeDtypeStruct(frames.sh...  36.5 us
    pallas_call x1, Pallas kernels, conv_pool(): pl.pallas_call(conv_pool_kernel, out_shape=jax.ShapeDtypeStruct((count, h...  28 us
    pallas_call x1, Pallas kernels, scatter_sum(): pl.pallas_call(scatter_kernel, out_shape=jax.ShapeDtypeStruct((rows, 128)...  19.6 us
    dot_general x3, matrix products, local(): jnp.dot(lagged, full_mix[offset], preferred_element_type=jnp.float32)  2.95 us

profile of v21, /device:TPU:1, one launch (start us, length us, event | category | flops | bytes accessed | tf_op | source)
XLA Modules:
  0.0 91.1 jit_solution(9644831957233023642)
XLA Ops:
  0.6 0.0 copy-start
  0.6 36.5 %shard_map.59 = (bf16[2,64,32,128]{3,2,1,0:T(8,128)(2,1)}, bf16[8,27,16,128]{3,2,1,0:T(8,128)(2,1)}, bf16[8,3,16,128]{3,2,1,0:T(8,128)(2,1)}, bf16[4,64,128]{2,1,0:T(8,128)(2,1)}, bf16[4,64,128]{2,1,0:T(8,128)(2,1)}) custom-call(bf16[2,64,32,128]{3,2,1,0:T(8,128)(2,1)} %x_ref.3, bf16[27,16,128]{2,1,0:T(8,128)(2,1)} %bitcast.50, bf16[3,16,128]{2,1,0:T(8,128)(2,1)} %bitcast.52), custom_call_target="tpu_custom_call" | custom-call | tf_op jit(solution)/shard_map/pallas_call | solution.py:332
  37.1 0.0 copy-start.2
  37.1 28.0 %shard_map.60 = bf16[32,2,32,128]{3,2,1,0:T(8,128)(2,1)} custom-call(bf16[2,64,32,128]{3,2,1,0:T(8,128)(2,1)} %get-tuple-element.7.h_ref, bf16[2,64,32,128]{3,2,1,0:T(8,128)(2,1)} %x_ref.3, bf16[4,64,128]{2,1,0:T(8,128)(2,1)} %get-tuple-element.8.l_ref, bf16[4,64,128]{2,1,0:T(8,128)(2,1)} %get-tuple-element.9.r_ref, ...), custom_call_target="tpu_custom_call" | custom-call | flops 3623878656 | bytes 3506176 | tf_op jit(solution)/shard_map/pallas_call | solution.py:225
  65.1 0.0 copy-done.2
  65.2 0.0 copy-start.1
  65.2 1.6 %convolution_add_fusion.2 = f32[2048,128]{1,0:T(8,128)S(1)} fusion(bf16[2048,128]{1,0:T(8,128)(2,1)} %bitcast.43, bf16[128,128]{0,1:T(8,128)(2,1)S(1)} %bitcast.48), kind=kOutput, calls=%fused_computation.2 | convolution fusion | flops 67633152 | bytes 1605632 | tf_op jit(solution)/shard_map/dot_general | solution.py:374
  66.7 0.0 copy-done.1
  66.7 0.2 pad_slice_fusion
  67.0 0.3 convolution_add_fusion.1
  67.3 1.1 %fusion = bf16[2048,128]{1,0:T(8,128)(2,1)} fusion(f32[2048,128]{1,0:T(8,128)S(1)} %convolution_add_fusion.1, bf16[2048,128]{1,0:T(8,128)(2,1)S(1)} %bitcast.44, bf16[128,128]{0,1:T(8,128)(2,1)S(1)} %bitcast.47), kind=kOutput, calls=%fused_computation.3 | convolution fusion | flops 67633152 | bytes 2129920 | tf_op jit(solution)/shard_map/dot_general | solution.py:374
  68.4 0.0 copy-done
  68.4 0.3 convolution_bitcast_fusion
  68.7 0.3 convolution_bitcast_fusion.1
  69.1 0.3 convolution_bitcast_fusion.2
  69.4 0.7 reshape_reshape.3.p_ref
  70.2 19.6 %shard_map.61 = f32[12,128]{1,0:T(8,128)} custom-call(f32[32,12,128]{2,1,0:T(8,128)} %reshape_reshape.3.p_ref), custom_call_target="tpu_custom_call" | custom-call | tf_op jit(solution)/shard_map/pallas_call | solution.py:91
  89.8 1.3 %dynamic_slice.3 = f32[192]{0:T(256)} dynamic-slice(f32[1536]{0:T(1024)} %bitcast.53, s32[]{:T(128)S(6)} %select_n.3), dynamic_slice_sizes={192} | dynamic-slice | bytes 1540 | tf_op jit(solution)/shard_map/dynamic_slice | solution.py:110
  (2 shorter events, 0.0 us)
Async XLA Ops:
  0.6 67.8 %copy-start = (bf16[32,2,32,128]{3,2,1,0:T(8,128)(2,1)S(1)}, bf16[32,2,32,128]{3,2,1,0:T(8,128)(2,1)}, u32[]{:S(2)}) copy-start(bf16[32,2,32,128]{3,2,1,0:T(8,128)(2,1)} %param.7) | copy-start | bytes 1572868
  37.1 28.0 %copy-start.2 = (bf16[8,3,16,128]{3,2,1,0:T(8,128)(2,1)S(1)}, bf16[8,3,16,128]{3,2,1,0:T(8,128)(2,1)}, u32[]{:S(2)}) copy-start(bf16[8,3,16,128]{3,2,1,0:T(8,128)(2,1)} %get-tuple-element.11) | copy-start | bytes 294916
  65.2 1.6 %copy-start.1 = (bf16[32,2,32,128]{3,2,1,0:T(8,128)(2,1)S(1)}, bf16[32,2,32,128]{3,2,1,0:T(8,128)(2,1)}, u32[]{:S(2)}) copy-start(bf16[32,2,32,128]{3,2,1,0:T(8,128)(2,1)} %shard_map.60) | copy-start | bytes 1572868

commit v22 on v20

--- a/solution.py
+++ b/solution.py
@@ -248,7 +248,9 @@
     )(halo, frames, left, right, wall)
 
 
-def prologue_kernel(x_ref, w_ref, m_ref, lcol_ref, rcol_ref, halo_ref, wall_ref, mall_ref, left_ref, right_ref, sends, recvs, wsends, wrecvs, msends, mrecvs, lsems, esends, erecvs):
+def prologue_kernel(x_ref, w_ref, m_ref, halo_ref, wall_ref, mall_ref, left_ref, right_ref, lcol_ref, rcol_ref, sends, recvs, wsends, wrecvs, msends, mrecvs, lsems, esends, erecvs):
+    lcol_ref[...] = x_ref[:, :, 0, :]
+    rcol_ref[...] = x_ref[:, :, x_ref.shape[2] - 1, :]
     count, groups = lax.axis_size("tm"), lax.axis_size("fsdp")
     t, f = lax.axis_index("tm"), lax.axis_index("fsdp")
     t_next, t_prev = lax.rem(t + 1, count), lax.rem(t + count - 1, count)
@@ -329,8 +331,6 @@
 def prologue(frames, conv_shard, mix_shard):
     groups = lax.axis_size("fsdp")
     depth, height, width, channels = frames.shape
-    lcol = frames[:, :, 0, :]
-    rcol = frames[:, :, width - 1, :]
     edge = jax.ShapeDtypeStruct((2 * depth, height, channels), frames.dtype)
     vmem = pl.BlockSpec(memory_space=pltpu.VMEM)
     return pl.pallas_call(
@@ -342,9 +342,11 @@
             edge,
             edge,
         ),
-        in_specs=[vmem] * 5,
+        in_specs=[vmem] * 3,
         out_specs=(vmem,) * 5,
         scratch_shapes=[
+            pltpu.VMEM((depth, height, channels), frames.dtype),
+            pltpu.VMEM((depth, height, channels), frames.dtype),
             pltpu.SemaphoreType.DMA((4,)),
             pltpu.SemaphoreType.DMA((4,)),
             pltpu.SemaphoreType.DMA((groups,)),
@@ -356,7 +358,7 @@
             pltpu.SemaphoreType.DMA((4,)),
         ],
         compiler_params=pltpu.CompilerParams(collective_id=2, has_side_effects=True),
-    )(frames, conv_shard, mix_shard, lcol, rcol)
+    )(frames, conv_shard, mix_shard)
 
 
 def local(frames, conv_weight, mix_weight, cotangent):

time: 93.9 us -> 92.4 us (0.984)
  local copies, waits for them, and re-layouts: 4.12 us -> 2.31 us
    slice x1 -> x0, local copies, waits for them, and re-layouts: 1.2 us -> none  [prologue(): rcol = frames[:, :, width - 1, :]]
where the time goes in v22:
time: 92.4 us; the launch traced here: 92.2 us
  Pallas kernels  85.2 us (92%)
  matrix products  3.95 us (4%)
  local copies, waits for them, and re-layouts  2.31 us (2%)
    pallas_call x1, Pallas kernels, prologue(): pl.pallas_call(prologue_kernel, out_shape=(jax.ShapeDtypeStruct(frames.sh...  36.5 us
    pallas_call x1, Pallas kernels, conv_pool(): pl.pallas_call(conv_pool_kernel, out_shape=jax.ShapeDtypeStruct((count, h...  28 us
    pallas_call x1, Pallas kernels, scatter_sum(): pl.pallas_call(scatter_kernel, out_shape=jax.ShapeDtypeStruct((wide // 12...  20.7 us
    dot_general x3, matrix products, local(): jnp.dot(lagged, full_mix[offset], preferred_element_type=jnp.float32)  2.94 us

profile of v22, /device:TPU:1, one launch (start us, length us, event | category | flops | bytes accessed | tf_op | source)
XLA Modules:
  0.0 92.2 jit_solution(9583791246687603751)
XLA Ops:
  0.6 0.0 copy-start
  0.6 36.5 %shard_map.59 = (bf16[2,64,32,128]{3,2,1,0:T(8,128)(2,1)}, bf16[8,27,16,128]{3,2,1,0:T(8,128)(2,1)}, bf16[8,3,16,128]{3,2,1,0:T(8,128)(2,1)}, bf16[4,64,128]{2,1,0:T(8,128)(2,1)}, bf16[4,64,128]{2,1,0:T(8,128)(2,1)}) custom-call(bf16[2,64,32,128]{3,2,1,0:T(8,128)(2,1)} %x_ref.3, bf16[27,16,128]{2,1,0:T(8,128)(2,1)} %bitcast.51, bf16[3,16,128]{2,1,0:T(8,128)(2,1)} %bitcast.53), custom_call_target="tpu_custom_call" | custom-call | tf_op jit(solution)/shard_map/pallas_call | solution.py:336
  37.2 0.0 copy-start.2
  37.2 28.0 %shard_map.60 = bf16[32,2,32,128]{3,2,1,0:T(8,128)(2,1)} custom-call(bf16[2,64,32,128]{3,2,1,0:T(8,128)(2,1)} %get-tuple-element.7.h_ref, bf16[2,64,32,128]{3,2,1,0:T(8,128)(2,1)} %x_ref.3, bf16[4,64,128]{2,1,0:T(8,128)(2,1)} %get-tuple-element.8.l_ref, bf16[4,64,128]{2,1,0:T(8,128)(2,1)} %get-tuple-element.9.r_ref, ...), custom_call_target="tpu_custom_call" | custom-call | flops 3623878656 | bytes 3506176 | tf_op jit(solution)/shard_map/pallas_call | solution.py:229
  65.2 0.0 copy-done.2
  65.2 0.0 copy-start.1
  65.2 1.5 %convolution_add_fusion.2 = f32[2048,128]{1,0:T(8,128)S(1)} fusion(bf16[2048,128]{1,0:T(8,128)(2,1)} %bitcast.44, bf16[128,128]{0,1:T(8,128)(2,1)S(1)} %bitcast.49), kind=kOutput, calls=%fused_computation.2 | convolution fusion | flops 67633152 | bytes 1605632 | tf_op jit(solution)/shard_map/dot_general | solution.py:378
  66.7 0.0 copy-done.1
  66.8 0.2 pad_slice_fusion
  67.0 0.3 convolution_add_fusion.1
  67.3 1.1 %fusion = bf16[2048,128]{1,0:T(8,128)(2,1)} fusion(f32[2048,128]{1,0:T(8,128)S(1)} %convolution_add_fusion.1, bf16[2048,128]{1,0:T(8,128)(2,1)S(1)} %bitcast.45, bf16[128,128]{0,1:T(8,128)(2,1)S(1)} %bitcast.48), kind=kOutput, calls=%fused_computation.3 | convolution fusion | flops 67633152 | bytes 2129920 | tf_op jit(solution)/shard_map/dot_general | solution.py:378
  68.4 0.0 copy-done
  68.4 0.3 convolution_bitcast_fusion
  68.8 0.3 convolution_bitcast_fusion.1
  69.1 0.3 convolution_bitcast_fusion.2
  69.5 0.1 reshape_reshape.3
  69.6 0.7 reshape.43.p_ref
  70.3 20.7 %shard_map.61 = f32[2,128]{1,0:T(2,128)} custom-call(f32[32,16,128]{2,1,0:T(8,128)} %reshape.43.p_ref), custom_call_target="tpu_custom_call" | custom-call | tf_op jit(solution)/shard_map/pallas_call | solution.py:96
  91.0 0.0 copy-start.3
  91.0 0.6 copy-done.3
  91.6 0.6 copy.10
  (3 shorter events, 0.0 us)
Async XLA Ops:
  0.6 67.8 %copy-start = (bf16[32,2,32,128]{3,2,1,0:T(8,128)(2,1)S(1)}, bf16[32,2,32,128]{3,2,1,0:T(8,128)(2,1)}, u32[]{:S(2)}) copy-start(bf16[32,2,32,128]{3,2,1,0:T(8,128)(2,1)} %param.7) | copy-start | bytes 1572868
  37.2 28.0 %copy-start.2 = (bf16[8,3,16,128]{3,2,1,0:T(8,128)(2,1)S(1)}, bf16[8,3,16,128]{3,2,1,0:T(8,128)(2,1)}, u32[]{:S(2)}) copy-start(bf16[8,3,16,128]{3,2,1,0:T(8,128)(2,1)} %get-tuple-element.11) | copy-start | bytes 294916
  65.2 1.6 %copy-start.1 = (bf16[32,2,32,128]{3,2,1,0:T(8,128)(2,1)S(1)}, bf16[32,2,32,128]{3,2,1,0:T(8,128)(2,1)}, u32[]{:S(2)}) copy-start(bf16[32,2,32,128]{3,2,1,0:T(8,128)(2,1)} %shard_map.60) | copy-start | bytes 1572868
  91.0 0.6 copy-start.3

commit v23 on v21

--- a/solution.py
+++ b/solution.py
@@ -283,14 +283,15 @@
         )
         for i, (src, dst, dev) in enumerate(edges)
     ]
-    for copy in edges[:2]:
-        copy.start()
     halo = halo + edges[2:]
 
     @pl.when(t < count - 1)
     def _():
         for copy in halo:
             copy.start()
+
+    for copy in edges[:2]:
+        copy.start()
 
     copies = []
     locals_ = [

time: 91.3 us -> 91.3 us (level)
  no operation moved by 1% of the time
where the time goes in v23:
time: 91.3 us; the launch traced here: 91.1 us
  Pallas kernels  84 us (92%)
  matrix products  3.96 us (4%)
  local copies, waits for them, and re-layouts  2.33 us (3%)
    pallas_call x1, Pallas kernels, prologue(): pl.pallas_call(prologue_kernel, out_shape=(jax.ShapeDtypeStruct(frames.sh...  36.5 us
    pallas_call x1, Pallas kernels, conv_pool(): pl.pallas_call(conv_pool_kernel, out_shape=jax.ShapeDtypeStruct((count, h...  28 us
    pallas_call x1, Pallas kernels, scatter_sum(): pl.pallas_call(scatter_kernel, out_shape=jax.ShapeDtypeStruct((rows, 128)...  19.5 us
    dot_general x3, matrix products, local(): jnp.dot(lagged, full_mix[offset], preferred_element_type=jnp.float32)  2.95 us

profile of v23, /device:TPU:1, one launch (start us, length us, event | category | flops | bytes accessed | tf_op | source)
XLA Modules:
  0.0 91.1 jit_solution(384099284819447222)
XLA Ops:
  0.6 0.0 copy-start
  0.6 36.5 %shard_map.59 = (bf16[2,64,32,128]{3,2,1,0:T(8,128)(2,1)}, bf16[8,27,16,128]{3,2,1,0:T(8,128)(2,1)}, bf16[8,3,16,128]{3,2,1,0:T(8,128)(2,1)}, bf16[4,64,128]{2,1,0:T(8,128)(2,1)}, bf16[4,64,128]{2,1,0:T(8,128)(2,1)}) custom-call(bf16[2,64,32,128]{3,2,1,0:T(8,128)(2,1)} %x_ref.3, bf16[27,16,128]{2,1,0:T(8,128)(2,1)} %bitcast.50, bf16[3,16,128]{2,1,0:T(8,128)(2,1)} %bitcast.52), custom_call_target="tpu_custom_call" | custom-call | tf_op jit(solution)/shard_map/pallas_call | solution.py:333
  37.1 0.0 copy-start.2
  37.1 28.0 %shard_map.60 = bf16[32,2,32,128]{3,2,1,0:T(8,128)(2,1)} custom-call(bf16[2,64,32,128]{3,2,1,0:T(8,128)(2,1)} %get-tuple-element.7.h_ref, bf16[2,64,32,128]{3,2,1,0:T(8,128)(2,1)} %x_ref.3, bf16[4,64,128]{2,1,0:T(8,128)(2,1)} %get-tuple-element.8.l_ref, bf16[4,64,128]{2,1,0:T(8,128)(2,1)} %get-tuple-element.9.r_ref, ...), custom_call_target="tpu_custom_call" | custom-call | flops 3623878656 | bytes 3506176 | tf_op jit(solution)/shard_map/pallas_call | solution.py:225
  65.2 0.0 copy-done.2
  65.2 0.0 copy-start.1
  65.2 1.6 %convolution_add_fusion.2 = f32[2048,128]{1,0:T(8,128)S(1)} fusion(bf16[2048,128]{1,0:T(8,128)(2,1)} %bitcast.43, bf16[128,128]{0,1:T(8,128)(2,1)S(1)} %bitcast.48), kind=kOutput, calls=%fused_computation.2 | convolution fusion | flops 67633152 | bytes 1605632 | tf_op jit(solution)/shard_map/dot_general | solution.py:375
  66.8 0.0 copy-done.1
  66.8 0.2 pad_slice_fusion
  67.0 0.3 convolution_add_fusion.1
  67.3 1.1 %fusion = bf16[2048,128]{1,0:T(8,128)(2,1)} fusion(f32[2048,128]{1,0:T(8,128)S(1)} %convolution_add_fusion.1, bf16[2048,128]{1,0:T(8,128)(2,1)S(1)} %bitcast.44, bf16[128,128]{0,1:T(8,128)(2,1)S(1)} %bitcast.47), kind=kOutput, calls=%fused_computation.3 | convolution fusion | flops 67633152 | bytes 2129920 | tf_op jit(solution)/shard_map/dot_general | solution.py:375
  68.4 0.0 copy-done
  68.4 0.3 convolution_bitcast_fusion
  68.8 0.3 convolution_bitcast_fusion.1
  69.1 0.3 convolution_bitcast_fusion.2
  69.5 0.7 reshape_reshape.3.p_ref
  70.2 19.5 %shard_map.61 = f32[12,128]{1,0:T(8,128)} custom-call(f32[32,12,128]{2,1,0:T(8,128)} %reshape_reshape.3.p_ref), custom_call_target="tpu_custom_call" | custom-call | tf_op jit(solution)/shard_map/pallas_call | solution.py:91
  89.8 1.3 %dynamic_slice.3 = f32[192]{0:T(256)} dynamic-slice(f32[1536]{0:T(1024)} %bitcast.53, s32[]{:T(128)S(6)} %select_n.3), dynamic_slice_sizes={192} | dynamic-slice | bytes 1540 | tf_op jit(solution)/shard_map/dynamic_slice | solution.py:110
  (2 shorter events, 0.0 us)
Async XLA Ops:
  0.6 67.8 %copy-start = (bf16[32,2,32,128]{3,2,1,0:T(8,128)(2,1)S(1)}, bf16[32,2,32,128]{3,2,1,0:T(8,128)(2,1)}, u32[]{:S(2)}) copy-start(bf16[32,2,32,128]{3,2,1,0:T(8,128)(2,1)} %param.7) | copy-start | bytes 1572868
  37.1 28.0 %copy-start.2 = (bf16[8,3,16,128]{3,2,1,0:T(8,128)(2,1)S(1)}, bf16[8,3,16,128]{3,2,1,0:T(8,128)(2,1)}, u32[]{:S(2)}) copy-start(bf16[8,3,16,128]{3,2,1,0:T(8,128)(2,1)} %get-tuple-element.11) | copy-start | bytes 294916
  65.2 1.6 %copy-start.1 = (bf16[32,2,32,128]{3,2,1,0:T(8,128)(2,1)S(1)}, bf16[32,2,32,128]{3,2,1,0:T(8,128)(2,1)}, u32[]{:S(2)}) copy-start(bf16[32,2,32,128]{3,2,1,0:T(8,128)(2,1)} %shard_map.60) | copy-start | bytes 1572868

commit v24 on v21

--- a/solution.py
+++ b/solution.py
@@ -126,7 +126,7 @@
             [wall_ref[:, a * 9 + tap].reshape(w_ref.shape[1], channels) for a in range(3)], axis=-1
         )
     t, f = lax.axis_index("tm"), lax.axis_index("fsdp")
-    rows = 8
+    rows = 16
     zero_rows = jnp.zeros((3, 2 * depth, 1, width, channels), xs_ref.dtype)
     xs_ref[:, :, pl.ds(0, 1)] = zero_rows
     xs_ref[:, :, pl.ds(height + 1, 1)] = zero_rows

time: 91.3 us -> 90.9 us (level)
  no operation moved by 1% of the time
where the time goes in v24:
time: 90.9 us; the launch traced here: 90.7 us
  Pallas kernels  83.6 us (92%)
  matrix products  3.96 us (4%)
  local copies, waits for them, and re-layouts  2.33 us (3%)
    pallas_call x1, Pallas kernels, prologue(): pl.pallas_call(prologue_kernel, out_shape=(jax.ShapeDtypeStruct(frames.sh...  36.5 us
    pallas_call x1, Pallas kernels, conv_pool(): pl.pallas_call(conv_pool_kernel, out_shape=jax.ShapeDtypeStruct((count, h...  27.4 us
    pallas_call x1, Pallas kernels, scatter_sum(): pl.pallas_call(scatter_kernel, out_shape=jax.ShapeDtypeStruct((rows, 128)...  19.8 us
    dot_general x3, matrix products, local(): jnp.dot(lagged, full_mix[offset], preferred_element_type=jnp.float32)  2.95 us

profile of v24, /device:TPU:1, one launch (start us, length us, event | category | flops | bytes accessed | tf_op | source)
XLA Modules:
  0.0 90.7 jit_solution(12825640536974952070)
XLA Ops:
  0.6 0.0 copy-start
  0.6 36.5 %shard_map.59 = (bf16[2,64,32,128]{3,2,1,0:T(8,128)(2,1)}, bf16[8,27,16,128]{3,2,1,0:T(8,128)(2,1)}, bf16[8,3,16,128]{3,2,1,0:T(8,128)(2,1)}, bf16[4,64,128]{2,1,0:T(8,128)(2,1)}, bf16[4,64,128]{2,1,0:T(8,128)(2,1)}) custom-call(bf16[2,64,32,128]{3,2,1,0:T(8,128)(2,1)} %x_ref.3, bf16[27,16,128]{2,1,0:T(8,128)(2,1)} %bitcast.50, bf16[3,16,128]{2,1,0:T(8,128)(2,1)} %bitcast.52), custom_call_target="tpu_custom_call" | custom-call | tf_op jit(solution)/shard_map/pallas_call | solution.py:332
  37.1 0.0 copy-start.2
  37.1 27.4 %shard_map.60 = bf16[32,2,32,128]{3,2,1,0:T(8,128)(2,1)} custom-call(bf16[2,64,32,128]{3,2,1,0:T(8,128)(2,1)} %get-tuple-element.7.h_ref, bf16[2,64,32,128]{3,2,1,0:T(8,128)(2,1)} %x_ref.3, bf16[4,64,128]{2,1,0:T(8,128)(2,1)} %get-tuple-element.8.l_ref, bf16[4,64,128]{2,1,0:T(8,128)(2,1)} %get-tuple-element.9.r_ref, ...), custom_call_target="tpu_custom_call" | custom-call | flops 3623878656 | bytes 3506176 | tf_op jit(solution)/shard_map/pallas_call | solution.py:225
  64.5 0.0 copy-done.2
  64.5 0.0 copy-start.1
  64.6 1.5 %convolution_add_fusion.2 = f32[2048,128]{1,0:T(8,128)S(1)} fusion(bf16[2048,128]{1,0:T(8,128)(2,1)} %bitcast.43, bf16[128,128]{0,1:T(8,128)(2,1)S(1)} %bitcast.48), kind=kOutput, calls=%fused_computation.2 | convolution fusion | flops 67633152 | bytes 1605632 | tf_op jit(solution)/shard_map/dot_general | solution.py:374
  66.1 0.0 copy-done.1
  66.1 0.2 pad_slice_fusion
  66.4 0.3 convolution_add_fusion.1
  66.7 1.1 %fusion = bf16[2048,128]{1,0:T(8,128)(2,1)} fusion(f32[2048,128]{1,0:T(8,128)S(1)} %convolution_add_fusion.1, bf16[2048,128]{1,0:T(8,128)(2,1)S(1)} %bitcast.44, bf16[128,128]{0,1:T(8,128)(2,1)S(1)} %bitcast.47), kind=kOutput, calls=%fused_computation.3 | convolution fusion | flops 67633152 | bytes 2129920 | tf_op jit(solution)/shard_map/dot_general | solution.py:374
  67.8 0.0 copy-done
  67.8 0.3 convolution_bitcast_fusion
  68.1 0.3 convolution_bitcast_fusion.1
  68.5 0.3 convolution_bitcast_fusion.2
  68.8 0.7 reshape_reshape.3.p_ref
  69.6 19.8 %shard_map.61 = f32[12,128]{1,0:T(8,128)} custom-call(f32[32,12,128]{2,1,0:T(8,128)} %reshape_reshape.3.p_ref), custom_call_target="tpu_custom_call" | custom-call | tf_op jit(solution)/shard_map/pallas_call | solution.py:91
  89.3 1.3 %dynamic_slice.3 = f32[192]{0:T(256)} dynamic-slice(f32[1536]{0:T(1024)} %bitcast.53, s32[]{:T(128)S(6)} %select_n.3), dynamic_slice_sizes={192} | dynamic-slice | bytes 1540 | tf_op jit(solution)/shard_map/dynamic_slice | solution.py:110
  (2 shorter events, 0.0 us)
Async XLA Ops:
  0.6 67.2 %copy-start = (bf16[32,2,32,128]{3,2,1,0:T(8,128)(2,1)S(1)}, bf16[32,2,32,128]{3,2,1,0:T(8,128)(2,1)}, u32[]{:S(2)}) copy-start(bf16[32,2,32,128]{3,2,1,0:T(8,128)(2,1)} %param.7) | copy-start | bytes 1572868
  37.1 27.4 %copy-start.2 = (bf16[8,3,16,128]{3,2,1,0:T(8,128)(2,1)S(1)}, bf16[8,3,16,128]{3,2,1,0:T(8,128)(2,1)}, u32[]{:S(2)}) copy-start(bf16[8,3,16,128]{3,2,1,0:T(8,128)(2,1)} %get-tuple-element.11) | copy-start | bytes 294916
  64.5 1.6 %copy-start.1 = (bf16[32,2,32,128]{3,2,1,0:T(8,128)(2,1)S(1)}, bf16[32,2,32,128]{3,2,1,0:T(8,128)(2,1)}, u32[]{:S(2)}) copy-start(bf16[32,2,32,128]{3,2,1,0:T(8,128)(2,1)} %shard_map.60) | copy-start | bytes 1572868
